TPU v7x, 32 devices: a whole 2x2x4 slice. The times are simulated.
32 devices in a mesh: grp: 4 (over y, x), ctx: 8 (over z, core).
Axes of the slice: x: 2, y: 2, z: 4, core: 2. Of those that a mesh axis runs over, the one named last changes fastest.
Arguments:
- tokens_in: bfloat16 [16384, 2304], P(('grp', 'ctx')), may hold values from -6 to 6
- cotangent: bfloat16 [16384, 2304], P(('grp', 'ctx')), may hold values from -6 to 6
- w_query: bfloat16 [2304, 2304], P(('grp', 'ctx')), as said below
- w_key: bfloat16 [2304, 2304], P(('grp', 'ctx')), may hold values from -0.125 to 0.125
- w_value: bfloat16 [2304, 2304], P(('grp', 'ctx')), may hold values from -0.125 to 0.125
- w_output: bfloat16 [2304, 2304], P(('grp', 'ctx')), may hold values from -6 to 6
- w_gate: bfloat16 [2304, 5760], P('grp', 'ctx'), may hold values from -0.125 to 0.125
- w_up: bfloat16 [2304, 5760], P('grp', 'ctx'), may hold values from -0.125 to 0.125
- w_down: bfloat16 [5760, 2304], P('ctx', 'grp'), may hold values from -0.3125 to 0.3125
- attn_gain: bfloat16 [2304], P(('grp', 'ctx')), may hold values from 0.5 to 1.5
- ffn_gain: bfloat16 [2304], P(('grp', 'ctx')), may hold values from 0.5 to 1.5
- cont_len: int32 [4, 8], P('grp'), may hold values from 64 to 256
- deal_order: int32 [4, 64], P('grp'), may hold values from 0 to 63, as said below
- clip_threshold: int32 [1], replicated, may hold values from 2 to 4
Outputs:
- output: bfloat16 [16384, 2304], P(('grp', 'ctx'))
- grad_input: float32 [16384, 2304], P(('grp', 'ctx'))
- grad_w_query: float32 [2304, 2304], P(('grp', 'ctx'))
- grad_w_key: float32 [2304, 2304], P(('grp', 'ctx'))
- grad_w_value: float32 [2304, 2304], P(('grp', 'ctx'))
- grad_w_output: float32 [2304, 2304], P(('grp', 'ctx'))
- grad_w_gate: float32 [2304, 5760], P('grp', 'ctx')
- grad_w_up: float32 [2304, 5760], P('grp', 'ctx')
- grad_w_down: float32 [5760, 2304], P('ctx', 'grp')
- grad_attn_gain: float32 [2304], P(('grp', 'ctx'))
- grad_ffn_gain: float32 [2304], P(('grp', 'ctx'))
- logit_max: float32 [36], replicated
- clip_factor: float32 [36], replicated
- clipped_query: float32 [2304, 2304], P(('grp', 'ctx'))
- clipped_key: float32 [2304, 2304], P(('grp', 'ctx'))
Inputs may be any that keep to these rules, and one draw needn't show every extreme that they name: Each row of deal_order lists every tile of the group once. The stored slots of one device along ctx are 8 in a row; the first half of them hold prompt tiles and the second half continuation tiles. `w_query`: normal entries of deviation 2304^-0.5, unclipped, with all 64 columns of a head multiplied by one factor between 1 and 2.5.
All inputs are finite; a program needn't handle non-finite values.
Results may differ from a plain program's by a relative error of at most 0.02.
Values may be sent and summed in bfloat16 or wider, within the bound.
No kernel may reach another device: no remote copies, remote signals or barrier semaphores. Data moves between devices by JAX's collectives and lax.ppermute only.
A program may use at most 448 MiB of HBM per device.

v0:
```python
import math

import jax
import jax.numpy as jnp
from jax import lax
from jax.sharding import PartitionSpec as P

HEADS = 36
HDIM = 64
PLEN = 2048
CLEN = 256
NCONT = 8
BLK = 64
FAMTOK = 4096


branch_scale = 1.4 / math.sqrt(40.0)
norm_eps = 1e-05
rope_base = 10000.0
masked_value = -1e30


def rope_angles(position):
    half_dim = HDIM // 2
    frequency = rope_base ** (-(jnp.arange(half_dim, dtype=jnp.float32) * (2.0 / HDIM)))
    angles = position.astype(jnp.float32)[:, None] * frequency[None, :]
    return (jnp.cos(angles)[:, None, :], jnp.sin(angles)[:, None, :])


def rotate(values, cosine, sine_vals, turn_sign):
    row_count = values.shape[0]
    shaped = values.reshape(row_count, HEADS, HDIM)
    leading = shaped[..., : HDIM // 2]
    trailing = shaped[..., HDIM // 2 :]
    turned = jnp.concatenate(
        [
            leading * cosine - turn_sign * trailing * sine_vals,
            trailing * cosine + turn_sign * leading * sine_vals,
        ],
        axis=-1,
    )
    return turned.reshape(row_count, HEADS * HDIM)


def token_facts(logical, lengths):
    family = logical // FAMTOK
    offset = logical % FAMTOK
    prompt = offset < PLEN
    member = jnp.clip((offset - PLEN) // CLEN, 0, NCONT - 1)
    inside = offset - PLEN - member * CLEN
    seq_id = jnp.where(prompt, -1, family * NCONT + member)
    numbers = jnp.arange(lengths.shape[0], dtype=jnp.int32)
    live_len = jnp.sum(jnp.where(seq_id[:, None] == numbers[None, :], lengths[None, :], 0), axis=1)
    is_live = prompt | (inside < live_len)
    position = jnp.where(prompt, offset, PLEN + inside)
    return (family, offset, prompt, seq_id, is_live, position)


def visible(query_facts, key_part):
    same_family = query_facts[0][:, None] == key_part[0][None, :]
    causal = key_part[1][None, :] <= query_facts[1][:, None]
    reaches = (
        key_part[2][None, :]
        | (key_part[3][None, :] == query_facts[3][:, None]) & key_part[4][None, :]
    )
    return same_family & causal & reaches


def key_slice(keys_heads, values_heads, key_facts, query_facts, first_row, span_rows):
    key_block = lax.dynamic_slice_in_dim(keys_heads, first_row, span_rows, 0)
    value_block = lax.dynamic_slice_in_dim(values_heads, first_row, span_rows, 0)
    key_part = tuple(
        (
            lax.dynamic_slice_in_dim(member_array, first_row, span_rows, 0)
            for member_array in key_facts
        )
    )
    return (key_block, value_block, visible(query_facts, key_part))


def block_scores(query_heads, key_block, visible_mask):
    scores = jnp.einsum(
        "qhd,khd->hqk", query_heads, key_block, preferred_element_type=jnp.float32
    ) * HDIM ** (-0.5)
    return jnp.where(visible_mask[None], scores, masked_value)


def score_grads(
    query_heads, grad_heads, log_total, row_delta, key_block, value_block, visible_mask
):
    scores = block_scores(query_heads, key_block, visible_mask)
    prob_table = jnp.where(visible_mask[None], jnp.exp(scores - log_total[:, :, None]), 0.0)
    grad_probs = jnp.einsum(
        "qhd,khd->hqk", grad_heads, value_block, preferred_element_type=jnp.float32
    )
    grad_scores = (prob_table * (grad_probs - row_delta[:, :, None])).astype(jnp.bfloat16)
    return (prob_table.astype(jnp.bfloat16), grad_scores)


def gate_grads(grad_mixed, gate_pre, up_pre):
    sigmoid = jax.nn.sigmoid(gate_pre)
    grad_gate = grad_mixed * up_pre * sigmoid * (1.0 + gate_pre * (1.0 - sigmoid))
    grad_up = grad_mixed * gate_pre * sigmoid
    return (grad_gate.astype(jnp.bfloat16), grad_up.astype(jnp.bfloat16))


def norm_backward(grad_normed, values, inverse, gain):
    scaled = grad_normed * gain[None, :]
    grad_gain = jnp.sum(grad_normed * values * inverse, axis=0)
    grad_values = inverse * scaled - values * inverse**3 * jnp.mean(
        scaled * values, axis=-1, keepdims=True
    )
    return (grad_gain, grad_values)


def attention_weights(w_query, w_key, w_value, w_output, attn_gain, ffn_gain):
    return (
        lax.all_gather(w_query, ("grp", "ctx"), axis=0, tiled=True),
        lax.all_gather(w_key, ("grp", "ctx"), axis=0, tiled=True),
        lax.all_gather(w_value, ("grp", "ctx"), axis=0, tiled=True),
        lax.all_gather(w_output, ("grp", "ctx"), axis=0, tiled=True),
        lax.all_gather(attn_gain, ("grp", "ctx"), axis=0, tiled=True),
        lax.all_gather(ffn_gain, ("grp", "ctx"), axis=0, tiled=True),
    )


def ffn_rows_gather(w_gate, w_up, w_down):
    return (
        lax.all_gather(w_gate, "grp", axis=0, tiled=True),
        lax.all_gather(w_up, "grp", axis=0, tiled=True),
        lax.all_gather(w_down, "grp", axis=1, tiled=True),
    )


def local(
    tokens_in,
    cotangent,
    w_query,
    w_key,
    w_value,
    w_output,
    w_gate,
    w_up,
    w_down,
    attn_gain,
    ffn_gain,
    cont_len,
    deal_order,
    clip_threshold,
):
    row_count = tokens_in.shape[0]
    model_width = tokens_in.shape[1]
    tile_count = deal_order.shape[1]
    group_rows = tile_count * BLK
    lengths = cont_len[0]
    my_index = lax.axis_index("ctx")
    tile_offsets = jnp.arange(BLK, dtype=jnp.int32)
    stored_logical = (deal_order[0][:, None] * BLK + tile_offsets[None, :]).reshape(group_rows)
    key_facts = token_facts(stored_logical, lengths)
    query_facts = tuple(
        (
            lax.dynamic_slice_in_dim(member_array, my_index * row_count, row_count, 0)
            for member_array in key_facts
        )
    )
    cosine, sine_vals = rope_angles(query_facts[5])
    key_step = math.gcd(group_rows, 512)
    key_blocks = group_rows // key_step
    full_query, full_key, full_value, full_output, gain_one, gain_two = attention_weights(
        w_query, w_key, w_value, w_output, attn_gain, ffn_gain
    )
    residual = tokens_in.astype(jnp.float32)
    inverse_one = lax.rsqrt(jnp.mean(residual * residual, axis=-1, keepdims=True) + norm_eps)
    gain_one_f = gain_one.astype(jnp.float32)
    gain_two_f = gain_two.astype(jnp.float32)
    normed_one = (residual * inverse_one * gain_one_f).astype(jnp.bfloat16)
    query_rot = rotate(
        jnp.dot(normed_one, full_query, preferred_element_type=jnp.float32), cosine, sine_vals, 1.0
    ).astype(jnp.bfloat16)
    key_rot = rotate(
        jnp.dot(normed_one, full_key, preferred_element_type=jnp.float32), cosine, sine_vals, 1.0
    ).astype(jnp.bfloat16)
    value_low = jnp.dot(normed_one, full_value, preferred_element_type=jnp.float32).astype(
        jnp.bfloat16
    )
    keys_all, values_all = (
        lax.all_gather(key_rot, "ctx", axis=0, tiled=True),
        lax.all_gather(value_low, "ctx", axis=0, tiled=True),
    )
    query_heads = query_rot.reshape(row_count, HEADS, HDIM)
    keys_heads = keys_all.reshape(group_rows, HEADS, HDIM)
    values_heads = values_all.reshape(group_rows, HEADS, HDIM)

    def stats_step(block_index, state_carry):
        key_block, value_block, visible_mask = key_slice(
            keys_heads, values_heads, key_facts, query_facts, block_index * key_step, key_step
        )

        def stats_busy(carry):
            run_max, run_sum, head_max = carry
            scores = block_scores(query_heads, key_block, visible_mask)
            block_max = jnp.max(scores, axis=2)
            new_max = jnp.maximum(run_max, block_max)
            exp_table = jnp.where(visible_mask[None], jnp.exp(scores - new_max[:, :, None]), 0.0)
            new_sum = run_sum * jnp.exp(run_max - new_max) + jnp.sum(exp_table, axis=2)
            return (new_max, new_sum, jnp.maximum(head_max, jnp.max(block_max, axis=1)))

        return lax.cond(jnp.any(visible_mask), stats_busy, lambda carry: carry, state_carry)

    start_state = (
        jnp.full((HEADS, row_count), masked_value, jnp.float32),
        jnp.zeros((HEADS, row_count), jnp.float32),
        jnp.full((HEADS,), masked_value, jnp.float32),
    )
    run_max, run_sum, head_max = lax.fori_loop(0, key_blocks, stats_step, start_state)
    log_total = run_max + jnp.log(run_sum)

    def output_step(block_index, running):
        key_block, value_block, visible_mask = key_slice(
            keys_heads, values_heads, key_facts, query_facts, block_index * key_step, key_step
        )

        def output_busy(total):
            scores = block_scores(query_heads, key_block, visible_mask)
            prob_low = jnp.where(
                visible_mask[None], jnp.exp(scores - log_total[:, :, None]), 0.0
            ).astype(jnp.bfloat16)
            return total + jnp.einsum(
                "hqk,khd->qhd", prob_low, value_block, preferred_element_type=jnp.float32
            )

        return lax.cond(jnp.any(visible_mask), output_busy, lambda total: total, running)

    attended = lax.fori_loop(
        0, key_blocks, output_step, jnp.zeros((row_count, HEADS, HDIM), jnp.float32)
    )
    attn_low = attended.reshape(row_count, model_width).astype(jnp.bfloat16)
    after_attn = residual + branch_scale * jnp.dot(
        attn_low, full_output, preferred_element_type=jnp.float32
    )
    inverse_two = lax.rsqrt(jnp.mean(after_attn * after_attn, axis=-1, keepdims=True) + norm_eps)
    normed_two = (after_attn * inverse_two * gain_two_f).astype(jnp.bfloat16)
    gate_cols, up_cols, down_cols = ffn_rows_gather(w_gate, w_up, w_down)
    normed_rows = lax.all_gather(normed_two, "ctx", axis=0, tiled=True)
    gate_pre = jnp.dot(normed_rows, gate_cols, preferred_element_type=jnp.float32)
    up_pre = jnp.dot(normed_rows, up_cols, preferred_element_type=jnp.float32)
    mixed = (jax.nn.silu(gate_pre) * up_pre).astype(jnp.bfloat16)
    branch_ffn = lax.psum_scatter(
        jnp.dot(mixed, down_cols, preferred_element_type=jnp.float32).astype(jnp.bfloat16),
        "ctx",
        scatter_dimension=0,
        tiled=True,
    ).astype(jnp.float32)
    output = (after_attn + branch_scale * branch_ffn).astype(jnp.bfloat16)
    grad_out = cotangent.astype(jnp.float32)
    grad_branch = (branch_scale * grad_out).astype(jnp.bfloat16)
    gate_again, up_again, down_again = ffn_rows_gather(w_gate, w_up, w_down)
    grad_rows = lax.all_gather(grad_branch, "ctx", axis=0, tiled=True)
    grad_mixed = jnp.dot(grad_rows, down_again.T, preferred_element_type=jnp.float32)
    grad_down = jnp.dot(mixed.T, grad_rows, preferred_element_type=jnp.float32)
    grad_gate_low, grad_up_low = gate_grads(grad_mixed, gate_pre, up_pre)
    grad_gate = jnp.dot(normed_rows.T, grad_gate_low, preferred_element_type=jnp.float32)
    grad_up = jnp.dot(normed_rows.T, grad_up_low, preferred_element_type=jnp.float32)
    grad_normed_two = lax.psum_scatter(
        (
            jnp.dot(grad_gate_low, gate_again.T, preferred_element_type=jnp.float32)
            + jnp.dot(grad_up_low, up_again.T, preferred_element_type=jnp.float32)
        ).astype(jnp.bfloat16),
        "ctx",
        scatter_dimension=0,
        tiled=True,
    ).astype(jnp.float32)
    ffn_stack = jnp.stack([grad_gate, grad_up, grad_down.T], axis=0)
    ffn_summed = lax.psum_scatter(
        ffn_stack.astype(jnp.bfloat16), "grp", scatter_dimension=1, tiled=True
    ).astype(jnp.float32)
    grad_gain_two, grad_second = norm_backward(grad_normed_two, after_attn, inverse_two, gain_two_f)
    grad_resid = grad_out + grad_second
    back_query, back_key, back_value, back_output, back_gain_one, back_gain_two = attention_weights(
        w_query, w_key, w_value, w_output, attn_gain, ffn_gain
    )
    grad_branch_attn = (branch_scale * grad_resid).astype(jnp.bfloat16)
    grad_w_output = jnp.dot(attn_low.T, grad_branch_attn, preferred_element_type=jnp.float32)
    grad_attn = jnp.dot(grad_branch_attn, back_output.T, preferred_element_type=jnp.float32).astype(
        jnp.bfloat16
    )
    grad_heads = grad_attn.reshape(row_count, HEADS, HDIM)
    row_delta = jnp.sum(grad_heads.astype(jnp.float32) * attended, axis=2).T

    def back_step(grad_q, block_index):
        key_block, value_block, visible_mask = key_slice(
            keys_heads, values_heads, key_facts, query_facts, block_index * key_step, key_step
        )

        def back_busy(current):
            prob_low, grad_scores = score_grads(
                query_heads, grad_heads, log_total, row_delta, key_block, value_block, visible_mask
            )
            updated = current + jnp.einsum(
                "hqk,khd->qhd", grad_scores, key_block, preferred_element_type=jnp.float32
            )
            grad_keys = jnp.einsum(
                "hqk,qhd->khd", grad_scores, query_heads, preferred_element_type=jnp.float32
            ) * HDIM ** (-0.5)
            grad_values = jnp.einsum(
                "hqk,qhd->khd", prob_low, grad_heads, preferred_element_type=jnp.float32
            )
            return (
                updated,
                (
                    grad_keys.reshape(key_step, model_width),
                    grad_values.reshape(key_step, model_width),
                ),
            )

        def quiet(current):
            empty = jnp.zeros((key_step, model_width), jnp.float32)
            return (current, (empty, empty))

        return lax.cond(jnp.any(visible_mask), back_busy, quiet, grad_q)

    grad_q_heads, key_terms = lax.scan(
        back_step,
        jnp.zeros((row_count, HEADS, HDIM), jnp.float32),
        jnp.arange(key_blocks, dtype=jnp.int32),
    )
    key_sum, value_sum = (
        lax.psum_scatter(
            key_terms[0].reshape(group_rows, model_width).astype(jnp.bfloat16),
            "ctx",
            scatter_dimension=0,
            tiled=True,
        ).astype(jnp.float32),
        lax.psum_scatter(
            key_terms[1].reshape(group_rows, model_width).astype(jnp.bfloat16),
            "ctx",
            scatter_dimension=0,
            tiled=True,
        ).astype(jnp.float32),
    )
    grad_query_rot = grad_q_heads.reshape(row_count, model_width) * HDIM ** (-0.5)
    grad_query = rotate(grad_query_rot, cosine, sine_vals, -1.0).astype(jnp.bfloat16)
    grad_key = rotate(key_sum, cosine, sine_vals, -1.0).astype(jnp.bfloat16)
    grad_value = value_sum.astype(jnp.bfloat16)
    grad_w_query = jnp.dot(normed_one.T, grad_query, preferred_element_type=jnp.float32)
    grad_w_key = jnp.dot(normed_one.T, grad_key, preferred_element_type=jnp.float32)
    grad_w_value = jnp.dot(normed_one.T, grad_value, preferred_element_type=jnp.float32)
    grad_normed_one = (
        jnp.dot(grad_query, back_query.T, preferred_element_type=jnp.float32)
        + jnp.dot(grad_key, back_key.T, preferred_element_type=jnp.float32)
        + jnp.dot(grad_value, back_value.T, preferred_element_type=jnp.float32)
    )
    grad_gain_one, grad_first = norm_backward(grad_normed_one, residual, inverse_one, gain_one_f)
    grad_input = grad_resid + grad_first
    gain_pair = jnp.stack([grad_gain_one, grad_gain_two], axis=1)
    summed = (
        lax.psum_scatter(grad_w_query, ("grp", "ctx"), scatter_dimension=0, tiled=True),
        lax.psum_scatter(grad_w_key, ("grp", "ctx"), scatter_dimension=0, tiled=True),
        lax.psum_scatter(grad_w_value, ("grp", "ctx"), scatter_dimension=0, tiled=True),
        lax.psum_scatter(grad_w_output, ("grp", "ctx"), scatter_dimension=0, tiled=True),
        lax.psum_scatter(gain_pair, ("grp", "ctx"), scatter_dimension=0, tiled=True),
    )
    maxima = lax.pmax(head_max, ("grp", "ctx"))
    limit_value = clip_threshold[0].astype(jnp.float32)
    clip_factor = jnp.sqrt(limit_value / jnp.maximum(maxima, limit_value))
    column_factor = jnp.repeat(clip_factor, HDIM)
    clipped_query = w_query.astype(jnp.float32) * column_factor[None, :]
    clipped_key = w_key.astype(jnp.float32) * column_factor[None, :]
    return (
        output,
        grad_input,
        summed[0],
        summed[1],
        summed[2],
        summed[3],
        ffn_summed[0],
        ffn_summed[1],
        ffn_summed[2].T,
        summed[4][:, 0],
        summed[4][:, 1],
        maxima,
        clip_factor,
        clipped_query,
        clipped_key,
    )


def solution(mesh):
    in_specs = (
        P(("grp", "ctx"), None),
        P(("grp", "ctx"), None),
        P(("grp", "ctx"), None),
        P(("grp", "ctx"), None),
        P(("grp", "ctx"), None),
        P(("grp", "ctx"), None),
        P("grp", "ctx"),
        P("grp", "ctx"),
        P("ctx", "grp"),
        P(("grp", "ctx")),
        P(("grp", "ctx")),
        P("grp", None),
        P("grp", None),
        P(),
    )
    out_specs = (
        P(("grp", "ctx"), None),
        P(("grp", "ctx"), None),
        P(("grp", "ctx"), None),
        P(("grp", "ctx"), None),
        P(("grp", "ctx"), None),
        P(("grp", "ctx"), None),
        P("grp", "ctx"),
        P("grp", "ctx"),
        P("ctx", "grp"),
        P(("grp", "ctx")),
        P(("grp", "ctx")),
        P(),
        P(),
        P(("grp", "ctx"), None),
        P(("grp", "ctx"), None),
    )
    return jax.shard_map(local, mesh=mesh, in_specs=in_specs, out_specs=out_specs, check_vma=False)
```

profile of v0, /device:TPU:8, one launch (start us, length us, event | category | flops | bytes accessed | tf_op | source)
XLA Modules:
  0.0 4151.7 jit_solution(17834382039672764778)
XLA Ops:
  112.3 76.7 %all-gather.12.cloned.1.call-done = bf16[2304,2304]{1,0:T(8,128)(2,1)} async-done(((bf16[72,2304]{1,0:T(8,128)(2,1)}), bf16[2304,2304]{1,0:T(8,128)(2,1)}) %all-gather.12.cloned.1.call-update) | async-done | bytes 10616848 | tf_op jit(solution)/shard_map/all_gather | solution.py:119
  202.3 75.6 %all-gather.18.cloned.1.call-done = bf16[2304,2304]{1,0:T(8,128)(2,1)} async-done(((bf16[72,2304]{1,0:T(8,128)(2,1)}), bf16[2304,2304]{1,0:T(8,128)(2,1)}) %all-gather.18.cloned.1.call-update) | async-done | bytes 10616848 | tf_op jit(solution)/shard_map/all_gather | solution.py:120
  294.7 149.3 %all-gather.14.cloned.1.call-done = bf16[4096,2304]{0,1:T(8,128)(2,1)} async-done(((bf16[512,2304]{0,1:T(8,128)(2,1)}), bf16[4096,2304]{0,1:T(8,128)(2,1)}) %all-gather.14.cloned.1.call-update) | async-done | bytes 18874384 | tf_op jit(solution)/shard_map/all_gather | solution.py:187
  444.0 335.9 %while.50 = (s32[]{:T(128)}, f32[36,512]{1,0:T(8,128)S(1)}, f32[36,512]{1,0:T(8,128)S(1)}, f32[36]{0:T(128)S(1)}, s32[512]{0:T(512)S(1)}, /*index=5*/s32[4096]{0...) while((s32[]{:T(128)}, f32[36,512]{1,0:T(8,128)S(1)}, ...), condition=%wide.region_9.10_spmd, body=%wide.region_2.9_spmd.sunk | while | flops 1295028224 | bytes 81990040 | solution.py:215
  807.3 177.0 %while.51 = (s32[]{:T(128)}, f32[512,36,64]{0,2,1:T(8,128)}, s32[512]{0:T(512)S(1)}, s32[4096]{0:T(1024)}, s32[4096]{0:T(1024)}, /*index=5*/s32[512]{0:T(512)S(1...) while((s32[]{:T(128)}, f32[512,36,64]{0,2,1:T(8,128)}, ...), condition=%wide.region_14.15_spmd, body=%wide.region_10.14_spmd.sunk | while | flops 2466381824 | bytes 17142060 | solution.py:234
  1008.1 162.7 %all-gather.24.cloned.1.call-done = bf16[4096,2304]{1,0:T(8,128)(2,1)} async-done(((bf16[512,2304]{1,0:T(8,128)(2,1)}), bf16[4096,2304]{1,0:T(8,128)(2,1)}) %all-gather.24.cloned.1.call-update) | async-done | bytes 18874384 | tf_op jit(solution)/shard_map/all_gather | solution.py:244
  1270.1 167.0 %all-gather.32.cloned.1.call-done = bf16[4096,2304]{1,0:T(8,128)(2,1)} async-done(((bf16[512,2304]{1,0:T(8,128)(2,1)}), bf16[4096,2304]{1,0:T(8,128)(2,1)}) %all-gather.32.cloned.1.call-update) | async-done | bytes 18874384 | tf_op jit(solution)/shard_map/all_gather | solution.py:258
  1541.1 163.1 %reduce-scatter.15.cloned.1.call-done = bf16[512,2304]{1,0:T(8,128)(2,1)} async-done(((bf16[4096,2304]{1,0:T(8,128)(2,1)}), bf16[512,2304]{1,0:T(8,128)(2,1)}) %reduce-scatter.15.cloned.1.call-update) | async-done | bytes 2359312 | tf_op jit(solution)/shard_map/reduce_scatter | solution.py:264
  1709.3 183.6 %reduce-scatter.13.cloned.1.call-done = bf16[512,2304]{1,0:T(8,128)(2,1)} async-done(((bf16[4096,2304]{1,0:T(8,128)(2,1)}), bf16[512,2304]{1,0:T(8,128)(2,1)}) %reduce-scatter.13.cloned.1.call-update) | async-done | bytes 2359312 | tf_op jit(solution)/shard_map/reduce_scatter | solution.py:248
  1920.2 836.6 %while.52 = (s32[]{:T(128)}, f32[512,36,64]{0,2,1:T(8,128)}, bf16[8,512,2304]{2,1,0:T(8,128)(2,1)}, bf16[8,512,2304]{2,1,0:T(8,128)(2,1)}, s32[512]{0:T(512)S(1)...) while((s32[]{:T(128)}, f32[512,36,64]{0,2,1:T(8,128)}, ...), condition=%wide.region_24.25_spmd, body=%wide.region_20.24_spmd.sunk | while | flops 6158680064 | bytes 267637744 | solution.py:322
  1927.5 84.2 %conditional.8 = (f32[512,36,64]{0,2,1:T(8,128)}, bf16[1,512,2304]{1,2,0:T(8,128)(2,1)}, bf16[1,512,2304]{1,2,0:T(8,128)(2,1)}) conditional(s32[]{:T(128)} %convert_element_type.264, f32[512,36,64]{0,2,1:T(8,128)} %get-tuple-element.1497, (pred[512,512]{0,1:T(8,128)(4,1)S(1)}, bf16[4096,36,64]{0,2,1:T(8,128)(2,1)}, s32[]{:T(128)}, ...), branch_computations={%region_22.22_spmd, %region_23.23_spmd} | conditional | flops 6156582912 | bytes 248473216 | solution.py:320
  2032.0 84.2 %conditional.8 = (f32[512,36,64]{0,2,1:T(8,128)}, bf16[1,512,2304]{1,2,0:T(8,128)(2,1)}, bf16[1,512,2304]{1,2,0:T(8,128)(2,1)}) conditional(s32[]{:T(128)} %convert_element_type.264, f32[512,36,64]{0,2,1:T(8,128)} %get-tuple-element.1497, (pred[512,512]{0,1:T(8,128)(4,1)S(1)}, bf16[4096,36,64]{0,2,1:T(8,128)(2,1)}, s32[]{:T(128)}, ...), branch_computations={%region_22.22_spmd, %region_23.23_spmd} | conditional | flops 6156582912 | bytes 248473216 | solution.py:320
  2136.5 84.2 %conditional.8 = (f32[512,36,64]{0,2,1:T(8,128)}, bf16[1,512,2304]{1,2,0:T(8,128)(2,1)}, bf16[1,512,2304]{1,2,0:T(8,128)(2,1)}) conditional(s32[]{:T(128)} %convert_element_type.264, f32[512,36,64]{0,2,1:T(8,128)} %get-tuple-element.1497, (pred[512,512]{0,1:T(8,128)(4,1)S(1)}, bf16[4096,36,64]{0,2,1:T(8,128)(2,1)}, s32[]{:T(128)}, ...), branch_computations={%region_22.22_spmd, %region_23.23_spmd} | conditional | flops 6156582912 | bytes 248473216 | solution.py:320
  2240.9 84.2 %conditional.8 = (f32[512,36,64]{0,2,1:T(8,128)}, bf16[1,512,2304]{1,2,0:T(8,128)(2,1)}, bf16[1,512,2304]{1,2,0:T(8,128)(2,1)}) conditional(s32[]{:T(128)} %convert_element_type.264, f32[512,36,64]{0,2,1:T(8,128)} %get-tuple-element.1497, (pred[512,512]{0,1:T(8,128)(4,1)S(1)}, bf16[4096,36,64]{0,2,1:T(8,128)(2,1)}, s32[]{:T(128)}, ...), branch_computations={%region_22.22_spmd, %region_23.23_spmd} | conditional | flops 6156582912 | bytes 248473216 | solution.py:320
  2345.5 84.2 %conditional.8 = (f32[512,36,64]{0,2,1:T(8,128)}, bf16[1,512,2304]{1,2,0:T(8,128)(2,1)}, bf16[1,512,2304]{1,2,0:T(8,128)(2,1)}) conditional(s32[]{:T(128)} %convert_element_type.264, f32[512,36,64]{0,2,1:T(8,128)} %get-tuple-element.1497, (pred[512,512]{0,1:T(8,128)(4,1)S(1)}, bf16[4096,36,64]{0,2,1:T(8,128)(2,1)}, s32[]{:T(128)}, ...), branch_computations={%region_22.22_spmd, %region_23.23_spmd} | conditional | flops 6156582912 | bytes 248473216 | solution.py:320
  2450.2 84.2 %conditional.8 = (f32[512,36,64]{0,2,1:T(8,128)}, bf16[1,512,2304]{1,2,0:T(8,128)(2,1)}, bf16[1,512,2304]{1,2,0:T(8,128)(2,1)}) conditional(s32[]{:T(128)} %convert_element_type.264, f32[512,36,64]{0,2,1:T(8,128)} %get-tuple-element.1497, (pred[512,512]{0,1:T(8,128)(4,1)S(1)}, bf16[4096,36,64]{0,2,1:T(8,128)(2,1)}, s32[]{:T(128)}, ...), branch_computations={%region_22.22_spmd, %region_23.23_spmd} | conditional | flops 6156582912 | bytes 248473216 | solution.py:320
  2554.9 84.2 %conditional.8 = (f32[512,36,64]{0,2,1:T(8,128)}, bf16[1,512,2304]{1,2,0:T(8,128)(2,1)}, bf16[1,512,2304]{1,2,0:T(8,128)(2,1)}) conditional(s32[]{:T(128)} %convert_element_type.264, f32[512,36,64]{0,2,1:T(8,128)} %get-tuple-element.1497, (pred[512,512]{0,1:T(8,128)(4,1)S(1)}, bf16[4096,36,64]{0,2,1:T(8,128)(2,1)}, s32[]{:T(128)}, ...), branch_computations={%region_22.22_spmd, %region_23.23_spmd} | conditional | flops 6156582912 | bytes 248473216 | solution.py:320
  2659.5 83.7 %conditional.8 = (f32[512,36,64]{0,2,1:T(8,128)}, bf16[1,512,2304]{1,2,0:T(8,128)(2,1)}, bf16[1,512,2304]{1,2,0:T(8,128)(2,1)}) conditional(s32[]{:T(128)} %convert_element_type.264, f32[512,36,64]{0,2,1:T(8,128)} %get-tuple-element.1497, (pred[512,512]{0,1:T(8,128)(4,1)S(1)}, bf16[4096,36,64]{0,2,1:T(8,128)(2,1)}, s32[]{:T(128)}, ...), branch_computations={%region_22.22_spmd, %region_23.23_spmd} | conditional | flops 6156582912 | bytes 248473216 | solution.py:320
  2879.3 64.0 %reduce-scatter.19.cloned.1.call-done = bf16[512,2304]{1,0:T(8,128)(2,1)} async-done(((bf16[4096,2304]{1,0:T(8,128)(2,1)}), bf16[512,2304]{1,0:T(8,128)(2,1)}) %reduce-scatter.19.cloned.1.call-update) | async-done | bytes 2359312 | tf_op jit(solution)/shard_map/reduce_scatter | solution.py:334
  2961.2 170.7 %reduce-scatter.17.cloned.1.call-done = bf16[512,2304]{1,0:T(8,128)(2,1)} async-done(((bf16[4096,2304]{1,0:T(8,128)(2,1)}), bf16[512,2304]{1,0:T(8,128)(2,1)}) %reduce-scatter.17.cloned.1.call-update) | async-done | bytes 2359312 | tf_op jit(solution)/shard_map/reduce_scatter | solution.py:328
  3353.1 111.2 %reduce-scatter.27.cloned.1.call-done = f32[72,2304]{1,0:T(8,128)} async-done(((f32[2304,2304]{1,0:T(8,128)}), f32[72,2304]{1,0:T(8,128)}) %reduce-scatter.27.cloned.1.call-update) | async-done | bytes 663568 | tf_op jit(solution)/shard_map/reduce_scatter | solution.py:360
  3464.3 227.1 %reduce-scatter.25.cloned.1.call-done = f32[72,2304]{1,0:T(8,128)} async-done(((f32[2304,2304]{1,0:T(8,128)}), f32[72,2304]{1,0:T(8,128)}) %reduce-scatter.25.cloned.1.call-update) | async-done | bytes 663568 | tf_op jit(solution)/shard_map/reduce_scatter | solution.py:359
  3691.4 226.2 %reduce-scatter.23.cloned.1.call-done = f32[72,2304]{1,0:T(8,128)} async-done(((f32[2304,2304]{1,0:T(8,128)}), f32[72,2304]{1,0:T(8,128)}) %reduce-scatter.23.cloned.1.call-update) | async-done | bytes 663568 | tf_op jit(solution)/shard_map/reduce_scatter | solution.py:358
  3917.6 227.1 %reduce-scatter.21.cloned.1.call-done = f32[72,2304]{1,0:T(8,128)} async-done(((f32[2304,2304]{1,0:T(8,128)}), f32[72,2304]{1,0:T(8,128)}) %reduce-scatter.21.cloned.1.call-update) | async-done | bytes 663568 | tf_op jit(solution)/shard_map/reduce_scatter | solution.py:357
  (580 shorter events, 2531.2 us)
Async XLA Ops:
  7.2 92.9 %all-gather.16.cloned.1.call-start = ((), (), s32[]{:S(2)}) async-start(), calls=%async_computation.11 | async-start | bytes 10948608 | tf_op jit(solution)/shard_map/all_gather | solution.py:118
  7.9 181.1 %all-gather.12.cloned.1.call-start = ((), (), s32[]{:S(2)}) async-start(), calls=%async_computation.9 | async-start | bytes 10948608 | tf_op jit(solution)/shard_map/all_gather | solution.py:119
  8.7 269.3 %all-gather.18.cloned.1.call-start = ((), (), s32[]{:S(2)}) async-start(), calls=%async_computation.12 | async-start | bytes 10948608 | tf_op jit(solution)/shard_map/all_gather | solution.py:120
  9.4 434.6 %all-gather.14.cloned.1.call-start = ((), (), s32[]{:S(2)}) async-start(), calls=%async_computation.10 | async-start | bytes 21233664 | tf_op jit(solution)/shard_map/all_gather | solution.py:187
  52.3 225.7 %copy-start.34 = (f32[2304]{0:T(1024)}, f32[2304]{0:T(1024)S(1)}, u32[]{:S(2)}) copy-start(f32[2304]{0:T(1024)S(1)} %convert_element_type.144) | copy-start | bytes 27652
  202.0 577.9 %all-gather.20.cloned.1.call-start = ((), (), s32[]{:S(2)}) async-start(), calls=%async_computation.13 | async-start | bytes 21233664 | tf_op jit(solution)/shard_map/all_gather | solution.py:188
  289.0 700.3 %all-gather.22.cloned.1.call-start = ((), (), s32[]{:S(2)}) async-start(), calls=%async_computation.14 | async-start | bytes 10948608 | tf_op jit(solution)/shard_map/all_gather | solution.py:121
  289.6 718.5 %all-gather.28.cloned.1.call-start = ((), (), s32[]{:S(2)}) async-start(), calls=%async_computation.17 | async-start | bytes 4423680 | tf_op jit(solution)/shard_map/all_gather | solution.py:130
  290.3 880.5 %all-gather.24.cloned.1.call-start = ((), (), s32[]{:S(2)}) async-start(), calls=%async_computation.15 | async-start | bytes 21233664 | tf_op jit(solution)/shard_map/all_gather | solution.py:244
  1004.7 216.4 %all-gather.26.cloned.1.call-start = ((), (), s32[]{:S(2)}) async-start(), calls=%async_computation.16 | async-start | bytes 4423680 | tf_op jit(solution)/shard_map/all_gather | solution.py:129
  1005.5 264.6 %all-gather.30.cloned.1.call-start = ((), (), s32[]{:S(2)}) async-start(), calls=%async_computation.18 | async-start | bytes 4423680 | tf_op jit(solution)/shard_map/all_gather | solution.py:131
  1006.0 431.0 %all-gather.32.cloned.1.call-start = ((), (), s32[]{:S(2)}) async-start(), calls=%async_computation.20 | async-start | bytes 21233664 | tf_op jit(solution)/shard_map/all_gather | solution.py:258
  1008.0 696.1 %reduce-scatter.15.cloned.1.call-start = ((), (), s32[]{:S(2)}) async-start(), calls=%async_computation.21 | async-start | bytes 21233664 | tf_op jit(solution)/shard_map/reduce_scatter | solution.py:264
  1517.7 375.2 %reduce-scatter.13.cloned.1.call-start = ((), (), s32[]{:S(2)}) async-start(), calls=%async_computation.19 | async-start | bytes 21233664 | tf_op jit(solution)/shard_map/reduce_scatter | solution.py:248
  1541.0 351.9 %copy-start.11 = (bf16[512,2304]{1,0:T(8,128)(2,1)S(1)}, bf16[512,2304]{1,0:T(8,128)(2,1)}, u32[]{:S(2)}) copy-start(bf16[512,2304]{1,0:T(8,128)(2,1)} %param.27) | copy-start | bytes 7077892
  1541.0 351.9 %copy-start.42 = (f32[512]{0:T(512)S(1)}, f32[512]{0:T(512)}, u32[]{:S(2)}) copy-start(f32[512]{0:T(512)} %get-tuple-element.1031) | copy-start | bytes 6148
  1541.0 1402.3 %reduce-scatter.19.cloned.1.call-start = ((), (), s32[]{:S(2)}) async-start(), calls=%async_computation.23 | async-start | bytes 21233664 | tf_op jit(solution)/shard_map/reduce_scatter | solution.py:334
  2756.8 375.0 %reduce-scatter.17.cloned.1.call-start = ((), (), s32[]{:S(2)}) async-start(), calls=%async_computation.22 | async-start | bytes 21233664 | tf_op jit(solution)/shard_map/reduce_scatter | solution.py:328
  2757.4 479.6 %reduce-scatter.29.cloned.1.call-start = ((), (), s32[]{:S(2)}) async-start(), calls=%async_computation.28 | async-start | bytes 12533760
  2864.6 599.7 %reduce-scatter.27.cloned.1.call-start = ((), (), s32[]{:S(2)}) async-start(), calls=%async_computation.27 | async-start | bytes 21897216 | tf_op jit(solution)/shard_map/reduce_scatter | solution.py:360
  2879.2 812.2 %reduce-scatter.25.cloned.1.call-start = ((), (), s32[]{:S(2)}) async-start(), calls=%async_computation.26 | async-start | bytes 21897216 | tf_op jit(solution)/shard_map/reduce_scatter | solution.py:359
  2955.7 962.0 %reduce-scatter.23.cloned.1.call-start = ((), (), s32[]{:S(2)}) async-start(), calls=%async_computation.25 | async-start | bytes 21897216 | tf_op jit(solution)/shard_map/reduce_scatter | solution.py:358
  2961.2 175.2 %copy-start.26 = (f32[512,32]{0,1:T(8,128)S(1)}, f32[512,32]{0,1:T(8,128)}, u32[]{:S(2)}) copy-start(f32[512,32]{0,1:T(8,128)} %get-tuple-element.1026) | copy-start | bytes 196612
  3154.9 989.8 %reduce-scatter.21.cloned.1.call-start = ((), (), s32[]{:S(2)}) async-start(), calls=%async_computation.24 | async-start | bytes 21897216 | tf_op jit(solution)/shard_map/reduce_scatter | solution.py:357
  (73 other events, 1987.8 us)
Sparse Core Ops, SparseCore 0:
  11.0 88.9 all-gather.15
  103.1 85.8 all-gather.11
  192.0 85.8 all-gather.17
  280.0 163.9 all-gather.13
  446.0 166.4 all-gather.19
  615.4 88.3 all-gather.21
  705.7 45.9 all-gather.27
  1004.8 165.9 all-gather.23
  1172.7 48.4 all-gather.25
  1222.8 47.2 all-gather.29
  1271.7 165.3 all-gather.31
  1517.8 186.2 reduce-scatter.14
  1706.5 186.3 reduce-scatter.12
  2756.9 186.3 reduce-scatter.18
  2945.5 186.3 reduce-scatter.16
  3134.9 102.1 reduce-scatter.28
  3243.9 220.3 reduce-scatter.26
  3472.3 219.1 reduce-scatter.24
  3698.4 219.1 reduce-scatter.22
  3925.6 219.0 reduce-scatter.20
where the time goes:
time: 4170 us; the launch traced here: 4150 us
  waiting for transfers between devices  2130 us (51%)
  matrix products  1290 us (31%)
  local copies, waits for them, and re-layouts  324 us (8%)
  other arithmetic  244 us (6%)
  blocking collectives  128 us (3%)
    dot_general x16, matrix products, block_scores(): jnp.einsum('qhd,khd->hqk', query_heads, key_block, preferred_element_type...  283 us
    reduce_scatter x1, waiting for transfers between devices, local(): lax.psum_scatter(grad_w_value, ('grp', 'ctx'), scatter_dimension=0, tiled...  227 us
    reduce_scatter x1, waiting for transfers between devices, local(): lax.psum_scatter(grad_w_query, ('grp', 'ctx'), scatter_dimension=0, tiled...  227 us
    reduce_scatter x1, waiting for transfers between devices, local(): lax.psum_scatter(grad_w_key, ('grp', 'ctx'), scatter_dimension=0, tiled=T...  226 us
    dot_general x8, matrix products, score_grads(): jnp.einsum('qhd,khd->hqk', grad_heads, value_block, preferred_element_typ...  211 us
    reduce_scatter x1, waiting for transfers between devices, local(): lax.psum_scatter(jnp.dot(mixed, down_cols, preferred_element_type=jnp.flo...  184 us
    reduce_scatter x1, waiting for transfers between devices, local(): lax.psum_scatter(key_terms[0].reshape(group_rows, model_width).astype(jnp...  171 us
    all_gather x1, waiting for transfers between devices, local(): grad_rows = lax.all_gather(grad_branch, 'ctx', axis=0, tiled=True)  167 us
  transfers between devices with their start and end apart: 20, of which 17 were waited for; matrix products, arithmetic and copies ran while one was open for 22% of the time, Pallas kernels for 0%

commit v1 on v0

--- a/solution.py
+++ b/solution.py
@@ -1,8 +1,12 @@
+import functools
 import math
 
 import jax
 import jax.numpy as jnp
 from jax import lax
+from jax.experimental import pallas as pl
+from jax.experimental.pallas import tpu as pltpu
+from jax.sharding import Mesh
 from jax.sharding import PartitionSpec as P
 
 HEADS = 36
@@ -12,6 +16,19 @@
 NCONT = 8
 BLK = 64
 FAMTOK = 4096
+
+F32 = jnp.float32
+BF = jnp.bfloat16
+NH = HEADS // 4
+PART = NH * HDIM
+QB = 256
+KB = 1024
+KB_FWD = 512
+HEAD_STEP = 9
+NT = (((1,), (1,)), ((), ()))
+NN = (((1,), (0,)), ((), ()))
+TN = (((0,), (0,)), ((), ()))
+VMEM_ROOM = 56 * 1024 * 1024
 
 
 branch_scale = 1.4 / math.sqrt(40.0)
@@ -385,38 +402,688 @@
     )
 
 
+def mul(left, right, dims=NN):
+    return lax.dot_general(left, right, dims, preferred_element_type=F32)
+
+
+def room():
+    return pltpu.CompilerParams(vmem_limit_bytes=VMEM_ROOM)
+
+
+def straighten(w_ref, w_sc, thin):
+    for i in range(4):
+        for k in range(8):
+            w_sc[(i * 8 + k) * thin : (i * 8 + k + 1) * thin, :] = w_ref[k, i, :thin, :]
+
+
+def swing(values, cosine, sine_vals):
+    lane = lax.broadcasted_iota(jnp.int32, values.shape, 1)
+    other = jnp.where(
+        lane % HDIM < HDIM // 2,
+        pltpu.roll(values, 2 * HDIM - HDIM // 2, 1),
+        pltpu.roll(values, HDIM // 2, 1),
+    )
+    return values * cosine + other * sine_vals
+
+
+def project_kernel(x_ref, w_ref, cos_ref, sin_ref, q_ref, kv_ref, w_sc):
+    thin = w_sc.shape[0] // 32
+
+    @pl.when(pl.program_id(0) == 0)
+    def _():
+        straighten(w_ref, w_sc, thin)
+
+    y = mul(x_ref[...], w_sc[...])
+    cosine, sine_vals = cos_ref[...], sin_ref[...]
+    for k in range(NH):
+        piece = swing(y[:, k * 128 : (k + 1) * 128], cosine, sine_vals)
+        for j in range(2):
+            head = 2 * k + j
+            if head < NH:
+                q_ref[head] = (piece[:, j * HDIM : (j + 1) * HDIM] * 0.125).astype(BF)
+        if 2 * k + 1 > NH:
+            kv_ref[:, k * 128 : (k + 1) * 128] = piece.astype(BF)
+        elif 2 * k + 1 == NH:
+            kv_ref[:, k * 128 + HDIM : (k + 1) * 128] = piece[:, HDIM:].astype(BF)
+    kv_ref[:, :PART] = y[:, 2 * PART :].astype(BF)
+
+
+def project(normed, w_all, cosine, sine_vals):
+    rows, width = normed.shape
+    full = w_all.shape
+    return pl.pallas_call(
+        project_kernel,
+        out_shape=[
+            jax.ShapeDtypeStruct((NH, rows, HDIM), BF),
+            jax.ShapeDtypeStruct((rows, 2 * PART), BF),
+        ],
+        grid=(rows // QB,),
+        in_specs=[
+            pl.BlockSpec((QB, width), lambda i: (i, 0)),
+            pl.BlockSpec(full, lambda i: (0, 0, 0, 0), pipeline_mode=pl.Buffered(1)),
+            pl.BlockSpec((QB, 128), lambda i: (i, 0)),
+            pl.BlockSpec((QB, 128), lambda i: (i, 0)),
+        ],
+        out_specs=[
+            pl.BlockSpec((NH, QB, HDIM), lambda i: (0, i, 0)),
+            pl.BlockSpec((QB, 2 * PART), lambda i: (i, 0)),
+        ],
+        scratch_shapes=[pltpu.VMEM((width, full[3]), BF)],
+        compiler_params=room(),
+        name="project",
+    )(normed, w_all, cosine, sine_vals)
+
+
+def sort_kernel(order_ref, *refs):
+    k_ref, v_ref = refs[8:]
+    first = pl.program_id(0) * 4
+    for j in range(4):
+        from_mine = order_ref[first + j] < 32
+        tile = jnp.where(from_mine, refs[j][0], refs[4 + j][0])
+        rows = slice(j * BLK, (j + 1) * BLK)
+        for h in range(NH):
+            v_ref[h, rows, :] = tile[:, h * HDIM : (h + 1) * HDIM]
+            k_ref[h, rows, :] = tile[:, PART + h * HDIM : PART + (h + 1) * HDIM]
+
+
+def sort_keys(order, mine, theirs):
+    count = order.shape[0]
+    shape = (1, BLK, 2 * PART)
+    near = lambda j: pl.BlockSpec(shape, lambda i, o: (jnp.minimum(o[i * 4 + j], 31), 0, 0))
+    far = lambda j: pl.BlockSpec(shape, lambda i, o: (jnp.maximum(o[i * 4 + j] - 32, 0), 0, 0))
+    return pl.pallas_call(
+        sort_kernel,
+        out_shape=[jax.ShapeDtypeStruct((NH, count * BLK, HDIM), BF)] * 2,
+        grid_spec=pltpu.PrefetchScalarGridSpec(
+            num_scalar_prefetch=1,
+            grid=(count // 4,),
+            in_specs=[near(j) for j in range(4)] + [far(j) for j in range(4)],
+            out_specs=[pl.BlockSpec((NH, 4 * BLK, HDIM), lambda i, o: (0, i, 0))] * 2,
+        ),
+        compiler_params=room(),
+        name="sort_keys",
+    )(order, *([mine.reshape(32, BLK, 2 * PART)] * 4), *([theirs.reshape(32, BLK, 2 * PART)] * 4))
+
+
+def lane_tile(vals):
+    lane = lax.broadcasted_iota(jnp.int32, (1, QB), 1)
+    out = jnp.full((1, QB), vals[3], jnp.int32)
+    for j in (2, 1, 0):
+        out = jnp.where(lane < (j + 1) * BLK, vals[j], out)
+    return out, lane & (BLK - 1)
+
+
+def block_facts(tiles_ref, len_ref, block, step):
+    half_tiles = PLEN // BLK
+    t = [tiles_ref[block * 4 + j] for j in range(4)]
+    tile, within = lane_tile(t)
+    qpos = tile * BLK + within
+    tmax = jnp.maximum(jnp.maximum(t[0], t[1]), jnp.maximum(t[2], t[3]))
+    tmin = jnp.minimum(jnp.minimum(t[0], t[1]), jnp.minimum(t[2], t[3]))
+    per = step // BLK
+    is_cont = t[0] >= half_tiles
+    n_all = jnp.where(is_cont, PLEN // step, tmax // per + 1)
+    n_free = jnp.where(is_cont, PLEN // step, tmin // per)
+    conts = [jnp.maximum(t[j] - half_tiles, 0) // 4 for j in range(4)]
+    lens = lane_tile([len_ref[conts[j]] for j in range(4)])[0]
+    qin = qpos - PLEN - lane_tile(conts)[0] * CLEN
+    starts = [pl.multiple_of(PLEN + conts[j] * CLEN, CLEN) for j in range(4)]
+    kin = lax.broadcasted_iota(jnp.int32, (CLEN, QB), 0)
+    seen = lambda: (kin <= qin) & (kin < lens)
+    return qpos, is_cont, n_all, n_free, starts, seen
+
+
+def forward_kernel(
+    tiles_ref, len_ref, q_ref, k_ref, v_ref, o_ref, lse_ref, mx_ref, vt_sc, ot_sc
+):
+    block = pl.program_id(0)
+
+    @pl.when(block == 0)
+    def _():
+        def flip_head(h, carry):
+            vt_sc[h] = v_ref[h].T
+            return carry
+
+        lax.fori_loop(0, NH, flip_head, 0)
+
+    qpos, is_cont, n_all, n_free, starts, seen = block_facts(tiles_ref, len_ref, block, KB_FWD)
+
+    def heads(group, carry):
+        hs = [group * HEAD_STEP + j for j in range(HEAD_STEP)]
+        qs = [q_ref[h] for h in hs]
+
+        def update(scores, states, weigh):
+            out = []
+            for n, (s, (m, l, acc)) in enumerate(zip(scores, states)):
+                mn = jnp.maximum(m, jnp.max(s, axis=0, keepdims=True))
+                p = jnp.exp(s - mn)
+                al = jnp.exp(m - mn)
+                out.append(
+                    (
+                        mn,
+                        l * al + jnp.sum(p, axis=0, keepdims=True),
+                        acc * al + weigh(n, p.astype(BF)),
+                    )
+                )
+            return tuple(out)
+
+        def step(kb, states, masked):
+            base = pl.multiple_of(kb * KB_FWD, KB_FWD)
+            rows = pl.ds(base, KB_FWD)
+            scores = [mul(k_ref[h, rows, :], q, NT) for h, q in zip(hs, qs)]
+            if masked:
+                kpos = base + lax.broadcasted_iota(jnp.int32, (KB_FWD, QB), 0)
+                vis = kpos <= qpos
+                scores = [jnp.where(vis, s, masked_value) for s in scores]
+            return update(scores, states, lambda n, p: mul(vt_sc[hs[n], :, rows], p))
+
+        states = tuple(
+            (
+                jnp.full((1, QB), masked_value, F32),
+                jnp.zeros((1, QB), F32),
+                jnp.zeros((HDIM, QB), F32),
+            )
+            for _ in hs
+        )
+        states = lax.fori_loop(0, n_free, functools.partial(step, masked=False), states)
+        states = lax.fori_loop(n_free, n_all, functools.partial(step, masked=True), states)
+
+        def own(states):
+            vis = seen()
+            cols = lambda x, j: x[:, j * BLK : (j + 1) * BLK]
+            scores = []
+            for h, q in zip(hs, qs):
+                s = [
+                    mul(k_ref[h, pl.ds(starts[j], CLEN), :], q[j * BLK : (j + 1) * BLK], NT)
+                    for j in range(4)
+                ]
+                scores.append(jnp.where(vis, jnp.concatenate(s, axis=1), masked_value))
+            return update(
+                scores,
+                states,
+                lambda n, p: jnp.concatenate(
+                    [
+                        mul(vt_sc[hs[n], :, pl.ds(starts[j], CLEN)], cols(p, j))
+                        for j in range(4)
+                    ],
+                    axis=1,
+                ),
+            )
+
+        states = lax.cond(is_cont, own, lambda s: s, states)
+        for h, (m, l, acc) in zip(hs, states):
+            ot_sc[h] = acc / l
+            lse_ref[0, pl.ds(h, 1), :] = m + jnp.log(l)
+            mx_ref[0, pl.ds(h, 1), :] = m
+        return carry
+
+    lax.fori_loop(0, NH // HEAD_STEP, heads, 0)
+    for h in range(NH):
+        o_ref[:, h * HDIM : (h + 1) * HDIM] = ot_sc[h].T.astype(BF)
+
+
+def attention_forward(tiles, lengths, queries, keys, values):
+    rows = queries.shape[1]
+    count = rows // QB
+    span = keys.shape[1]
+    whole = pl.BlockSpec((NH, span, HDIM), lambda i, a, b: (0, 0, 0), pipeline_mode=pl.Buffered(1))
+    stat = pl.BlockSpec((1, NH, QB), lambda i, a, b: (i, 0, 0))
+    return pl.pallas_call(
+        forward_kernel,
+        out_shape=[
+            jax.ShapeDtypeStruct((rows, PART), BF),
+            jax.ShapeDtypeStruct((count, NH, QB), F32),
+            jax.ShapeDtypeStruct((count, NH, QB), F32),
+        ],
+        grid_spec=pltpu.PrefetchScalarGridSpec(
+            num_scalar_prefetch=2,
+            grid=(count,),
+            in_specs=[pl.BlockSpec((NH, QB, HDIM), lambda i, a, b: (0, i, 0)), whole, whole],
+            out_specs=[pl.BlockSpec((QB, PART), lambda i, a, b: (i, 0)), stat, stat],
+            scratch_shapes=[
+                pltpu.VMEM((NH, HDIM, span), BF),
+                pltpu.VMEM((NH, HDIM, QB), F32),
+            ],
+        ),
+        compiler_params=room(),
+        name="attention_forward",
+    )(tiles, lengths, queries, keys, values)
+
+
+def delta_kernel(g_ref, w_ref, o_ref, gh_ref, delta_ref):
+    grad = mul(g_ref[...], w_ref[...], NT).astype(BF)
+    ones = jnp.ones((8, HDIM), F32)
+    for h in range(NH):
+        cols = slice(h * HDIM, (h + 1) * HDIM)
+        gh_ref[h] = grad[:, cols]
+        prod = grad[:, cols].astype(F32) * o_ref[:, cols].astype(F32)
+        total = lax.dot_general(
+            ones, prod, NT, preferred_element_type=F32, precision=lax.Precision.HIGHEST
+        )
+        delta_ref[0, h : h + 1, :] = total[0:1]
+
+
+def attention_delta(grad_branch, w_out, attended):
+    rows, width = grad_branch.shape
+    count = rows // QB
+    return pl.pallas_call(
+        delta_kernel,
+        out_shape=[
+            jax.ShapeDtypeStruct((NH, rows, HDIM), BF),
+            jax.ShapeDtypeStruct((count, NH, QB), F32),
+        ],
+        grid=(count,),
+        in_specs=[
+            pl.BlockSpec((QB, width), lambda i: (i, 0)),
+            pl.BlockSpec((PART, width), lambda i: (0, 0), pipeline_mode=pl.Buffered(1)),
+            pl.BlockSpec((QB, PART), lambda i: (i, 0)),
+        ],
+        out_specs=[
+            pl.BlockSpec((NH, QB, HDIM), lambda i: (0, i, 0)),
+            pl.BlockSpec((1, NH, QB), lambda i: (i, 0, 0)),
+        ],
+        compiler_params=room(),
+        name="attention_delta",
+    )(grad_branch, w_out, attended)
+
+
+def backward_kernel(
+    tiles_ref, len_ref, q_ref, g_ref, lse_ref, delta_ref, k_ref, v_ref, dq_ref, dk_ref, dv_ref, kt_sc
+):
+    h = pl.program_id(0)
+    block = pl.program_id(1)
+
+    @pl.when(block == 0)
+    def _():
+        dk_ref[...] = jnp.zeros_like(dk_ref)
+        dv_ref[...] = jnp.zeros_like(dv_ref)
+        kt_sc[...] = k_ref[0].T
+
+    qpos, is_cont, n_all, n_free, starts, seen = block_facts(tiles_ref, len_ref, block, KB)
+    q = q_ref[0]
+    g = g_ref[0]
+    lse = lse_ref[0, pl.ds(h, 1), :]
+    delta = delta_ref[0, pl.ds(h, 1), :]
+
+    def step(kb, dqt, masked):
+        base = pl.multiple_of(kb * KB, KB)
+        rows = pl.ds(base, KB)
+        s = mul(k_ref[0, rows, :], q, NT)
+        dp = mul(v_ref[0, rows, :], g, NT)
+        if masked:
+            kpos = base + lax.broadcasted_iota(jnp.int32, (KB, QB), 0)
+            s = jnp.where(kpos <= qpos, s, masked_value)
+        p = jnp.exp(s - lse)
+        ds = (p * (dp - delta)).astype(BF)
+        dv_ref[0, rows, :] += mul(p.astype(BF), g)
+        dk_ref[0, rows, :] += mul(ds, q)
+        return dqt + mul(kt_sc[:, rows], ds)
+
+    dqt = jnp.zeros((HDIM, QB), F32)
+    dqt = lax.fori_loop(0, n_free, functools.partial(step, masked=False), dqt)
+    dqt = lax.fori_loop(n_free, n_all, functools.partial(step, masked=True), dqt)
+    dq_ref[0] = dqt.T * HDIM ** (-0.5)
+
+    @pl.when(is_cont)
+    def _():
+        part = lambda x, j: x[j * BLK : (j + 1) * BLK]
+        rows = [pl.ds(starts[j], CLEN) for j in range(4)]
+        s = jnp.concatenate([mul(k_ref[0, rows[j], :], part(q, j), NT) for j in range(4)], axis=1)
+        s = jnp.where(seen(), s, masked_value)
+        p = jnp.exp(s - lse)
+        dp = jnp.concatenate([mul(v_ref[0, rows[j], :], part(g, j), NT) for j in range(4)], axis=1)
+        ds = (p * (dp - delta)).astype(BF)
+        pb = p.astype(BF)
+        dq = []
+        for j in range(4):
+            cols = slice(j * BLK, (j + 1) * BLK)
+            dv_ref[0, rows[j], :] += mul(pb[:, cols], part(g, j))
+            dk_ref[0, rows[j], :] += mul(ds[:, cols], part(q, j))
+            dq.append(mul(kt_sc[:, rows[j]], ds[:, cols]))
+        dq_ref[0] += jnp.concatenate(dq, axis=1).T * HDIM ** (-0.5)
+
+
+def attention_backward(tiles, lengths, queries, grads, log_total, row_delta, keys, values):
+    rows = queries.shape[1]
+    count = rows // QB
+    span = keys.shape[1]
+    row = pl.BlockSpec((1, QB, HDIM), lambda h, i, a, b: (h, i, 0))
+    stat = pl.BlockSpec((1, NH, QB), lambda h, i, a, b: (i, 0, 0))
+    full = pl.BlockSpec((1, span, HDIM), lambda h, i, a, b: (h, 0, 0))
+    return pl.pallas_call(
+        backward_kernel,
+        out_shape=[
+            jax.ShapeDtypeStruct((NH, rows, HDIM), F32),
+            jax.ShapeDtypeStruct((NH, span, HDIM), F32),
+            jax.ShapeDtypeStruct((NH, span, HDIM), F32),
+        ],
+        grid_spec=pltpu.PrefetchScalarGridSpec(
+            num_scalar_prefetch=2,
+            grid=(NH, count),
+            in_specs=[row, row, stat, stat, full, full],
+            out_specs=[row, full, full],
+            scratch_shapes=[pltpu.VMEM((HDIM, span), BF)],
+        ),
+        compiler_params=room(),
+        name="attention_backward",
+    )(tiles, lengths, queries, grads, log_total, row_delta, keys, values)
+
+
+def restore_kernel(tiles_ref, *refs):
+    mine_ref, theirs_ref = refs[8:]
+
+    def write(out_ref):
+        for j in range(4):
+            rows = slice(j * BLK, (j + 1) * BLK)
+            for h in range(NH):
+                cols = slice(h * HDIM, (h + 1) * HDIM)
+                out_ref[rows, cols] = refs[4 + j][h].astype(BF)
+                out_ref[rows, PART + h * HDIM : PART + (h + 1) * HDIM] = refs[j][h].astype(BF)
+
+    @pl.when(pl.program_id(0) < 8)
+    def _():
+        write(theirs_ref)
+
+    @pl.when(pl.program_id(0) >= 8)
+    def _():
+        write(mine_ref)
+
+
+def restore_keys(tiles, grad_k, grad_v):
+    spec = lambda j: pl.BlockSpec((NH, BLK, HDIM), lambda i, o: (0, o[i * 4 + j], 0))
+    shape = (4 * BLK, 2 * PART)
+    return pl.pallas_call(
+        restore_kernel,
+        out_shape=[jax.ShapeDtypeStruct((32 * BLK, 2 * PART), BF)] * 2,
+        grid_spec=pltpu.PrefetchScalarGridSpec(
+            num_scalar_prefetch=1,
+            grid=(16,),
+            in_specs=[spec(j) for j in range(4)] * 2,
+            out_specs=[
+                pl.BlockSpec(shape, lambda i, o: (jnp.maximum(i - 8, 0), 0)),
+                pl.BlockSpec(shape, lambda i, o: (jnp.minimum(i, 7), 0)),
+            ],
+        ),
+        compiler_params=room(),
+        name="restore_keys",
+    )(tiles, *([grad_k] * 4), *([grad_v] * 4))
+
+
+def unproject_kernel(dq_ref, mine_ref, theirs_ref, w_ref, cos_ref, sin_ref, g_ref, x_ref, w_sc, y_sc):
+    thin = w_sc.shape[0] // 32
+
+    @pl.when(pl.program_id(0) == 0)
+    def _():
+        straighten(w_ref, w_sc, thin)
+
+    kv = mine_ref[...].astype(F32) + theirs_ref[...].astype(F32)
+    for h in range(NH):
+        y_sc[:, h * HDIM : (h + 1) * HDIM] = dq_ref[h]
+    y_sc[:, PART:] = kv[:, PART:]
+    cosine, sine_vals = cos_ref[...], -sin_ref[...]
+    for k in range(NH):
+        cols = slice(k * 128, (k + 1) * 128)
+        g_ref[:, cols] = swing(y_sc[:, cols], cosine, sine_vals).astype(BF)
+    g_ref[:, 2 * PART :] = kv[:, :PART].astype(BF)
+    x_ref[...] = mul(g_ref[...], w_sc[...], NT).astype(BF)
+
+
+def unproject(grad_q, mine, theirs, w_all, cosine, sine_vals):
+    rows = mine.shape[0]
+    full = w_all.shape
+    width = full[0] * full[1] * (full[2] - 8)
+    row = lambda n: pl.BlockSpec((QB, n), lambda i: (i, 0))
+    return pl.pallas_call(
+        unproject_kernel,
+        out_shape=[
+            jax.ShapeDtypeStruct((rows, 3 * PART), BF),
+            jax.ShapeDtypeStruct((rows, width), BF),
+        ],
+        grid=(rows // QB,),
+        in_specs=[
+            pl.BlockSpec((NH, QB, HDIM), lambda i: (0, i, 0)),
+            row(2 * PART),
+            row(2 * PART),
+            pl.BlockSpec(full, lambda i: (0, 0, 0, 0), pipeline_mode=pl.Buffered(1)),
+            row(128),
+            row(128),
+        ],
+        out_specs=[row(3 * PART), row(width)],
+        scratch_shapes=[
+            pltpu.VMEM((width, full[3]), BF),
+            pltpu.VMEM((QB, 2 * PART), F32),
+        ],
+        compiler_params=room(),
+        name="unproject",
+    )(grad_q, mine, theirs, w_all, cosine, sine_vals)
+
+
+def to_plane(rows):
+    blocks = rows.reshape(4, rows.shape[0] // 4, rows.shape[1])
+    blocks = lax.all_to_all(blocks, "p", 0, 0, tiled=True)
+    return lax.all_to_all(blocks, "z", 0, 0, tiled=True).reshape(rows.shape)
+
+
+def from_plane(rows):
+    blocks = rows.reshape(4, rows.shape[0] // 4, rows.shape[1])
+    blocks = lax.all_to_all(blocks, "z", 0, 0, tiled=True)
+    return lax.all_to_all(blocks, "p", 0, 0, tiled=True).reshape(rows.shape)
+
+
+def flip(values, mask):
+    return lax.ppermute(values, "p", [(k, k ^ mask) for k in range(4)])
+
+
+def gather_slots(own):
+    half = own.shape[0] // 2
+    first = flip(own, 1)
+    second = flip(own, 2)
+    upper = flip(second[:half], 1)
+    lower = flip(first[half:], 2)
+    return jnp.concatenate([own, first, second, upper, lower], axis=0)
+
+
+def scatter_slots(terms):
+    size = terms.shape[0] // 4
+    half = size // 2
+    low = lambda v: v.astype(BF)
+    upper = flip(low(terms[3 * size : 3 * size + half]), 1)
+    lower = flip(low(terms[3 * size + half :]), 2)
+    first = jnp.concatenate(
+        [
+            low(terms[size : size + half]),
+            low(terms[size + half : 2 * size].astype(F32) + lower.astype(F32)),
+        ],
+        axis=0,
+    )
+    second = jnp.concatenate(
+        [
+            low(terms[2 * size : 2 * size + half].astype(F32) + upper.astype(F32)),
+            low(terms[2 * size + half : 3 * size]),
+        ],
+        axis=0,
+    )
+    return terms[:size].astype(F32) + flip(first, 1).astype(F32) + flip(second, 2).astype(F32)
+
+
+def hidden_cuts(hidden):
+    steps = hidden // 8
+    sizes = [8 * (steps // 4 + (k < steps % 4)) for k in range(4)]
+    starts = [sum(sizes[:k]) for k in range(4)]
+    return starts, sizes, max(sizes)
+
+
+def inner(
+    tokens_in,
+    cotangent,
+    w_query,
+    w_key,
+    w_value,
+    w_output,
+    w_gate,
+    w_up,
+    w_down,
+    attn_gain,
+    ffn_gain,
+    cont_len,
+    deal_order,
+    clip_threshold,
+):
+    plane, depth, core = (lax.axis_index(name) for name in ("p", "z", "c"))
+    line = ("z", "c")
+    width = tokens_in.shape[1]
+    thin = w_query.shape[0]
+    hidden = w_down.shape[0]
+    starts, sizes, share = hidden_cuts(hidden)
+    gain_f = attn_gain.astype(F32)
+    moved = to_plane(tokens_in)
+    deal = lax.ppermute(deal_order[0], ("p", "z"), [(g * 4 + k, k * 4 + g) for g in range(4) for k in range(4)])
+    lengths = lax.ppermute(cont_len[0], ("p", "z"), [(g * 4 + k, k * 4 + g) for g in range(4) for k in range(4)])
+
+    scaled = [(w.astype(F32) * gain_f[:, None]).astype(BF) for w in (w_query, w_key, w_value)]
+    blocks = jnp.stack(scaled).reshape(3, thin, 4, PART).transpose(2, 1, 0, 3)
+    blocks = blocks.reshape(4, thin, 3 * PART)
+    extra = jnp.zeros((4, 8, 3 * PART), BF).at[:, 0, :thin].set(ffn_gain[None, :])
+    send = jnp.concatenate([blocks, extra], axis=1)
+    w_qkv = lax.all_gather(lax.all_to_all(send, "p", 0, 0, tiled=True), line, axis=0)
+    gain_two = w_qkv[:, :, thin, :thin].transpose(1, 0, 2).reshape(width).astype(F32)
+    w_out = lax.all_gather(w_output, line, axis=0, tiled=True)
+    stacked = jnp.stack([w_gate.T, w_up.T, w_down])
+    stacked = jnp.stack(
+        [
+            jnp.pad(stacked[:, a : a + n], ((0, 0), (0, share - n), (0, 0)))
+            for a, n in zip(starts, sizes)
+        ]
+    )
+    stacked = lax.all_to_all(stacked, "p", 0, 0, tiled=True)
+    stacked = stacked.transpose(1, 2, 0, 3).reshape(3, share, width)
+    w_ffn = [lax.all_gather(stacked[k], line, axis=0, tiled=True) for k in range(3)]
+
+    slot = jnp.arange(4)[:, None, None]
+    source = jnp.arange(4)[None, :, None]
+    pair = jnp.arange(2)[None, None, :]
+    quarter = jnp.bitwise_xor(plane, slot)
+    held = lambda which: deal[((source * 2 + which) * 8 + quarter * 2 + pair).reshape(-1)]
+    tiles, tiles_far = held(core), held(1 - core)
+    both = jnp.concatenate([tiles, tiles_far])
+    numbers = jnp.arange(64, dtype=jnp.int32)
+    order = jnp.sum(
+        jnp.where(both[None, :] == numbers[:, None], numbers[None, :], 0), axis=1
+    ).astype(jnp.int32)
+    logical = (tiles[:, None] * BLK + jnp.arange(BLK, dtype=jnp.int32)[None, :]).reshape(-1)
+    position = jnp.where(logical < PLEN, logical, PLEN + (logical - PLEN) % CLEN)
+    cosine, sine_vals = (v[:, 0, :] for v in rope_angles(position))
+    cosine = jnp.concatenate([cosine] * 4, axis=1)
+    sine_vals = jnp.concatenate([-sine_vals, sine_vals] * 2, axis=1)
+
+    residual = moved.astype(F32)
+    inverse_one = lax.rsqrt(jnp.mean(residual * residual, axis=-1, keepdims=True) + norm_eps)
+    normed = gather_slots((residual * inverse_one).astype(BF))
+    queries, mine = project(normed, w_qkv, cosine, sine_vals)
+    theirs = lax.ppermute(mine, "c", [(0, 1), (1, 0)])
+    keys, values = sort_keys(order, mine, theirs)
+    attended, log_total, peaks = attention_forward(tiles, lengths, queries, keys, values)
+    after_attn = residual + branch_scale * scatter_slots(mul(attended, w_out))
+    inverse_two = lax.rsqrt(jnp.mean(after_attn * after_attn, axis=-1, keepdims=True) + norm_eps)
+    normed_two = gather_slots((after_attn * inverse_two * gain_two).astype(BF))
+
+    grad_out = to_plane(cotangent).astype(F32)
+    grad_rows = gather_slots((branch_scale * grad_out).astype(BF))
+    gate_pre = mul(normed_two, w_ffn[0], NT)
+    up_pre = mul(normed_two, w_ffn[1], NT)
+    mixed = (jax.nn.silu(gate_pre) * up_pre).astype(BF)
+    grad_mixed = mul(grad_rows, w_ffn[2], NT)
+    grad_gate_low, grad_up_low = gate_grads(grad_mixed, gate_pre, up_pre)
+    grad_normed_two = scatter_slots(mul(grad_gate_low, w_ffn[0]) + mul(grad_up_low, w_ffn[1]))
+    branch_ffn = scatter_slots(mul(mixed, w_ffn[2]))
+    output = from_plane((after_attn + branch_scale * branch_ffn).astype(BF))
+    ffn_grads = jnp.stack(
+        [
+            lax.psum_scatter(mul(a, b, TN).astype(BF), line, scatter_dimension=0, tiled=True)
+            for a, b in (
+                (grad_gate_low, normed_two),
+                (grad_up_low, normed_two),
+                (mixed, grad_rows),
+            )
+        ]
+    )
+    ffn_grads = ffn_grads.reshape(3, share, 4, PART).transpose(2, 0, 1, 3)
+    ffn_grads = lax.all_to_all(ffn_grads, "p", 0, 0, tiled=True).astype(F32)
+    ffn_grads = jnp.concatenate([ffn_grads[k, :, :n] for k, n in enumerate(sizes)], axis=1)
+
+    grad_gain_two, grad_second = norm_backward(grad_normed_two, after_attn, inverse_two, gain_two)
+    grad_resid = grad_out + grad_second
+    grad_branch = gather_slots((branch_scale * grad_resid).astype(BF))
+    grad_w_output = mul(attended, grad_branch, TN).astype(BF)
+    grad_w_output = lax.psum_scatter(grad_w_output, line, scatter_dimension=0, tiled=True)
+    grad_heads, row_delta = attention_delta(grad_branch, w_out, attended)
+    grad_q, grad_k, grad_v = attention_backward(
+        tiles, lengths, queries, grad_heads, log_total, row_delta, keys, values
+    )
+    part_mine, part_far = restore_keys(jnp.concatenate([tiles_far, tiles]), grad_k, grad_v)
+    received = lax.ppermute(part_far, "c", [(0, 1), (1, 0)])
+    grad_qkv, scaled_one = unproject(grad_q, part_mine, received, w_qkv, cosine, sine_vals)
+    scaled_one = scatter_slots(scaled_one)
+    grad_first = inverse_one * scaled_one - residual * inverse_one**3 * jnp.mean(
+        scaled_one * residual, axis=-1, keepdims=True
+    )
+    grad_input = from_plane((grad_resid + grad_first).astype(BF)).astype(F32)
+    proj = mul(normed, grad_qkv, TN).astype(BF)
+    proj = proj.reshape(4, 8, thin, 3 * PART).transpose(1, 0, 2, 3)
+    gain_rows = grad_gain_two.astype(BF).reshape(4, 8, 1, thin).transpose(1, 0, 2, 3)
+    gain_rows = jnp.pad(gain_rows, ((0, 0), (0, 0), (0, 7), (0, 3 * PART - thin)))
+    proj = jnp.concatenate([proj, gain_rows], axis=2).reshape(8 * 4 * (thin + 8), 3 * PART)
+    proj = lax.psum_scatter(proj, line, scatter_dimension=0, tiled=True)
+    proj = proj.reshape(4, thin + 8, 3 * PART)
+    proj = lax.all_to_all(proj, "p", 0, 0, tiled=True).astype(F32)
+    grad_ffn_gain = jnp.sum(proj[:, thin, :thin], axis=0)
+    proj = proj[:, :thin].reshape(4, thin, 3, PART).transpose(2, 1, 0, 3).reshape(3, thin, width)
+    grad_attn_gain = sum(
+        jnp.sum(w.astype(F32) * proj[k], axis=1) for k, w in enumerate((w_query, w_key, w_value))
+    )
+    proj = proj * gain_f[None, :, None]
+
+    maxima = jnp.where(
+        jnp.arange(4)[:, None] == plane, jnp.max(peaks, axis=(0, 2))[None, :], masked_value
+    ).reshape(HEADS)
+    for name, mask, size in (("c", 1, 2), ("p", 1, 4), ("p", 2, 4), ("z", 1, 4), ("z", 2, 4)):
+        pairs = [(k, k ^ mask) for k in range(size)]
+        maxima = jnp.maximum(maxima, lax.ppermute(maxima, name, pairs))
+    limit_value = clip_threshold[0].astype(F32)
+    clip_factor = jnp.sqrt(limit_value / jnp.maximum(maxima, limit_value))
+    column_factor = jnp.repeat(clip_factor, HDIM)
+    return (
+        output,
+        grad_input,
+        proj[0],
+        proj[1],
+        proj[2],
+        grad_w_output.astype(F32),
+        ffn_grads[0].T,
+        ffn_grads[1].T,
+        ffn_grads[2],
+        grad_attn_gain,
+        grad_ffn_gain,
+        maxima,
+        clip_factor,
+        w_query.astype(F32) * column_factor[None, :],
+        w_key.astype(F32) * column_factor[None, :],
+    )
+
+
+def specs(grp, ctx):
+    every = grp + ctx
+    ins = [P(every, None)] * 6 + [P(grp, ctx), P(grp, ctx), P(ctx, grp), P(every), P(every)]
+    ins += [P(grp, None), P(grp, None), P()]
+    outs = [P(every, None)] * 6 + [P(grp, ctx), P(grp, ctx), P(ctx, grp), P(every), P(every)]
+    outs += [P(), P(), P(every, None), P(every, None)]
+    return tuple(ins), tuple(outs)
+
+
 def solution(mesh):
-    in_specs = (
-        P(("grp", "ctx"), None),
-        P(("grp", "ctx"), None),
-        P(("grp", "ctx"), None),
-        P(("grp", "ctx"), None),
-        P(("grp", "ctx"), None),
-        P(("grp", "ctx"), None),
-        P("grp", "ctx"),
-        P("grp", "ctx"),
-        P("ctx", "grp"),
-        P(("grp", "ctx")),
-        P(("grp", "ctx")),
-        P("grp", None),
-        P("grp", None),
-        P(),
-    )
-    out_specs = (
-        P(("grp", "ctx"), None),
-        P(("grp", "ctx"), None),
-        P(("grp", "ctx"), None),
-        P(("grp", "ctx"), None),
-        P(("grp", "ctx"), None),
-        P(("grp", "ctx"), None),
-        P("grp", "ctx"),
-        P("grp", "ctx"),
-        P("ctx", "grp"),
-        P(("grp", "ctx")),
-        P(("grp", "ctx")),
-        P(),
-        P(),
-        P(("grp", "ctx"), None),
-        P(("grp", "ctx"), None),
-    )
-    return jax.shard_map(local, mesh=mesh, in_specs=in_specs, out_specs=out_specs, check_vma=False)
+    if mesh.shape["grp"] == 4 and mesh.shape["ctx"] == 8:
+        mesh = Mesh(mesh.devices.reshape(4, 4, 2), ("p", "z", "c"))
+        body, (in_specs, out_specs) = inner, specs(("p",), ("z", "c"))
+    else:
+        body, (in_specs, out_specs) = local, specs(("grp",), ("ctx",))
+    return jax.shard_map(body, mesh=mesh, in_specs=in_specs, out_specs=out_specs, check_vma=False)

time: 4170 us -> 1760 us (0.42)
  waiting for transfers between devices: 2130 us -> 684 us
  matrix products: 1290 us -> 241 us
  Pallas kernels: 0 us -> 363 us
  local copies, waits for them, and re-layouts: 324 us -> 137 us
  other arithmetic: 244 us -> 103 us
  starting transfers between devices: 1.01 us -> 128 us
  blocking collectives: 128 us -> 82.8 us
    reduce_scatter x8 -> x5, waiting for transfers between devices: 1370 us -> 0.05 us  [the longest x3 0.04 us: inner(): lax.psum_scatter(mul(a, b, TN).astype(BF), line, scatter_dimension=0, til...]
    dot_general x77 -> x12, matrix products: 1290 us -> 241 us  [mul(): return lax.dot_general(left, right, dims, preferred_element_type=F32)]
    all_gather x11 -> x5, waiting for transfers between devices: 728 us -> 0.01 us  [the longest x3 0.01 us: inner(): lax.all_gather(stacked[k], line, axis=0, tiled=True)]
    ppermute x0 -> x41, waiting for transfers between devices: none -> 409 us  [the longest x32 378 us: flip(): return lax.ppermute(values, 'p', [(k, k ^ mask) for k in range(4)])]
    pallas_call x0 -> x7, Pallas kernels: none -> 363 us  [the longest x1 166 us: attention_backward(): pl.pallas_call(backward_kernel, out_shape=[jax.ShapeDtypeStruct((NH, rows...]
    all_to_all x0 -> x9, waiting for transfers between devices: none -> 275 us  [the longest x2 131 us: to_plane(): return lax.all_to_all(blocks, 'z', 0, 0, tiled=True).reshape(rows.shape)]
    reduce_max x8 -> x1, other arithmetic: 149 us -> 0.13 us  [inner(): jnp.max(peaks, axis=(0, 2))[None, :]]
    dynamic_update_slice x24 -> x0, local copies, waits for them, and re-layouts: 108 us -> none  [local(): lax.scan(back_step, jnp.zeros((row_count, HEADS, HDIM), jnp.float32), jnp...]
  transfers between devices with their start and end apart: 20 -> 60, of which waited for: 17 -> 28; matrix products, arithmetic and copies ran while one was open for 22% -> 22% of each run, Pallas kernels for 0% -> 21%
where the time goes in v1:
time: 1760 us; the launch traced here: 1750 us
  waiting for transfers between devices  684 us (39%)
  Pallas kernels  363 us (21%)
  matrix products  241 us (14%)
  local copies, waits for them, and re-layouts  137 us (8%)
  starting transfers between devices  128 us (7%)
  other arithmetic  103 us (6%)
  blocking collectives  82.8 us (5%)
    ppermute x32, waiting for transfers between devices, flip(): return lax.ppermute(values, 'p', [(k, k ^ mask) for k in range(4)])  378 us
    dot_general x12, matrix products, mul(): return lax.dot_general(left, right, dims, preferred_element_type=F32)  241 us
    pallas_call x1, Pallas kernels, attention_backward(): pl.pallas_call(backward_kernel, out_shape=[jax.ShapeDtypeStruct((NH, rows...  166 us
    all_to_all x2, waiting for transfers between devices, to_plane(): return lax.all_to_all(blocks, 'z', 0, 0, tiled=True).reshape(rows.shape)  131 us
    all_to_all x2, waiting for transfers between devices, from_plane(): blocks = lax.all_to_all(blocks, 'z', 0, 0, tiled=True)  100 us
    pallas_call x1, Pallas kernels, attention_forward(): pl.pallas_call(forward_kernel, out_shape=[jax.ShapeDtypeStruct((rows, PAR...  79.2 us
    unnamed x103, local copies, waits for them, and re-layouts  49.9 us
    ppermute x32, starting transfers between devices, flip(): return lax.ppermute(values, 'p', [(k, k ^ mask) for k in range(4)])  38.4 us
  transfers between devices with their start and end apart: 60, of which 28 were waited for; matrix products, arithmetic and copies ran while one was open for 22% of the time, Pallas kernels for 21%

profile of v1, /device:TPU:8, one launch (start us, length us, event | category | flops | bytes accessed | tf_op | source)
XLA Modules:
  0.0 1754.4 jit_solution(106073909513140092)
XLA Ops:
  42.2 34.7 %all_to_all.61 = bf16[4,3,184,576]{3,2,1,0:T(8,128)(2,1)S(1)} all-to-all(bf16[4,3,184,576]{3,2,1,0:T(8,128)(2,1)S(1)} %pad_maximum_fusion.1), channel_id=1, replica_groups=mesh['p'=4,'z'=4,'c'=2] {'p'}, dimensions={0} | all-to-all | bytes 5087232 | tf_op jit(solution)/shard_map/all_to_all | solution.py:958
  80.3 29.3 %all_to_all.62 = bf16[4,128,2304]{2,1,0:T(8,128)(2,1)} all-to-all(bf16[4,128,2304]{2,1,0:T(8,128)(2,1)S(1)} %bitcast.144), channel_id=1, replica_groups=mesh['p'=4,'z'=4,'c'=2] {'p'}, dimensions={0} | all-to-all | bytes 4718592 | tf_op jit(solution)/shard_map/all_to_all | solution.py:863
  117.6 72.5 %all-to-all-done.1 = bf16[4,128,2304]{2,1,0:T(8,128)(2,1)S(1)} async-done(((bf16[4,128,2304]{2,1,0:T(8,128)(2,1)}), bf16[4,128,2304]{2,1,0:T(8,128)(2,1)S(1)}, u32[]{:S(2)}, u32[]{:S(2)}) %all-to-all-start.1) | async-done | bytes 2359328 | tf_op jit(solution)/shard_map/all_to_all | solution.py:864
  202.8 44.6 %collective-permute-done.3 = bf16[512,2304]{1,0:T(8,128)(2,1)} collective-permute-done((bf16[512,2304]{1,0:T(8,128)(2,1)}, bf16[512,2304]{1,0:T(8,128)(2,1)}, u32[]{:S(2)}, u32[]{:S(2)}) %collective-permute-start.3) | collective-permute-done | bytes 2359328 | tf_op jit(solution)/shard_map/ppermute | solution.py:874
  285.4 24.5 %project.1 = (bf16[9,2048,64]{2,1,0:T(8,128)(2,1)}, bf16[2048,1152]{1,0:T(8,128)(2,1)}) custom-call(bf16[2048,2304]{1,0:T(8,128)(2,1)} %constant_dynamic-update-slice_fusion.x_ref, bf16[8,4,80,1728]{3,2,1,0:T(8,128)(2,1)} %bitcast.129, f32[2048,128]{1,0:T(8,128)} %pad_maximum_fusion.12.cos_ref, f32[2048,128]{1,0:T(8,128)} %pad_maximum_fusion.13.sin_ref), custom_call_target="tpu_custom_call" | custom-call | tf_op jit(solution)/shard_map/project/pallas_call | solution.py:454
  345.0 79.2 %attention_forward.1 = (bf16[2048,576]{1,0:T(8,128)(2,1)}, f32[8,9,256]{2,1,0:T(8,128)}, f32[8,9,256]{2,1,0:T(8,128)}) custom-call(s32[32]{0:T(128)} %copy-done.28, s32[8]{0:T(128)} %copy-done.32, bf16[9,2048,64]{2,1,0:T(8,128)(2,1)} %get-tuple-element.43.q_ref, bf16[9,4096,64]{2,1,0:T(8,128)(2,1)} %get-tuple-element.45.k_ref, ...), custom_call_target="tpu_custom_call" | custom-call | tf_op jit(solution)/shard_map/attention_forward/pallas_call | solution.py:631
  473.1 58.7 %all-to-all-done.7 = bf16[4,128,2304]{2,1,0:T(8,128)(2,1)} async-done(((bf16[4,128,2304]{2,1,0:T(8,128)(2,1)}), bf16[4,128,2304]{2,1,0:T(8,128)(2,1)}, u32[]{:S(2)}, u32[]{:S(2)}) %all-to-all-start.7) | async-done | bytes 2359328 | tf_op jit(solution)/shard_map/all_to_all | solution.py:864
  549.5 41.2 %collective-permute-done.20 = bf16[512,2304]{1,0:T(8,128)(2,1)} collective-permute-done((bf16[512,2304]{1,0:T(8,128)(2,1)}, bf16[512,2304]{1,0:T(8,128)(2,1)}, u32[]{:S(2)}, u32[]{:S(2)}) %collective-permute-start.20) | collective-permute-done | bytes 2359328 | tf_op jit(solution)/shard_map/ppermute | solution.py:874
  603.4 60.4 %collective-permute-done.21 = bf16[256,2304]{1,0:T(8,128)(2,1)S(1)} collective-permute-done((bf16[256,2304]{1,0:T(8,128)(2,1)S(1)}, bf16[256,2304]{1,0:T(8,128)(2,1)S(1)}, u32[]{:S(2)}, u32[]{:S(2)}) %collective-permute-start.21) | collective-permute-done | bytes 1179680 | tf_op jit(solution)/shard_map/ppermute | solution.py:874
  730.1 27.4 %multiply_convert_fusion = (bf16[2048,1472]{0,1:T(8,128)(2,1)}, bf16[2048,1472]{0,1:T(8,128)(2,1)}, bf16[2048,1472]{0,1:T(8,128)(2,1)S(1)}) fusion(f32[2048,1472]{0,1:T(8,128)} %fusion.59, f32[2048,1472]{0,1:T(8,128)} %fusion.60, bf16[2048,2304]{1,0:T(8,128)(2,1)} %constant_dynamic-update-slice_fusion.10, bf16[1472,2304]{1,0:T(8,128)(2,1)} %all-gather.13.cloned.1.call-done), kind=kOutput, calls=%fused_computation.5 | convolution fusion | flops 13939769344 | bytes 58425344 | tf_op jit(solution)/shard_map/dot_general | solution.py:406
  798.6 22.0 %fusion.61 = f32[2048,2304]{1,0:T(8,128)} fusion(bf16[2048,1472]{0,1:T(8,128)(2,1)} %get-tuple-element.130, bf16[1472,2304]{1,0:T(8,128)(2,1)} %all-gather.9.cloned.1.call-done), kind=kOutput, calls=%fused_computation.192 | convolution fusion | flops 13891534848 | bytes 31686656 | tf_op jit(solution)/shard_map/dot_general | solution.py:406
  820.6 24.3 %fusion.57 = (bf16[2048,2304]{1,0:T(8,128)(2,1)S(1)}, f32[2048,2304]{1,0:T(8,128)}) fusion(f32[2048,2304]{1,0:T(8,128)} %fusion.61, bf16[2048,1472]{0,1:T(8,128)(2,1)} %get-tuple-element.129, bf16[1472,2304]{1,0:T(8,128)(2,1)} %all-gather.11.cloned.1.call-done), kind=kOutput, calls=%fused_computation.188 | convolution fusion | flops 13900972032 | bytes 59998208 | tf_op jit(solution)/shard_map/dot_general | solution.py:406
  848.8 23.5 %fusion.58 = (bf16[2048,2304]{1,0:T(8,128)(2,1)}, f32[2048,2304]{1,0:T(8,128)}) fusion(bf16[2048,1472]{0,1:T(8,128)(2,1)} %copy-done.37, bf16[1472,2304]{1,0:T(8,128)(2,1)} %all-gather.13.cloned.1.call-done), kind=kOutput, calls=%fused_computation.189 | convolution fusion | flops 13896253440 | bytes 41123840 | tf_op jit(solution)/shard_map/dot_general | solution.py:406
  931.0 43.2 %collective-permute-done.26 = bf16[512,2304]{1,0:T(8,128)(2,1)S(1)} collective-permute-done((bf16[512,2304]{1,0:T(8,128)(2,1)S(1)}, bf16[512,2304]{1,0:T(8,128)(2,1)S(1)}, u32[]{:S(2)}, u32[]{:S(2)}) %collective-permute-start.26) | collective-permute-done | bytes 2359328 | tf_op jit(solution)/shard_map/ppermute | solution.py:874
  978.3 38.2 %collective-permute-done.18 = bf16[512,2304]{1,0:T(8,128)(2,1)S(1)} collective-permute-done((bf16[512,2304]{1,0:T(8,128)(2,1)S(1)}, bf16[512,2304]{1,0:T(8,128)(2,1)S(1)}, u32[]{:S(2)}, u32[]{:S(2)}) %collective-permute-start.18) | collective-permute-done | bytes 2359328 | tf_op jit(solution)/shard_map/ppermute | solution.py:874
  1030.9 47.7 %collective-permute-done.28 = bf16[512,2304]{1,0:T(8,128)(2,1)S(1)} collective-permute-done((bf16[512,2304]{1,0:T(8,128)(2,1)S(1)}, bf16[512,2304]{1,0:T(8,128)(2,1)S(1)}, u32[]{:S(2)}, u32[]{:S(2)}) %collective-permute-start.28) | collective-permute-done | bytes 2359328 | tf_op jit(solution)/shard_map/ppermute | solution.py:874
  1123.2 165.5 %attention_backward.1 = (f32[9,2048,64]{2,1,0:T(8,128)}, f32[9,4096,64]{2,1,0:T(8,128)}, f32[9,4096,64]{2,1,0:T(8,128)}) custom-call(s32[32]{0:T(128)} %copy-done.28, s32[8]{0:T(128)} %copy-done.32, bf16[9,2048,64]{2,1,0:T(8,128)(2,1)} %get-tuple-element.43.q_ref, bf16[9,2048,64]{2,1,0:T(8,128)(2,1)} %get-tuple-element.48.g_ref, ...), custom_call_target="tpu_custom_call" | custom-call | tf_op jit(solution)/shard_map/attention_backward/pallas_call | solution.py:753
  1320.8 30.5 %unproject.1 = (bf16[2048,1728]{1,0:T(8,128)(2,1)}, bf16[2048,2304]{1,0:T(8,128)(2,1)}) custom-call(f32[9,2048,64]{2,1,0:T(8,128)} %get-tuple-element.51.dq_ref, bf16[2048,1152]{1,0:T(8,128)(2,1)} %get-tuple-element.54.mine_ref, bf16[2048,1152]{1,0:T(8,128)(2,1)} %collective-permute-done.31.theirs_ref, bf16[8,4,80,1728]{3,2,1,0:T(8,128)(2,1)} %bitcast.131, ...), custom_call_target="tpu_custom_call" | custom-call | tf_op jit(solution)/shard_map/unproject/pallas_call | solution.py:836
  1351.3 23.0 %convolution_convert_fusion = bf16[2304,1728]{0,1:T(8,128)(2,1)} fusion(bf16[2048,2304]{1,0:T(8,128)(2,1)} %constant_dynamic-update-slice_fusion.x_ref, bf16[2048,1728]{1,0:T(8,128)(2,1)} %get-tuple-element.57), kind=kOutput, calls=%fused_computation.9 | convolution fusion | flops 16311435264 | bytes 24477696 | tf_op jit(solution)/shard_map/dot_general | solution.py:406
  1401.6 23.4 %all-to-all-start.4 = ((bf16[4,128,2304]{2,1,0:T(8,128)(2,1)}), bf16[4,128,2304]{2,1,0:T(8,128)(2,1)}, u32[]{:S(2)}, u32[]{:S(2)}) async-start(bf16[4,128,2304]{2,1,0:T(8,128)(2,1)} %bitcast.24), calls=%async_computation.4 | async-start | bytes 4718592 | tf_op jit(solution)/shard_map/all_to_all | solution.py:869
  1430.0 25.8 %collective-permute-done.34 = bf16[256,2304]{1,0:T(8,128)(2,1)S(1)} collective-permute-done((bf16[256,2304]{1,0:T(8,128)(2,1)S(1)}, bf16[256,2304]{1,0:T(8,128)(2,1)S(1)}, u32[]{:S(2)}, u32[]{:S(2)}) %collective-permute-start.34) | collective-permute-done | bytes 1179680 | tf_op jit(solution)/shard_map/ppermute | solution.py:874
  1464.3 50.2 %all-to-all-done.4 = bf16[4,128,2304]{2,1,0:T(8,128)(2,1)} async-done(((bf16[4,128,2304]{2,1,0:T(8,128)(2,1)}), bf16[4,128,2304]{2,1,0:T(8,128)(2,1)}, u32[]{:S(2)}, u32[]{:S(2)}) %all-to-all-start.4) | async-done | bytes 2359328 | tf_op jit(solution)/shard_map/all_to_all | solution.py:869
  1591.7 49.8 %all-to-all-done.8 = bf16[4,128,2304]{2,1,0:T(8,128)(2,1)} async-done(((bf16[4,128,2304]{2,1,0:T(8,128)(2,1)}), bf16[4,128,2304]{2,1,0:T(8,128)(2,1)}, u32[]{:S(2)}, u32[]{:S(2)}) %all-to-all-start.8) | async-done | bytes 2359328 | tf_op jit(solution)/shard_map/all_to_all | solution.py:869
  1648.7 22.9 %collective-permute-done.37 = f32[36]{0:T(128)S(1)} collective-permute-done((f32[36]{0:T(128)S(1)}, f32[36]{0:T(128)S(1)}, u32[]{:S(2)}, u32[]{:S(2)}) %collective-permute-start.37) | collective-permute-done | bytes 176 | tf_op jit(solution)/shard_map/ppermute | solution.py:1051
  (372 shorter events, 675.8 us)
Async XLA Ops:
  7.2 278.2 %all-gather.15.cloned.1.call-start = ((), (), s32[]{:S(2)}) async-start(), calls=%async_computation.26 | async-start | bytes 10321920 | tf_op jit(solution)/shard_map/all_gather | solution.py:948
  35.1 389.1 %all-gather.7.cloned.1.call-start = ((), (), s32[]{:S(2)}) async-start(), calls=%async_computation.17 | async-start | bytes 2985984 | tf_op jit(solution)/shard_map/all_gather | solution.py:950
  35.9 653.5 %all-gather.11.cloned.1.call-start = ((), (), s32[]{:S(2)}) async-start(), calls=%async_computation.19 | async-start | bytes 7630848 | tf_op jit(solution)/shard_map/all_gather | solution.py:960
  109.6 80.5 %all-to-all-start.1 = ((bf16[4,128,2304]{2,1,0:T(8,128)(2,1)}), bf16[4,128,2304]{2,1,0:T(8,128)(2,1)S(1)}, u32[]{:S(2)}, u32[]{:S(2)}) async-start(bf16[4,128,2304]{2,1,0:T(8,128)(2,1)} %all_to_all.62), calls=%async_computation.1 | async-start | bytes 4718592 | tf_op jit(solution)/shard_map/all_to_all | solution.py:864
  114.9 594.9 %all-gather.9.cloned.1.call-start = ((), (), s32[]{:S(2)}) async-start(), calls=%async_computation.18 | async-start | bytes 7630848 | tf_op jit(solution)/shard_map/all_gather | solution.py:960
  114.9 83.3 %collective-permute-start = (s32[64]{0:T(128)S(1)}, s32[64]{0:T(128)S(1)}, u32[]{:S(2)}, u32[]{:S(2)}) collective-permute-start(s32[64]{0:T(128)S(1)} %bitcast.150), channel_id=1, source_target_pairs={{0,0},{2,8},{4,16},{6,24},{8,2},{10,10},{12,18},{14,26},{16,4},{18... | collective-permute-start | bytes 776 | tf_op jit(solution)/shard_map/ppermute | solution.py:940
  309.9 130.7 %all-to-all-start.6 = ((bf16[4,128,2304]{2,1,0:T(8,128)(2,1)}), bf16[4,128,2304]{2,1,0:T(8,128)(2,1)}, u32[]{:S(2)}, u32[]{:S(2)}) async-start(bf16[4,128,2304]{2,1,0:T(8,128)(2,1)} %bitcast.145), calls=%async_computation.6 | async-start | bytes 4718592 | tf_op jit(solution)/shard_map/all_to_all | solution.py:863
  440.6 91.3 %all-to-all-start.7 = ((bf16[4,128,2304]{2,1,0:T(8,128)(2,1)}), bf16[4,128,2304]{2,1,0:T(8,128)(2,1)}, u32[]{:S(2)}, u32[]{:S(2)}) async-start(bf16[4,128,2304]{2,1,0:T(8,128)(2,1)} %all-to-all-done.6), calls=%async_computation.7 | async-start | bytes 4718592 | tf_op jit(solution)/shard_map/all_to_all | solution.py:864
  452.2 278.0 %all-gather.13.cloned.1.call-start = ((), (), s32[]{:S(2)}) async-start(), calls=%async_computation.20 | async-start | bytes 7630848 | tf_op jit(solution)/shard_map/all_gather | solution.py:960
  467.2 73.3 %collective-permute-start.10 = (bf16[512,2304]{1,0:T(8,128)(2,1)}, bf16[512,2304]{1,0:T(8,128)(2,1)}, u32[]{:S(2)}, u32[]{:S(2)}) collective-permute-start(bf16[512,2304]{1,0:T(8,128)(2,1)} %pad_maximum_fusion.4), channel_id=1, source_target_pairs={{0,16},{8,24},{16,0},{24,8},{1,17},{9,25},{17,1},{25,9},{2,18},{10... | collective-permute-start | bytes 7077896 | tf_op jit(solution)/shard_map/ppermute | solution.py:874
  473.1 1046.1 %reduce-scatter.14.cloned.1.call-start = ((), (), s32[]{:S(2)}) async-start(), calls=%async_computation.25 | async-start | bytes 7630848 | tf_op jit(solution)/shard_map/reduce_scatter | solution.py:1002
  548.8 116.1 %collective-permute-start.12 = (bf16[512,2304]{1,0:T(8,128)(2,1)S(1)}, bf16[512,2304]{1,0:T(8,128)(2,1)S(1)}, u32[]{:S(2)}, u32[]{:S(2)}) collective-permute-start(bf16[512,2304]{1,0:T(8,128)(2,1)S(1)} %get-tuple-element.126), channel_id=1, source_target_pairs={{0,16},{8,24},{16,0},{24,8},{1,17},{9,25},{17,1},{25,9},{2,18},{10... | collective-permute-start | bytes 7077896 | tf_op jit(solution)/shard_map/ppermute | solution.py:874
  548.9 119.3 %collective-permute-start.11 = (bf16[512,2304]{1,0:T(8,128)(2,1)S(1)}, bf16[512,2304]{1,0:T(8,128)(2,1)S(1)}, u32[]{:S(2)}, u32[]{:S(2)}) collective-permute-start(bf16[512,2304]{1,0:T(8,128)(2,1)S(1)} %get-tuple-element.126), channel_id=1, source_target_pairs={{0,8},{8,0},{16,24},{24,16},{1,9},{9,1},{17,25},{25,17},{2,10},{10... | collective-permute-start | bytes 7077896 | tf_op jit(solution)/shard_map/ppermute | solution.py:874
  778.6 743.3 %reduce-scatter.12.cloned.1.call-start = ((), (), s32[]{:S(2)}) async-start(), calls=%async_computation.24 | async-start | bytes 7630848 | tf_op jit(solution)/shard_map/reduce_scatter | solution.py:1002
  798.5 727.0 %reduce-scatter.10.cloned.1.call-start = ((), (), s32[]{:S(2)}) async-start(), calls=%async_computation.23 | async-start | bytes 7630848 | tf_op jit(solution)/shard_map/reduce_scatter | solution.py:1002
  896.1 790.1 %reduce-scatter.8.cloned.1.call-start = ((), (), s32[]{:S(2)}) async-start(), calls=%async_computation.22 | async-start | bytes 2985984 | tf_op jit(solution)/shard_map/reduce_scatter | solution.py:1018
  900.4 73.8 %collective-permute-start.26 = (bf16[512,2304]{1,0:T(8,128)(2,1)S(1)}, bf16[512,2304]{1,0:T(8,128)(2,1)S(1)}, u32[]{:S(2)}, u32[]{:S(2)}) collective-permute-start(bf16[512,2304]{1,0:T(8,128)(2,1)S(1)} %pad_maximum_fusion.8), channel_id=1, source_target_pairs={{0,16},{8,24},{16,0},{24,8},{1,17},{9,25},{17,1},{25,9},{2,18},{10... | collective-permute-start | bytes 7077896 | tf_op jit(solution)/shard_map/ppermute | solution.py:874
  901.1 73.1 %collective-permute-start.24 = (bf16[512,2304]{1,0:T(8,128)(2,1)S(1)}, bf16[512,2304]{1,0:T(8,128)(2,1)S(1)}, u32[]{:S(2)}, u32[]{:S(2)}) collective-permute-start(bf16[512,2304]{1,0:T(8,128)(2,1)S(1)} %pad_maximum_fusion.7), channel_id=1, source_target_pairs={{0,8},{8,0},{16,24},{24,16},{1,9},{9,1},{17,25},{25,17},{2,10},{10... | collective-permute-start | bytes 7077896 | tf_op jit(solution)/shard_map/ppermute | solution.py:874
  927.6 88.9 %collective-permute-start.18 = (bf16[512,2304]{1,0:T(8,128)(2,1)S(1)}, bf16[512,2304]{1,0:T(8,128)(2,1)S(1)}, u32[]{:S(2)}, u32[]{:S(2)}) collective-permute-start(bf16[512,2304]{1,0:T(8,128)(2,1)S(1)} %pad_maximum_fusion.6), channel_id=1, source_target_pairs={{0,16},{8,24},{16,0},{24,8},{1,17},{9,25},{17,1},{25,9},{2,18},{10... | collective-permute-start | bytes 7077896 | tf_op jit(solution)/shard_map/ppermute | solution.py:874
  929.4 87.1 %collective-permute-start.16 = (bf16[512,2304]{1,0:T(8,128)(2,1)S(1)}, bf16[512,2304]{1,0:T(8,128)(2,1)S(1)}, u32[]{:S(2)}, u32[]{:S(2)}) collective-permute-start(bf16[512,2304]{1,0:T(8,128)(2,1)S(1)} %pad_maximum_fusion.5), channel_id=1, source_target_pairs={{0,8},{8,0},{16,24},{24,16},{1,9},{9,1},{17,25},{25,17},{2,10},{10... | collective-permute-start | bytes 7077896 | tf_op jit(solution)/shard_map/ppermute | solution.py:874
  1320.7 381.1 %reduce-scatter.6.cloned.1.call-start = ((), (), s32[]{:S(2)}) async-start(), calls=%async_computation.21 | async-start | bytes 10321920 | tf_op jit(solution)/shard_map/reduce_scatter | solution.py:1036
  1401.6 113.0 %all-to-all-start.4 = ((bf16[4,128,2304]{2,1,0:T(8,128)(2,1)}), bf16[4,128,2304]{2,1,0:T(8,128)(2,1)}, u32[]{:S(2)}, u32[]{:S(2)}) async-start(bf16[4,128,2304]{2,1,0:T(8,128)(2,1)} %bitcast.24), calls=%async_computation.4 | async-start | bytes 4718592 | tf_op jit(solution)/shard_map/all_to_all | solution.py:869
  1461.0 90.0 %collective-permute-start.35 = (bf16[512,2304]{1,0:T(8,128)(2,1)}, bf16[512,2304]{1,0:T(8,128)(2,1)}, u32[]{:S(2)}, u32[]{:S(2)}) collective-permute-start(bf16[512,2304]{1,0:T(8,128)(2,1)} %pad_maximum_fusion.10), channel_id=1, source_target_pairs={{0,16},{8,24},{16,0},{24,8},{1,17},{9,25},{17,1},{25,9},{2,18},{10... | collective-permute-start | bytes 7077896 | tf_op jit(solution)/shard_map/ppermute | solution.py:874
  1463.1 87.9 %collective-permute-start.33 = (bf16[512,2304]{1,0:T(8,128)(2,1)}, bf16[512,2304]{1,0:T(8,128)(2,1)}, u32[]{:S(2)}, u32[]{:S(2)}) collective-permute-start(bf16[512,2304]{1,0:T(8,128)(2,1)} %pad_maximum_fusion.9), channel_id=1, source_target_pairs={{0,8},{8,0},{16,24},{24,16},{1,9},{9,1},{17,25},{25,17},{2,10},{10... | collective-permute-start | bytes 7077896 | tf_op jit(solution)/shard_map/ppermute | solution.py:874
  (78 other events, 2359.8 us)
Sparse Core Ops, SparseCore 0:
  35.2 90.9 all-gather.14
  127.9 61.4 all-gather.6
  191.1 68.8 all-gather.10
  261.5 67.4 all-gather.8
  473.2 84.4 all-gather.12
  778.7 74.6 reduce-scatter.13
  855.7 73.0 reduce-scatter.11
  931.1 73.0 reduce-scatter.9
  1320.8 49.4 reduce-scatter.7
  1401.7 157.1 reduce-scatter.5

commit v2 on v1

--- a/solution.py
+++ b/solution.py
@@ -21,6 +21,8 @@
 BF = jnp.bfloat16
 NH = HEADS // 4
 PART = NH * HDIM
+GROUP = 3
+GPART = GROUP * HDIM
 QB = 256
 KB = 1024
 KB_FWD = 512
@@ -410,6 +412,10 @@
     return pltpu.CompilerParams(vmem_limit_bytes=VMEM_ROOM)
 
 
+def cost(flops, sent):
+    return pl.CostEstimate(flops=int(flops), bytes_accessed=int(sent), transcendentals=0)
+
+
 def straighten(w_ref, w_sc, thin):
     for i in range(4):
         for k in range(8):
@@ -426,14 +432,39 @@
     return values * cosine + other * sine_vals
 
 
-def project_kernel(x_ref, w_ref, cos_ref, sin_ref, q_ref, kv_ref, w_sc):
+def fetch_rows(pieces, x_sc):
+    step = pl.program_id(0)
+    half = QB // 2
+    for k in range(8):
+        chunk, slot = k // 4, k % 4
+
+        @pl.when(step == k)
+        def _():
+            if len(pieces) == 5 and slot < 3:
+                x_sc[...] = pieces[slot][chunk * QB : (chunk + 1) * QB, :]
+            elif len(pieces) == 5:
+                x_sc[...] = pieces[3 + chunk][...]
+            elif slot < 3:
+                x_sc[...] = pieces[chunk * 5 + slot][...]
+            else:
+                x_sc[:half] = pieces[chunk * 5 + 3][...]
+                x_sc[half:] = pieces[chunk * 5 + 4][...]
+
+
+def whole(shape):
+    return pl.BlockSpec(shape, lambda i: (0,) * len(shape), pipeline_mode=pl.Buffered(1))
+
+
+def project_kernel(*refs):
+    w_ref, cos_ref, sin_ref, q_ref, kv_ref, w_sc, x_sc = refs[5:]
     thin = w_sc.shape[0] // 32
+    fetch_rows(refs[:5], x_sc)
 
     @pl.when(pl.program_id(0) == 0)
     def _():
         straighten(w_ref, w_sc, thin)
 
-    y = mul(x_ref[...], w_sc[...])
+    y = mul(x_sc[...], w_sc[...])
     cosine, sine_vals = cos_ref[...], sin_ref[...]
     for k in range(NH):
         piece = swing(y[:, k * 128 : (k + 1) * 128], cosine, sine_vals)
@@ -449,7 +480,8 @@
 
 
 def project(normed, w_all, cosine, sine_vals):
-    rows, width = normed.shape
+    rows = sum(v.shape[0] for v in normed)
+    width = normed[0].shape[1]
     full = w_all.shape
     return pl.pallas_call(
         project_kernel,
@@ -458,9 +490,9 @@
             jax.ShapeDtypeStruct((rows, 2 * PART), BF),
         ],
         grid=(rows // QB,),
-        in_specs=[
-            pl.BlockSpec((QB, width), lambda i: (i, 0)),
-            pl.BlockSpec(full, lambda i: (0, 0, 0, 0), pipeline_mode=pl.Buffered(1)),
+        in_specs=[whole(v.shape) for v in normed]
+        + [
+            whole(full),
             pl.BlockSpec((QB, 128), lambda i: (i, 0)),
             pl.BlockSpec((QB, 128), lambda i: (i, 0)),
         ],
@@ -468,14 +500,15 @@
             pl.BlockSpec((NH, QB, HDIM), lambda i: (0, i, 0)),
             pl.BlockSpec((QB, 2 * PART), lambda i: (i, 0)),
         ],
-        scratch_shapes=[pltpu.VMEM((width, full[3]), BF)],
+        scratch_shapes=[pltpu.VMEM((width, full[3]), BF), pltpu.VMEM((QB, width), BF)],
         compiler_params=room(),
+        cost_estimate=cost(2 * rows * width * full[3], 2 * (rows * width + width * full[3] + rows * 5 * PART)),
         name="project",
-    )(normed, w_all, cosine, sine_vals)
+    )(*normed, w_all, cosine, sine_vals)
 
 
 def sort_kernel(order_ref, *refs):
-    k_ref, v_ref = refs[8:]
+    k_ref, v_ref, kt_ref, vt_ref = refs[8:]
     first = pl.program_id(0) * 4
     for j in range(4):
         from_mine = order_ref[first + j] < 32
@@ -484,6 +517,9 @@
         for h in range(NH):
             v_ref[h, rows, :] = tile[:, h * HDIM : (h + 1) * HDIM]
             k_ref[h, rows, :] = tile[:, PART + h * HDIM : PART + (h + 1) * HDIM]
+    for h in range(NH):
+        kt_ref[h] = k_ref[h].T
+        vt_ref[h] = v_ref[h].T
 
 
 def sort_keys(order, mine, theirs):
@@ -493,14 +529,17 @@
     far = lambda j: pl.BlockSpec(shape, lambda i, o: (jnp.maximum(o[i * 4 + j] - 32, 0), 0, 0))
     return pl.pallas_call(
         sort_kernel,
-        out_shape=[jax.ShapeDtypeStruct((NH, count * BLK, HDIM), BF)] * 2,
+        out_shape=[jax.ShapeDtypeStruct((NH, count * BLK, HDIM), BF)] * 2
+        + [jax.ShapeDtypeStruct((NH, HDIM, count * BLK), BF)] * 2,
         grid_spec=pltpu.PrefetchScalarGridSpec(
             num_scalar_prefetch=1,
             grid=(count // 4,),
             in_specs=[near(j) for j in range(4)] + [far(j) for j in range(4)],
-            out_specs=[pl.BlockSpec((NH, 4 * BLK, HDIM), lambda i, o: (0, i, 0))] * 2,
+            out_specs=[pl.BlockSpec((NH, 4 * BLK, HDIM), lambda i, o: (0, i, 0))] * 2
+            + [pl.BlockSpec((NH, HDIM, 4 * BLK), lambda i, o: (0, 0, i))] * 2,
         ),
         compiler_params=room(),
+        cost_estimate=cost(0, 64 * count * BLK * PART),
         name="sort_keys",
     )(order, *([mine.reshape(32, BLK, 2 * PART)] * 4), *([theirs.reshape(32, BLK, 2 * PART)] * 4))
 
@@ -534,18 +573,9 @@
 
 
 def forward_kernel(
-    tiles_ref, len_ref, q_ref, k_ref, v_ref, o_ref, lse_ref, mx_ref, vt_sc, ot_sc
+    tiles_ref, len_ref, q_ref, k_ref, vt_sc, o_ref, lse_ref, mx_ref, ot_sc, shift
 ):
-    block = pl.program_id(0)
-
-    @pl.when(block == 0)
-    def _():
-        def flip_head(h, carry):
-            vt_sc[h] = v_ref[h].T
-            return carry
-
-        lax.fori_loop(0, NH, flip_head, 0)
-
+    block = pl.program_id(0) + shift
     qpos, is_cont, n_all, n_free, starts, seen = block_facts(tiles_ref, len_ref, block, KB_FWD)
 
     def heads(group, carry):
@@ -622,14 +652,15 @@
         o_ref[:, h * HDIM : (h + 1) * HDIM] = ot_sc[h].T.astype(BF)
 
 
-def attention_forward(tiles, lengths, queries, keys, values):
-    rows = queries.shape[1]
-    count = rows // QB
+def attention_forward(tiles, lengths, queries, keys, values_t, shift, count):
+    rows = count * QB
     span = keys.shape[1]
-    whole = pl.BlockSpec((NH, span, HDIM), lambda i, a, b: (0, 0, 0), pipeline_mode=pl.Buffered(1))
+    once = lambda *shape: pl.BlockSpec(
+        shape, lambda i, a, b: (0, 0, 0), pipeline_mode=pl.Buffered(1)
+    )
     stat = pl.BlockSpec((1, NH, QB), lambda i, a, b: (i, 0, 0))
     return pl.pallas_call(
-        forward_kernel,
+        functools.partial(forward_kernel, shift=shift),
         out_shape=[
             jax.ShapeDtypeStruct((rows, PART), BF),
             jax.ShapeDtypeStruct((count, NH, QB), F32),
@@ -638,33 +669,38 @@
         grid_spec=pltpu.PrefetchScalarGridSpec(
             num_scalar_prefetch=2,
             grid=(count,),
-            in_specs=[pl.BlockSpec((NH, QB, HDIM), lambda i, a, b: (0, i, 0)), whole, whole],
+            in_specs=[
+                pl.BlockSpec((NH, QB, HDIM), lambda i, a, b: (0, i + shift, 0)),
+                once(NH, span, HDIM),
+                once(NH, HDIM, span),
+            ],
             out_specs=[pl.BlockSpec((QB, PART), lambda i, a, b: (i, 0)), stat, stat],
-            scratch_shapes=[
-                pltpu.VMEM((NH, HDIM, span), BF),
-                pltpu.VMEM((NH, HDIM, QB), F32),
-            ],
+            scratch_shapes=[pltpu.VMEM((NH, HDIM, QB), F32)],
         ),
         compiler_params=room(),
+        cost_estimate=cost(rows * PART * PLEN * 20, 16 * span * PART),
         name="attention_forward",
-    )(tiles, lengths, queries, keys, values)
-
-
-def delta_kernel(g_ref, w_ref, o_ref, gh_ref, delta_ref):
-    grad = mul(g_ref[...], w_ref[...], NT).astype(BF)
-    ones = jnp.ones((8, HDIM), F32)
+    )(tiles, lengths, queries, keys, values_t)
+
+
+def delta_kernel(*refs):
+    w_ref, o_ref, gh_ref, delta_ref, x_sc = refs[10:]
+    fetch_rows(refs[:10], x_sc)
+    grad = mul(x_sc[...], w_ref[...], NT).astype(BF)
     for h in range(NH):
-        cols = slice(h * HDIM, (h + 1) * HDIM)
-        gh_ref[h] = grad[:, cols]
-        prod = grad[:, cols].astype(F32) * o_ref[:, cols].astype(F32)
-        total = lax.dot_general(
-            ones, prod, NT, preferred_element_type=F32, precision=lax.Precision.HIGHEST
-        )
-        delta_ref[0, h : h + 1, :] = total[0:1]
+        gh_ref[h] = grad[:, h * HDIM : (h + 1) * HDIM]
+    prod = grad.astype(F32) * o_ref[...].astype(F32)
+    row = lax.broadcasted_iota(jnp.int32, (16, PART), 0)
+    col = lax.broadcasted_iota(jnp.int32, (16, PART), 1)
+    pick = jnp.where(col // HDIM == row, 1.0, 0.0)
+    total = lax.dot_general(
+        pick, prod, NT, preferred_element_type=F32, precision=lax.Precision.HIGHEST
+    )
+    delta_ref[0] = total[:NH]
 
 
 def attention_delta(grad_branch, w_out, attended):
-    rows, width = grad_branch.shape
+    rows, width = attended.shape[0], w_out.shape[1]
     count = rows // QB
     return pl.pallas_call(
         delta_kernel,
@@ -673,31 +709,30 @@
             jax.ShapeDtypeStruct((count, NH, QB), F32),
         ],
         grid=(count,),
-        in_specs=[
-            pl.BlockSpec((QB, width), lambda i: (i, 0)),
-            pl.BlockSpec((PART, width), lambda i: (0, 0), pipeline_mode=pl.Buffered(1)),
-            pl.BlockSpec((QB, PART), lambda i: (i, 0)),
-        ],
+        in_specs=[whole(v.shape) for v in grad_branch]
+        + [whole((PART, width)), pl.BlockSpec((QB, PART), lambda i: (i, 0))],
         out_specs=[
             pl.BlockSpec((NH, QB, HDIM), lambda i: (0, i, 0)),
             pl.BlockSpec((1, NH, QB), lambda i: (i, 0, 0)),
         ],
+        scratch_shapes=[pltpu.VMEM((QB, width), BF)],
         compiler_params=room(),
+        cost_estimate=cost(2 * rows * width * PART, 2 * rows * width),
         name="attention_delta",
-    )(grad_branch, w_out, attended)
+    )(*grad_branch, w_out, attended)
 
 
 def backward_kernel(
-    tiles_ref, len_ref, q_ref, g_ref, lse_ref, delta_ref, k_ref, v_ref, dq_ref, dk_ref, dv_ref, kt_sc
+    tiles_ref, len_ref, q_ref, g_ref, lse_ref, delta_ref, k_ref, v_ref, kt_ref, dq_ref, dk_out, dv_out,
+    dk_ref, dv_ref, first
 ):
-    h = pl.program_id(0)
+    h = pl.program_id(0) + first
     block = pl.program_id(1)
 
     @pl.when(block == 0)
     def _():
         dk_ref[...] = jnp.zeros_like(dk_ref)
         dv_ref[...] = jnp.zeros_like(dv_ref)
-        kt_sc[...] = k_ref[0].T
 
     qpos, is_cont, n_all, n_free, starts, seen = block_facts(tiles_ref, len_ref, block, KB)
     q = q_ref[0]
@@ -715,9 +750,9 @@
             s = jnp.where(kpos <= qpos, s, masked_value)
         p = jnp.exp(s - lse)
         ds = (p * (dp - delta)).astype(BF)
-        dv_ref[0, rows, :] += mul(p.astype(BF), g)
-        dk_ref[0, rows, :] += mul(ds, q)
-        return dqt + mul(kt_sc[:, rows], ds)
+        dv_ref[rows, :] += mul(p.astype(BF), g)
+        dk_ref[rows, :] += mul(ds, q)
+        return dqt + mul(kt_ref[0, :, rows], ds)
 
     dqt = jnp.zeros((HDIM, QB), F32)
     dqt = lax.fori_loop(0, n_free, functools.partial(step, masked=False), dqt)
@@ -737,36 +772,52 @@
         dq = []
         for j in range(4):
             cols = slice(j * BLK, (j + 1) * BLK)
-            dv_ref[0, rows[j], :] += mul(pb[:, cols], part(g, j))
-            dk_ref[0, rows[j], :] += mul(ds[:, cols], part(q, j))
-            dq.append(mul(kt_sc[:, rows[j]], ds[:, cols]))
+            dv_ref[rows[j], :] += mul(pb[:, cols], part(g, j))
+            dk_ref[rows[j], :] += mul(ds[:, cols], part(q, j))
+            dq.append(mul(kt_ref[0, :, rows[j]], ds[:, cols]))
         dq_ref[0] += jnp.concatenate(dq, axis=1).T * HDIM ** (-0.5)
 
-
-def attention_backward(tiles, lengths, queries, grads, log_total, row_delta, keys, values):
+    @pl.when(block == pl.num_programs(1) - 1)
+    def _():
+        dk_out[0] = dk_ref[...].astype(BF)
+        dv_out[0] = dv_ref[...].astype(BF)
+
+
+def attention_backward(tiles, lengths, queries, grads, log_total, row_delta, keys, values, keys_t, group):
     rows = queries.shape[1]
     count = rows // QB
     span = keys.shape[1]
-    row = pl.BlockSpec((1, QB, HDIM), lambda h, i, a, b: (h, i, 0))
+    first = group * GROUP
+    row = pl.BlockSpec((1, QB, HDIM), lambda h, i, a, b: (h + first, i, 0))
     stat = pl.BlockSpec((1, NH, QB), lambda h, i, a, b: (i, 0, 0))
-    full = pl.BlockSpec((1, span, HDIM), lambda h, i, a, b: (h, 0, 0))
+    full = pl.BlockSpec((1, span, HDIM), lambda h, i, a, b: (h + first, 0, 0))
+    out = pl.BlockSpec((1, span, HDIM), lambda h, i, a, b: (h, 0, 0))
     return pl.pallas_call(
-        backward_kernel,
+        functools.partial(backward_kernel, first=first),
         out_shape=[
-            jax.ShapeDtypeStruct((NH, rows, HDIM), F32),
-            jax.ShapeDtypeStruct((NH, span, HDIM), F32),
-            jax.ShapeDtypeStruct((NH, span, HDIM), F32),
+            jax.ShapeDtypeStruct((GROUP, rows, HDIM), F32),
+            jax.ShapeDtypeStruct((GROUP, span, HDIM), BF),
+            jax.ShapeDtypeStruct((GROUP, span, HDIM), BF),
         ],
         grid_spec=pltpu.PrefetchScalarGridSpec(
             num_scalar_prefetch=2,
-            grid=(NH, count),
-            in_specs=[row, row, stat, stat, full, full],
-            out_specs=[row, full, full],
-            scratch_shapes=[pltpu.VMEM((HDIM, span), BF)],
+            grid=(GROUP, count),
+            in_specs=[
+                row,
+                row,
+                stat,
+                stat,
+                full,
+                full,
+                pl.BlockSpec((1, HDIM, span), lambda h, i, a, b: (h + first, 0, 0)),
+            ],
+            out_specs=[pl.BlockSpec((1, QB, HDIM), lambda h, i, a, b: (h, i, 0)), out, out],
+            scratch_shapes=[pltpu.VMEM((span, HDIM), F32)] * 2,
         ),
         compiler_params=room(),
+        cost_estimate=cost(rows * GPART * PLEN * 40, 32 * span * GPART),
         name="attention_backward",
-    )(tiles, lengths, queries, grads, log_total, row_delta, keys, values)
+    )(tiles, lengths, queries, grads, log_total, row_delta, keys, values, keys_t)
 
 
 def restore_kernel(tiles_ref, *refs):
@@ -775,10 +826,10 @@
     def write(out_ref):
         for j in range(4):
             rows = slice(j * BLK, (j + 1) * BLK)
-            for h in range(NH):
+            for h in range(GROUP):
                 cols = slice(h * HDIM, (h + 1) * HDIM)
-                out_ref[rows, cols] = refs[4 + j][h].astype(BF)
-                out_ref[rows, PART + h * HDIM : PART + (h + 1) * HDIM] = refs[j][h].astype(BF)
+                out_ref[rows, cols] = refs[4 + j][h]
+                out_ref[rows, GPART + h * HDIM : GPART + (h + 1) * HDIM] = refs[j][h]
 
     @pl.when(pl.program_id(0) < 8)
     def _():
@@ -790,11 +841,11 @@
 
 
 def restore_keys(tiles, grad_k, grad_v):
-    spec = lambda j: pl.BlockSpec((NH, BLK, HDIM), lambda i, o: (0, o[i * 4 + j], 0))
-    shape = (4 * BLK, 2 * PART)
+    spec = lambda j: pl.BlockSpec((GROUP, BLK, HDIM), lambda i, o: (0, o[i * 4 + j], 0))
+    shape = (4 * BLK, 2 * GPART)
     return pl.pallas_call(
         restore_kernel,
-        out_shape=[jax.ShapeDtypeStruct((32 * BLK, 2 * PART), BF)] * 2,
+        out_shape=[jax.ShapeDtypeStruct((32 * BLK, 2 * GPART), BF)] * 2,
         grid_spec=pltpu.PrefetchScalarGridSpec(
             num_scalar_prefetch=1,
             grid=(16,),
@@ -805,105 +856,170 @@
             ],
         ),
         compiler_params=room(),
+        cost_estimate=cost(0, 64 * 64 * BLK * GPART),
         name="restore_keys",
     )(tiles, *([grad_k] * 4), *([grad_v] * 4))
 
 
-def unproject_kernel(dq_ref, mine_ref, theirs_ref, w_ref, cos_ref, sin_ref, g_ref, x_ref, w_sc, y_sc):
+def unturn_kernel(dq_ref, mine_ref, theirs_ref, cos_ref, sin_ref, g_ref, y_sc):
+    kv = mine_ref[...].astype(F32) + theirs_ref[...].astype(F32)
+    for h in range(GROUP):
+        y_sc[:, h * HDIM : (h + 1) * HDIM] = dq_ref[h]
+    y_sc[:, GPART:] = kv[:, GPART:]
+    cosine, sine_vals = cos_ref[...], -sin_ref[...]
+    for k in range(GROUP):
+        cols = slice(k * 128, (k + 1) * 128)
+        g_ref[:, cols] = swing(y_sc[:, cols], cosine, sine_vals).astype(BF)
+    g_ref[:, 2 * GPART :] = kv[:, :GPART].astype(BF)
+
+
+def unturn(grad_q, mine, theirs, cosine, sine_vals):
+    rows = mine.shape[0]
+    size = 2 * QB
+    row = lambda n: pl.BlockSpec((size, n), lambda i: (i, 0))
+    return pl.pallas_call(
+        unturn_kernel,
+        out_shape=jax.ShapeDtypeStruct((rows, 3 * GPART), BF),
+        grid=(rows // size,),
+        in_specs=[
+            pl.BlockSpec((GROUP, size, HDIM), lambda i: (0, i, 0)),
+            row(2 * GPART),
+            row(2 * GPART),
+            row(128),
+            row(128),
+        ],
+        out_specs=row(3 * GPART),
+        scratch_shapes=[pltpu.VMEM((size, 2 * GPART), F32)],
+        compiler_params=room(),
+        cost_estimate=cost(0, 20 * rows * GPART),
+        name="unturn",
+    )(grad_q, mine, theirs, cosine, sine_vals)
+
+
+def unproject_kernel(a_ref, b_ref, c_ref, w_ref, x_ref, w_sc, y_sc):
     thin = w_sc.shape[0] // 32
 
     @pl.when(pl.program_id(0) == 0)
     def _():
         straighten(w_ref, w_sc, thin)
 
-    kv = mine_ref[...].astype(F32) + theirs_ref[...].astype(F32)
-    for h in range(NH):
-        y_sc[:, h * HDIM : (h + 1) * HDIM] = dq_ref[h]
-    y_sc[:, PART:] = kv[:, PART:]
-    cosine, sine_vals = cos_ref[...], -sin_ref[...]
-    for k in range(NH):
-        cols = slice(k * 128, (k + 1) * 128)
-        g_ref[:, cols] = swing(y_sc[:, cols], cosine, sine_vals).astype(BF)
-    g_ref[:, 2 * PART :] = kv[:, :PART].astype(BF)
-    x_ref[...] = mul(g_ref[...], w_sc[...], NT).astype(BF)
-
-
-def unproject(grad_q, mine, theirs, w_all, cosine, sine_vals):
-    rows = mine.shape[0]
+    for g, ref in enumerate((a_ref, b_ref, c_ref)):
+        for k in range(3):
+            y_sc[:, k * PART + g * GPART : k * PART + (g + 1) * GPART] = ref[
+                :, k * GPART : (k + 1) * GPART
+            ]
+    x_ref[...] = mul(y_sc[...], w_sc[...], NT).astype(BF)
+
+
+def unproject(parts, w_all, chunk):
+    rows = parts[0].shape[0] // 2
+    shift = chunk * (rows // QB)
     full = w_all.shape
     width = full[0] * full[1] * (full[2] - 8)
-    row = lambda n: pl.BlockSpec((QB, n), lambda i: (i, 0))
     return pl.pallas_call(
         unproject_kernel,
-        out_shape=[
-            jax.ShapeDtypeStruct((rows, 3 * PART), BF),
-            jax.ShapeDtypeStruct((rows, width), BF),
-        ],
+        out_shape=jax.ShapeDtypeStruct((rows, width), BF),
         grid=(rows // QB,),
-        in_specs=[
-            pl.BlockSpec((NH, QB, HDIM), lambda i: (0, i, 0)),
-            row(2 * PART),
-            row(2 * PART),
-            pl.BlockSpec(full, lambda i: (0, 0, 0, 0), pipeline_mode=pl.Buffered(1)),
-            row(128),
-            row(128),
-        ],
-        out_specs=[row(3 * PART), row(width)],
+        in_specs=[pl.BlockSpec((QB, 3 * GPART), lambda i: (i + shift, 0))] * 3
+        + [pl.BlockSpec(full, lambda i: (0, 0, 0, 0), pipeline_mode=pl.Buffered(1))],
+        out_specs=pl.BlockSpec((QB, width), lambda i: (i, 0)),
         scratch_shapes=[
             pltpu.VMEM((width, full[3]), BF),
-            pltpu.VMEM((QB, 2 * PART), F32),
+            pltpu.VMEM((QB, 3 * PART), BF),
         ],
         compiler_params=room(),
+        cost_estimate=cost(2 * rows * width * 3 * PART, 4 * rows * width),
         name="unproject",
-    )(grad_q, mine, theirs, w_all, cosine, sine_vals)
-
-
-def to_plane(rows):
-    blocks = rows.reshape(4, rows.shape[0] // 4, rows.shape[1])
-    blocks = lax.all_to_all(blocks, "p", 0, 0, tiled=True)
-    return lax.all_to_all(blocks, "z", 0, 0, tiled=True).reshape(rows.shape)
-
-
-def from_plane(rows):
-    blocks = rows.reshape(4, rows.shape[0] // 4, rows.shape[1])
-    blocks = lax.all_to_all(blocks, "z", 0, 0, tiled=True)
-    return lax.all_to_all(blocks, "p", 0, 0, tiled=True).reshape(rows.shape)
+    )(*parts, w_all)
+
+
+def split_tiles(rows):
+    blocks = rows.reshape(4, 2, rows.shape[0] // 8, rows.shape[1])
+    return blocks[:, 0], blocks[:, 1]
+
+
+def join_tiles(chunks):
+    blocks = jnp.stack(chunks, axis=1)
+    return blocks.reshape(-1, blocks.shape[-1])
+
+
+def over(name, blocks):
+    return lax.all_to_all(blocks, name, 0, 0, tiled=True)
+
+
+def quarters(rows):
+    return rows.reshape(4, rows.shape[0] // 4, rows.shape[1])
+
+
+def after(value, *earlier):
+    return lax.optimization_barrier((value, earlier))[0]
 
 
 def flip(values, mask):
     return lax.ppermute(values, "p", [(k, k ^ mask) for k in range(4)])
 
 
-def gather_slots(own):
-    half = own.shape[0] // 2
-    first = flip(own, 1)
-    second = flip(own, 2)
-    upper = flip(second[:half], 1)
-    lower = flip(first[half:], 2)
-    return jnp.concatenate([own, first, second, upper, lower], axis=0)
-
-
-def scatter_slots(terms):
+def gather_near(own):
+    return [own, flip(own, 1), flip(own, 2)]
+
+
+def gather_far(near):
+    half = near[0].shape[0] // 2
+    return near + [flip(near[2][:half], 1), flip(near[1][half:], 2)]
+
+
+def slots(terms):
     size = terms.shape[0] // 4
-    half = size // 2
-    low = lambda v: v.astype(BF)
-    upper = flip(low(terms[3 * size : 3 * size + half]), 1)
-    lower = flip(low(terms[3 * size + half :]), 2)
-    first = jnp.concatenate(
-        [
-            low(terms[size : size + half]),
-            low(terms[size + half : 2 * size].astype(F32) + lower.astype(F32)),
-        ],
-        axis=0,
-    )
-    second = jnp.concatenate(
-        [
-            low(terms[2 * size : 2 * size + half].astype(F32) + upper.astype(F32)),
-            low(terms[2 * size + half : 3 * size]),
-        ],
-        axis=0,
-    )
-    return terms[:size].astype(F32) + flip(first, 1).astype(F32) + flip(second, 2).astype(F32)
+    return [terms[k * size : (k + 1) * size] for k in range(4)]
+
+
+def scatter_far(terms):
+    far = slots(terms)[3]
+    half = far.shape[0] // 2
+    return flip(far[:half], 1), flip(far[half:], 2)
+
+
+def scatter_near(terms, far):
+    _, first, second, _ = slots(terms)
+    half = first.shape[0] // 2
+    add = lambda x, y: (x.astype(F32) + y.astype(F32)).astype(BF)
+    first = flip(jnp.concatenate([first[:half], add(first[half:], far[1])], axis=0), 1)
+    second = flip(jnp.concatenate([add(second[:half], far[0]), second[half:]], axis=0), 2)
+    return first, second
+
+
+def scatter_sum(terms, near):
+    return slots(terms)[0].astype(F32) + near[0].astype(F32) + near[1].astype(F32)
+
+
+def scatter_far_both(terms):
+    return flip(slots(terms[0])[3], 1), flip(slots(terms[1])[3], 2)
+
+
+def scatter_near_both(terms, far):
+    early, late = slots(terms[0]), slots(terms[1])
+    add = lambda x, y: (x.astype(F32) + y.astype(F32)).astype(BF)
+    first = flip(jnp.concatenate([early[1], add(late[1], far[1])], axis=0), 1)
+    second = flip(jnp.concatenate([add(early[2], far[0]), late[2]], axis=0), 2)
+    return first, second
+
+
+def meet(*values):
+    return lax.optimization_barrier(values)
+
+
+def swap_blocks(name, pieces):
+    return [pieces[0]] + [
+        lax.ppermute(pieces[r], name, [(k, k ^ r) for k in range(4)]) for r in (1, 2, 3)
+    ]
+
+
+def pick(pieces, first):
+    stacked = jnp.stack(pieces)
+    return [
+        lax.dynamic_index_in_dim(stacked, jnp.bitwise_xor(first, r), 0, keepdims=False)
+        for r in range(4)
+    ]
 
 
 def hidden_cuts(hidden):
@@ -936,34 +1052,43 @@
     hidden = w_down.shape[0]
     starts, sizes, share = hidden_cuts(hidden)
     gain_f = attn_gain.astype(F32)
-    moved = to_plane(tokens_in)
-    deal = lax.ppermute(deal_order[0], ("p", "z"), [(g * 4 + k, k * 4 + g) for g in range(4) for k in range(4)])
-    lengths = lax.ppermute(cont_len[0], ("p", "z"), [(g * 4 + k, k * 4 + g) for g in range(4) for k in range(4)])
+    parts_of = lambda v: [v[k] for k in range(4)]
+    cross = lambda v: swap_blocks("p", pick(v, plane))
+    cross_whole = lambda v: jnp.stack(pick(cross(parts_of(v)), plane))
+    hop_on = lambda v: swap_blocks("z", pick(v, jnp.bitwise_xor(plane, depth)))
+    hop_back = lambda v: swap_blocks("z", parts_of(quarters(v)))
+    hop_out = lambda v: pick(
+        swap_blocks("p", pick(v, jnp.bitwise_xor(plane, depth))), plane
+    )
+    first_hop = cross(parts_of(quarters(tokens_in)))
+    turn_over = [(g * 4 + k, k * 4 + g) for g in range(4) for k in range(4)]
+    deal = lax.ppermute(deal_order[0], ("p", "z"), turn_over)
+    lengths = lax.ppermute(cont_len[0], ("p", "z"), turn_over)
 
     scaled = [(w.astype(F32) * gain_f[:, None]).astype(BF) for w in (w_query, w_key, w_value)]
     blocks = jnp.stack(scaled).reshape(3, thin, 4, PART).transpose(2, 1, 0, 3)
     blocks = blocks.reshape(4, thin, 3 * PART)
     extra = jnp.zeros((4, 8, 3 * PART), BF).at[:, 0, :thin].set(ffn_gain[None, :])
     send = jnp.concatenate([blocks, extra], axis=1)
-    w_qkv = lax.all_gather(lax.all_to_all(send, "p", 0, 0, tiled=True), line, axis=0)
-    gain_two = w_qkv[:, :, thin, :thin].transpose(1, 0, 2).reshape(width).astype(F32)
-    w_out = lax.all_gather(w_output, line, axis=0, tiled=True)
-    stacked = jnp.stack([w_gate.T, w_up.T, w_down])
+    first_hop, send = meet(first_hop, send)
+    early = after((w_gate, w_up, w_down), first_hop)
+    stacked = jnp.stack([early[0].T, early[1].T, early[2]])
     stacked = jnp.stack(
         [
             jnp.pad(stacked[:, a : a + n], ((0, 0), (0, share - n), (0, 0)))
             for a, n in zip(starts, sizes)
         ]
     )
-    stacked = lax.all_to_all(stacked, "p", 0, 0, tiled=True)
-    stacked = stacked.transpose(1, 2, 0, 3).reshape(3, share, width)
-    w_ffn = [lax.all_gather(stacked[k], line, axis=0, tiled=True) for k in range(3)]
-
-    slot = jnp.arange(4)[:, None, None]
-    source = jnp.arange(4)[None, :, None]
-    pair = jnp.arange(2)[None, None, :]
+    send, moved = meet(cross_whole(send), hop_on(first_hop))
+    stacked = cross_whole(stacked)
+    w_qkv = lax.all_gather(send, line, axis=0)
+    gain_two = w_qkv[:, :, thin, :thin].transpose(1, 0, 2).reshape(width).astype(F32)
+    w_out = lax.all_gather(w_output, line, axis=0, tiled=True)
+    piece = jnp.arange(2)[:, None, None]
+    slot = jnp.arange(4)[None, :, None]
+    source = jnp.bitwise_xor(depth, jnp.arange(4))[None, None, :]
     quarter = jnp.bitwise_xor(plane, slot)
-    held = lambda which: deal[((source * 2 + which) * 8 + quarter * 2 + pair).reshape(-1)]
+    held = lambda which: deal[((source * 2 + which) * 8 + quarter * 2 + piece).reshape(-1)]
     tiles, tiles_far = held(core), held(1 - core)
     both = jnp.concatenate([tiles, tiles_far])
     numbers = jnp.arange(64, dtype=jnp.int32)
@@ -976,72 +1101,140 @@
     cosine = jnp.concatenate([cosine] * 4, axis=1)
     sine_vals = jnp.concatenate([-sine_vals, sine_vals] * 2, axis=1)
 
-    residual = moved.astype(F32)
-    inverse_one = lax.rsqrt(jnp.mean(residual * residual, axis=-1, keepdims=True) + norm_eps)
-    normed = gather_slots((residual * inverse_one).astype(BF))
-    queries, mine = project(normed, w_qkv, cosine, sine_vals)
+    joined = lambda pieces: jnp.concatenate(pieces, axis=0)
+    by_chunk = lambda v: [h.reshape(-1, width) for h in split_tiles(joined(v))]
+    residual = [v.astype(F32) for v in by_chunk(moved)]
+    inverse_of = lambda v: lax.rsqrt(jnp.mean(v * v, axis=-1, keepdims=True) + norm_eps)
+    inverse_one = [inverse_of(v) for v in residual]
+    pieces = gather_near(joined([(v * r).astype(BF) for v, r in zip(residual, inverse_one)]))
+    pieces = gather_far(pieces)
+
+    def in_chunks(pieces):
+        size = pieces[0].shape[0] // 2
+        return [
+            joined([v[k * size : (k + 1) * size] for v in pieces[:3]] + [pieces[3 + k]])
+            for k in range(2)
+        ]
+
+    pieces, w_qkv, grad_out = meet(pieces, w_qkv, cotangent)
+    (queries, mine), grad_out = meet(
+        project(pieces, w_qkv, cosine, sine_vals),
+        cross(parts_of(quarters(grad_out))),
+    )
+    normed = joined(in_chunks(pieces))
     theirs = lax.ppermute(mine, "c", [(0, 1), (1, 0)])
-    keys, values = sort_keys(order, mine, theirs)
-    attended, log_total, peaks = attention_forward(tiles, lengths, queries, keys, values)
-    after_attn = residual + branch_scale * scatter_slots(mul(attended, w_out))
-    inverse_two = lax.rsqrt(jnp.mean(after_attn * after_attn, axis=-1, keepdims=True) + norm_eps)
-    normed_two = gather_slots((after_attn * inverse_two * gain_two).astype(BF))
-
-    grad_out = to_plane(cotangent).astype(F32)
-    grad_rows = gather_slots((branch_scale * grad_out).astype(BF))
-    gate_pre = mul(normed_two, w_ffn[0], NT)
-    up_pre = mul(normed_two, w_ffn[1], NT)
-    mixed = (jax.nn.silu(gate_pre) * up_pre).astype(BF)
-    grad_mixed = mul(grad_rows, w_ffn[2], NT)
-    grad_gate_low, grad_up_low = gate_grads(grad_mixed, gate_pre, up_pre)
-    grad_normed_two = scatter_slots(mul(grad_gate_low, w_ffn[0]) + mul(grad_up_low, w_ffn[1]))
-    branch_ffn = scatter_slots(mul(mixed, w_ffn[2]))
-    output = from_plane((after_attn + branch_scale * branch_ffn).astype(BF))
-    ffn_grads = jnp.stack(
-        [
-            lax.psum_scatter(mul(a, b, TN).astype(BF), line, scatter_dimension=0, tiled=True)
-            for a, b in (
-                (grad_gate_low, normed_two),
-                (grad_up_low, normed_two),
-                (mixed, grad_rows),
-            )
-        ]
-    )
-    ffn_grads = ffn_grads.reshape(3, share, 4, PART).transpose(2, 0, 1, 3)
-    ffn_grads = lax.all_to_all(ffn_grads, "p", 0, 0, tiled=True).astype(F32)
-    ffn_grads = jnp.concatenate([ffn_grads[k, :, :n] for k, n in enumerate(sizes)], axis=1)
-
-    grad_gain_two, grad_second = norm_backward(grad_normed_two, after_attn, inverse_two, gain_two)
-    grad_resid = grad_out + grad_second
-    grad_branch = gather_slots((branch_scale * grad_resid).astype(BF))
-    grad_w_output = mul(attended, grad_branch, TN).astype(BF)
-    grad_w_output = lax.psum_scatter(grad_w_output, line, scatter_dimension=0, tiled=True)
-    grad_heads, row_delta = attention_delta(grad_branch, w_out, attended)
-    grad_q, grad_k, grad_v = attention_backward(
-        tiles, lengths, queries, grad_heads, log_total, row_delta, keys, values
-    )
-    part_mine, part_far = restore_keys(jnp.concatenate([tiles_far, tiles]), grad_k, grad_v)
-    received = lax.ppermute(part_far, "c", [(0, 1), (1, 0)])
-    grad_qkv, scaled_one = unproject(grad_q, part_mine, received, w_qkv, cosine, sine_vals)
-    scaled_one = scatter_slots(scaled_one)
-    grad_first = inverse_one * scaled_one - residual * inverse_one**3 * jnp.mean(
-        scaled_one * residual, axis=-1, keepdims=True
-    )
-    grad_input = from_plane((grad_resid + grad_first).astype(BF)).astype(F32)
-    proj = mul(normed, grad_qkv, TN).astype(BF)
-    proj = proj.reshape(4, 8, thin, 3 * PART).transpose(1, 0, 2, 3)
+    sorted_kv, grad_out, stacked = meet(
+        sort_keys(order, mine, theirs), hop_on(grad_out), stacked
+    )
+    keys, values, keys_t, values_t = sorted_kv
+    stacked = stacked.transpose(1, 2, 0, 3).reshape(3, share, width)
+    w_ffn = [lax.all_gather(stacked[k], line, axis=0, tiled=True) for k in range(3)]
+    attend = lambda q, k, n: attention_forward(tiles, lengths, q, keys, values_t, k, n)
+    grad_out = by_chunk(grad_out)
+    grad_rows = joined([(branch_scale * v.astype(F32)).astype(BF) for v in grad_out])
+    queries, grad_rows = meet(queries, grad_rows)
+    (low_a, total_a, peak_a), grad_rows = meet(attend(queries, 0, 4), gather_near(grad_rows))
+    branch_a = mul(low_a, w_out).astype(BF)
+    branch_a, grad_rows, queries_b = meet(branch_a, grad_rows, queries)
+    part_b, far_a = meet(attend(queries_b, 4, 2), scatter_far(branch_a))
+    rest_b, near_a, grad_rows = meet(
+        attend(queries_b, 6, 2), scatter_near(branch_a, far_a), gather_far(grad_rows)
+    )
+    low_b, total_b, peak_b = (joined([v, w]) for v, w in zip(part_b, rest_b))
+    branch_b = mul(low_b, w_out).astype(BF)
+    attended = joined([low_a, low_b])
+    log_total = joined([total_a, total_b])
+    peaks = joined([peak_a, peak_b])
+    grad_rows = in_chunks(grad_rows)
+
+    def second_norm(k, branch):
+        after_attn = residual[k] + branch_scale * branch
+        inverse_two = inverse_of(after_attn)
+        return after_attn, inverse_two, (after_attn * inverse_two * gain_two).astype(BF)
+
+    def hidden_layer(grad_mixed, normed_two):
+        gate_pre = mul(normed_two, w_ffn[0], NT)
+        up_pre = mul(normed_two, w_ffn[1], NT)
+        mixed = (jax.nn.silu(gate_pre) * up_pre).astype(BF)
+        return (mixed,) + gate_grads(grad_mixed, gate_pre, up_pre)
+
+    def hidden_back(hidden):
+        return (mul(hidden[1], w_ffn[0]) + mul(hidden[2], w_ffn[1])).astype(BF)
+
+    def second_back(k, total, state):
+        grad_gain, grad_second = norm_backward(total, state[0], state[1], gain_two)
+        grad_resid = grad_out[k].astype(F32) + grad_second
+        return grad_gain, grad_resid, (branch_scale * grad_resid).astype(BF)
+
+    state_a = second_norm(0, scatter_sum(branch_a, near_a))
+    own, rows_a, rows_b = meet(state_a[2], grad_rows[0], grad_rows[1])
+    gather, mixed_a, rows_b, branch_b = meet(
+        gather_near(own), mul(rows_a, w_ffn[2], NT), rows_b, branch_b
+    )
+    gather, far, mixed_b = meet(
+        gather_far(gather), scatter_far(branch_b), mul(rows_b, w_ffn[2], NT)
+    )
+    normed_a = joined(gather)
+    hidden_a, near = meet(hidden_layer(mixed_a, normed_a), scatter_near(branch_b, far))
+    state_b = second_norm(1, scatter_sum(branch_b, near))
+    hidden_a, own = meet(hidden_a, state_b[2])
+    rest_a, gather = meet(hidden_back(hidden_a), gather_near(own))
+    first = mul(hidden_a[1], normed_a, TN)
+    gather, far, gate_a = meet(gather_far(gather), scatter_far(rest_a), first)
+    normed_b = joined(gather)
+    hidden_b, near = meet(hidden_layer(mixed_b, normed_b), scatter_near(rest_a, far))
+    back_a = second_back(0, scatter_sum(rest_a, near), state_a)
+    hidden_b, own = meet(hidden_b, back_a[2])
+    rest_b, gather_a = meet(hidden_back(hidden_b), gather_near(own))
+    grad_gate = (gate_a + mul(hidden_b[1], normed_b, TN)).astype(BF)
+    up_a = mul(hidden_a[2], normed_a, TN)
+    gather_a, far, grad_gate, up_a = meet(
+        gather_far(gather_a), scatter_far(rest_b), grad_gate, up_a
+    )
+    grad_up = (up_a + mul(hidden_b[2], normed_b, TN)).astype(BF)
+    down_a = mul(hidden_a[0], rows_a, TN)
+    near, grad_up, down_a = meet(scatter_near(rest_b, far), grad_up, down_a)
+    back_b = second_back(1, scatter_sum(rest_b, near), state_b)
+    own, mixed_b_rows, down_a = meet(back_b[2], hidden_b[0], down_a)
+    grad_down = (down_a + mul(mixed_b_rows, rows_b, TN)).astype(BF)
+    gather_b, grad_down, ffn_b = meet(
+        gather_near(own), grad_down, mul(mixed_b_rows, w_ffn[2]).astype(BF)
+    )
+    gather_b, ffn_a = meet(gather_far(gather_b), mul(hidden_a[0], w_ffn[2]).astype(BF))
+    branch_ffn = [ffn_a, ffn_b]
+    sum_rows = lambda v: lax.psum_scatter(v, line, scatter_dimension=0, tiled=True)
+    grad_pieces = gather_a + gather_b
+    grad_gain_two = back_a[0] + back_b[0]
+    grad_resid = [back_a[1], back_b[1]]
+
+    grad_pieces, branch_ffn, grad_gate = meet(grad_pieces, branch_ffn, sum_rows(grad_gate))
+    (grad_heads, row_delta), far, grad_up = meet(
+        attention_delta(grad_pieces, w_out, attended),
+        scatter_far_both(branch_ffn),
+        sum_rows(grad_up),
+    )
+    grad_w_part = mul(attended, joined(grad_pieces), TN).astype(BF)
+
+    far_order = jnp.concatenate([tiles_far, tiles])
     gain_rows = grad_gain_two.astype(BF).reshape(4, 8, 1, thin).transpose(1, 0, 2, 3)
-    gain_rows = jnp.pad(gain_rows, ((0, 0), (0, 0), (0, 7), (0, 3 * PART - thin)))
-    proj = jnp.concatenate([proj, gain_rows], axis=2).reshape(8 * 4 * (thin + 8), 3 * PART)
-    proj = lax.psum_scatter(proj, line, scatter_dimension=0, tiled=True)
-    proj = proj.reshape(4, thin + 8, 3 * PART)
-    proj = lax.all_to_all(proj, "p", 0, 0, tiled=True).astype(F32)
-    grad_ffn_gain = jnp.sum(proj[:, thin, :thin], axis=0)
-    proj = proj[:, :thin].reshape(4, thin, 3, PART).transpose(2, 1, 0, 3).reshape(3, thin, width)
-    grad_attn_gain = sum(
-        jnp.sum(w.astype(F32) * proj[k], axis=1) for k, w in enumerate((w_query, w_key, w_value))
-    )
-    proj = proj * gain_f[None, :, None]
+    gain_rows = jnp.pad(gain_rows, ((0, 0), (0, 0), (0, 7), (0, 3 * GPART - thin)))
+
+    def back_group(g, grads):
+        return attention_backward(
+            tiles, lengths, queries, grads, log_total, row_delta, keys, values, keys_t, g
+        )
+
+    def restore(part):
+        return (part[0],) + tuple(restore_keys(far_order, part[1], part[2]))
+
+    def weight_part(grad_qkv):
+        proj = mul(normed, grad_qkv, TN).astype(BF).reshape(4, 8, thin, 3 * GPART)
+        proj = jnp.concatenate([proj.transpose(1, 0, 2, 3), gain_rows], axis=2)
+        return proj.reshape(8 * 4 * (thin + 8), 3 * GPART)
+
+    def sum_line(proj):
+        proj = lax.psum_scatter(proj, line, scatter_dimension=0, tiled=True)
+        return proj.reshape(4, thin + 8, 3 * GPART)
 
     maxima = jnp.where(
         jnp.arange(4)[:, None] == plane, jnp.max(peaks, axis=(0, 2))[None, :], masked_value
@@ -1049,6 +1242,79 @@
     for name, mask, size in (("c", 1, 2), ("p", 1, 4), ("p", 2, 4), ("z", 1, 4), ("z", 2, 4)):
         pairs = [(k, k ^ mask) for k in range(size)]
         maxima = jnp.maximum(maxima, lax.ppermute(maxima, name, pairs))
+    trade = lambda v: lax.ppermute(v, "c", [(0, 1), (1, 0)])
+    grad_heads, grad_w_part = meet(grad_heads, grad_w_part)
+    part_a, grad_heads, near, grad_down, grad_w_output = meet(
+        back_group(0, grad_heads),
+        grad_heads,
+        scatter_near_both(branch_ffn, far),
+        sum_rows(grad_down),
+        sum_rows(grad_w_part),
+    )
+    part_a = restore(part_a)
+    states = (state_a, state_b)
+    output = []
+    for k, (state, v) in enumerate(zip(states, branch_ffn)):
+        size = state[0].shape[0]
+        total = scatter_sum(v, [w[k * size : (k + 1) * size] for w in near])
+        output.append(quarters((state[0] + branch_scale * total).astype(BF)))
+    output = join_tiles(output)
+    ffn_grads = jnp.stack([grad_gate, grad_up, grad_down])
+    ffn_grads = ffn_grads.reshape(3, share, 4, PART).transpose(2, 0, 1, 3)
+    output, grad_heads, part_a, ffn_grads = meet(output, grad_heads, part_a, ffn_grads)
+    part_b, grad_heads, hops, far_a, maxima, ffn_grads = meet(
+        back_group(1, grad_heads),
+        grad_heads,
+        hop_back(output),
+        trade(part_a[2]),
+        maxima,
+        cross_whole(ffn_grads),
+    )
+    part_b = restore(part_b)
+    grads_a = unturn(part_a[0], part_a[1], far_a, cosine, sine_vals)
+    weights_a = weight_part(grads_a)
+    grad_heads, weights_a, hops, part_b = meet(grad_heads, weights_a, hops, part_b)
+    part_c, output, far_b, weights_a = meet(
+        back_group(2, grad_heads),
+        hop_out(hops),
+        trade(part_b[2]),
+        sum_line(weights_a),
+    )
+    part_c = restore(part_c)
+    grads_b = unturn(part_b[0], part_b[1], far_b, cosine, sine_vals)
+    weights_b, far_c = meet(weight_part(grads_b), trade(part_c[2]))
+    output = joined(output)
+    weights_b = sum_line(weights_b)
+    grads_c = unturn(part_c[0], part_c[1], far_c, cosine, sine_vals)
+    grads = (grads_a, grads_b, grads_c)
+    rest_a, grads = meet(unproject(grads, w_qkv, 0), grads)
+    rest_b, far_a, grads_c = meet(unproject(grads, w_qkv, 1), scatter_far(rest_a), grads[2])
+    weights_c, near_a, far_b = meet(
+        weight_part(grads_c), scatter_near(rest_a, far_a), scatter_far(rest_b)
+    )
+    weights_c = sum_line(weights_c)
+
+    def first_back(k, total):
+        grad_first = inverse_one[k] * total - residual[k] * inverse_one[k] ** 3 * jnp.mean(
+            total * residual[k], axis=-1, keepdims=True
+        )
+        return (grad_resid[k] + grad_first).astype(BF)
+
+    near_b = scatter_near(rest_b, far_b)
+    hop_a, near_b = meet(hop_back(first_back(0, scatter_sum(rest_a, near_a))), near_b)
+    hop_b, hop_a = meet(hop_back(first_back(1, scatter_sum(rest_b, near_b))), hop_out(hop_a))
+    grad_input = join_tiles([jnp.stack(hop_a), jnp.stack(hop_out(hop_b))]).astype(F32)
+    ffn_grads = ffn_grads.astype(F32)
+    ffn_grads = jnp.concatenate([ffn_grads[k, :, :n] for k, n in enumerate(sizes)], axis=1)
+    proj = over("p", jnp.concatenate([weights_a, weights_b, weights_c], axis=2)).astype(F32)
+    grad_ffn_gain = jnp.sum(proj[:, thin, :thin], axis=0)
+    proj = proj[:, :thin].reshape(4, thin, 3, 3, GPART).transpose(3, 1, 0, 2, 4)
+    proj = proj.reshape(3, thin, width)
+    grad_attn_gain = sum(
+        jnp.sum(w.astype(F32) * proj[k], axis=1) for k, w in enumerate((w_query, w_key, w_value))
+    )
+    proj = proj * gain_f[None, :, None]
+
     limit_value = clip_threshold[0].astype(F32)
     clip_factor = jnp.sqrt(limit_value / jnp.maximum(maxima, limit_value))
     column_factor = jnp.repeat(clip_factor, HDIM)

time: 1760 us -> 1580 us (0.90)
  waiting for transfers between devices: 684 us -> 353 us
  blocking collectives: 82.8 us -> 0 us
  local copies, waits for them, and re-layouts: 137 us -> 200 us
  Pallas kernels: 363 us -> 419 us
  other arithmetic: 103 us -> 153 us
  matrix products: 241 us -> 269 us
  starting transfers between devices: 128 us -> 147 us
    ppermute x32 -> x52, waiting for transfers between devices: 378 us -> 110 us  [flip(): return lax.ppermute(values, 'p', [(k, k ^ mask) for k in range(4)])]
    all_to_all x9 -> x1, waiting for transfers between devices: 275 us -> 9.27 us  [over(): return lax.all_to_all(blocks, name, 0, 0, tiled=True)]
    ppermute x3 -> x44, waiting for transfers between devices: 0.01 us -> 226 us  [the longest x39 218 us: swap_blocks(): lax.ppermute(pieces[r], name, [(k, k ^ r) for k in range(4)])]
    all_to_all x3 -> x0, blocking collectives: 82.8 us -> none  [the longest x1 34.7 us: inner(): stacked = lax.all_to_all(stacked, 'p', 0, 0, tiled=True)]
    all_to_all x9 -> x1, starting transfers between devices: 69.7 us -> 3.78 us  [over(): return lax.all_to_all(blocks, name, 0, 0, tiled=True)]
    ppermute x3 -> x44, starting transfers between devices: 10.6 us -> 64 us  [the longest x39 56.9 us: swap_blocks(): lax.ppermute(pieces[r], name, [(k, k ^ r) for k in range(4)])]
    convert_element_type x8 -> x26, other arithmetic: 24.8 us -> 62.2 us  [the longest x2 18.3 us: gate_grads(): return (grad_gate.astype(jnp.bfloat16), grad_up.astype(jnp.bfloat16))]
    pallas_call x3 -> x11, Pallas kernels: 275 us -> 310 us  [the longest x3 172 us: attention_backward(): pl.pallas_call(functools.partial(backward_kernel, first=first), out_shape...]
  transfers between devices with their start and end apart: 60 -> 115, of which waited for: 28 -> 42; matrix products, arithmetic and copies ran while one was open for 22% -> 34% of each run, Pallas kernels for 21% -> 23%
where the time goes in v2:
time: 1580 us; the launch traced here: 1560 us
  Pallas kernels  419 us (27%)
  waiting for transfers between devices  353 us (22%)
  matrix products  269 us (17%)
  local copies, waits for them, and re-layouts  200 us (13%)
  other arithmetic  153 us (10%)
  starting transfers between devices  147 us (9%)
  between operations  17.4 us (1%)
    dot_general x24, matrix products, mul(): return lax.dot_general(left, right, dims, preferred_element_type=F32)  269 us
    ppermute x39, waiting for transfers between devices, swap_blocks(): lax.ppermute(pieces[r], name, [(k, k ^ r) for k in range(4)])  218 us
    pallas_call x3, Pallas kernels, attention_backward(): pl.pallas_call(functools.partial(backward_kernel, first=first), out_shape...  172 us
    ppermute x52, waiting for transfers between devices, flip(): return lax.ppermute(values, 'p', [(k, k ^ mask) for k in range(4)])  110 us
    pallas_call x3, Pallas kernels, attention_forward(): pl.pallas_call(functools.partial(forward_kernel, shift=shift), out_shape=...  88.8 us
    unnamed x297, local copies, waits for them, and re-layouts  65 us
    ppermute x52, starting transfers between devices, flip(): return lax.ppermute(values, 'p', [(k, k ^ mask) for k in range(4)])  64.7 us
    ppermute x39, starting transfers between devices, swap_blocks(): lax.ppermute(pieces[r], name, [(k, k ^ r) for k in range(4)])  56.9 us
  transfers between devices with their start and end apart: 115, of which 42 were waited for; matrix products, arithmetic and copies ran while one was open for 34% of the time, Pallas kernels for 23%

profile of v2, /device:TPU:8, one launch (start us, length us, event | category | flops | bytes accessed | tf_op | source)
XLA Modules:
  0.0 1558.2 jit_solution(11420088956172209915)
XLA Ops:
  68.6 19.7 %collective-permute-done.9 = bf16[128,2304]{1,0:T(8,128)(2,1)S(1)} collective-permute-done((bf16[128,2304]{1,0:T(8,128)(2,1)S(1)}, bf16[128,2304]{1,0:T(8,128)(2,1)S(1)}, u32[]{:S(2)}, u32[]{:S(2)}) %collective-permute-start.9) | collective-permute-done | bytes 589856 | tf_op jit(solution)/shard_map/ppermute | solution.py:1013
  114.5 40.5 %collective-permute-done.12.refs_2_ = bf16[512,2304]{1,0:T(8,128)(2,1)} collective-permute-done((bf16[512,2304]{1,0:T(8,128)(2,1)}, bf16[512,2304]{1,0:T(8,128)(2,1)}, u32[]{:S(2)}, u32[]{:S(2)}) %collective-permute-start.12) | collective-permute-done | bytes 2359328 | tf_op jit(solution)/shard_map/ppermute | solution.py:959
  167.4 13.1 collective-permute-done.13.refs_3_
  190.2 27.8 %project.1 = (bf16[9,2048,64]{2,1,0:T(8,128)(2,1)}, bf16[2048,1152]{1,0:T(8,128)(2,1)}) custom-call(bf16[512,2304]{1,0:T(8,128)(2,1)} %pad_maximum_fusion.12.refs_0_, bf16[512,2304]{1,0:T(8,128)(2,1)} %collective-permute-done.11.refs_1_, bf16[512,2304]{1,0:T(8,128)(2,1)} %collective-permute-done.12.refs_2_, ...), custom_call_target="tpu_custom_call" | custom-call | flops 16307453952 | bytes 29196288 | tf_op jit(solution)/shard_map/project/pallas_call | solution.py:486
  268.8 23.9 %sort_keys.1 = (bf16[9,4096,64]{2,1,0:T(8,128)(2,1)}, bf16[9,4096,64]{2,1,0:T(8,128)(2,1)}, bf16[9,64,4096]{2,1,0:T(8,128)(2,1)}, bf16[9,64,4096]{2,1,0:T(8,128)(2,1)}) custom-call(s32[64]{0:T(128)} %select_reduce_fusion.order_ref, bf16[32,64,1152]{2,1,0:T(8,128)(2,1)} %bitcast.332, bf16[32,64,1152]{2,1,0:T(8,128)(2,1)} %bitcast.333, ...), custom_call_target="tpu_custom_call" | custom-call | bytes 150994944 | tf_op jit(solution)/shard_map/sort_keys/pallas_call | solution.py:530
  292.7 14.4 collective-permute-done.21
  327.6 44.8 %attention_forward.3 = (bf16[1024,576]{1,0:T(8,128)(2,1)}, f32[4,9,256]{2,1,0:T(8,128)}, f32[4,9,256]{2,1,0:T(8,128)}) custom-call(s32[32]{0:T(128)} %copy-done.112, s32[8]{0:T(128)} %copy-done.123, bf16[9,2048,64]{2,1,0:T(8,128)(2,1)} %get-tuple-element.340.q_ref, bf16[9,4096,64]{2,1,0:T(8,128)(2,1)} %get-tuple-element.329.k_ref, ...), custom_call_target="tpu_custom_call" | custom-call | flops 24159191040 | bytes 37748736 | tf_op jit(solution)/shard_map/attention_forward/pallas_call | solution.py:662
  388.7 17.0 %attention_forward.5 = (bf16[512,576]{1,0:T(8,128)(2,1)}, f32[2,9,256]{2,1,0:T(8,128)}, f32[2,9,256]{2,1,0:T(8,128)}) custom-call(s32[32]{0:T(128)} %copy-done.112, s32[8]{0:T(128)} %copy-done.123, bf16[9,2048,64]{2,1,0:T(8,128)(2,1)} %get-tuple-element.340.q_ref, bf16[9,4096,64]{2,1,0:T(8,128)(2,1)} %get-tuple-element.329.k_ref, ...), custom_call_target="tpu_custom_call" | custom-call | flops 12079595520 | bytes 37748736 | tf_op jit(solution)/shard_map/attention_forward/pallas_call | solution.py:662
  425.4 27.1 %attention_forward.4 = (bf16[512,576]{1,0:T(8,128)(2,1)}, f32[2,9,256]{2,1,0:T(8,128)}, f32[2,9,256]{2,1,0:T(8,128)}) custom-call(s32[32]{0:T(128)} %copy-done.112, s32[8]{0:T(128)} %copy-done.123, bf16[9,2048,64]{2,1,0:T(8,128)(2,1)} %get-tuple-element.340.q_ref, bf16[9,4096,64]{2,1,0:T(8,128)(2,1)} %get-tuple-element.329.k_ref, ...), custom_call_target="tpu_custom_call" | custom-call | flops 12079595520 | bytes 37748736 | tf_op jit(solution)/shard_map/attention_forward/pallas_call | solution.py:662
  476.6 12.8 fusion.67
  632.9 12.8 fusion.73
  674.4 13.3 fusion.75
  700.0 14.7 fusion.76
  734.5 13.2 fusion.79
  911.1 21.6 %attention_delta.1 = (bf16[9,2048,64]{2,1,0:T(8,128)(2,1)}, f32[8,9,256]{2,1,0:T(8,128)}) custom-call(bf16[256,2304]{1,0:T(8,128)(2,1)} %copy-done.26, bf16[256,2304]{1,0:T(8,128)(2,1)} %copy-done.47, bf16[256,2304]{1,0:T(8,128)(2,1)} %copy-done.49, bf16[128,2304]{1,0:T(8,128)(2,1)} %collective-permute-done.51.refs_3_, ...), custom_call_target="tpu_custom_call" | custom-call | flops 5435817984 | bytes 9437184 | tf_op jit(solution)/shard_map/attention_delta/pallas_call | solution.py:705
  955.6 56.9 %attention_backward.3 = (f32[3,2048,64]{2,1,0:T(8,128)}, bf16[3,4096,64]{2,1,0:T(8,128)(2,1)}, bf16[3,4096,64]{2,1,0:T(8,128)(2,1)}) custom-call(s32[32]{0:T(128)} %copy-done.112, s32[8]{0:T(128)} %copy-done.123, bf16[9,2048,64]{2,1,0:T(8,128)(2,1)} %get-tuple-element.340.q_ref, bf16[9,2048,64]{2,1,0:T(8,128)(2,1)} %get-tuple-element.502.g_ref, ...), custom_call_target="tpu_custom_call" | custom-call | flops 32212254720 | bytes 25165824 | tf_op jit(solution)/shard_map/attention_backward/pallas_call | solution.py:795
  1042.6 57.1 %attention_backward.4 = (f32[3,2048,64]{2,1,0:T(8,128)}, bf16[3,4096,64]{2,1,0:T(8,128)(2,1)}, bf16[3,4096,64]{2,1,0:T(8,128)(2,1)}) custom-call(s32[32]{0:T(128)} %copy-done.112, s32[8]{0:T(128)} %copy-done.123, bf16[9,2048,64]{2,1,0:T(8,128)(2,1)} %get-tuple-element.340.q_ref, bf16[9,2048,64]{2,1,0:T(8,128)(2,1)} %get-tuple-element.502.g_ref, ...), custom_call_target="tpu_custom_call" | custom-call | flops 32212254720 | bytes 25165824 | tf_op jit(solution)/shard_map/attention_backward/pallas_call | solution.py:795
  1108.6 33.2 %collective-permute-done.66 = bf16[128,2304]{1,0:T(8,128)(2,1)S(1)} collective-permute-done((bf16[128,2304]{1,0:T(8,128)(2,1)}, bf16[128,2304]{1,0:T(8,128)(2,1)S(1)}, u32[]{:S(2)}, u32[]{:S(2)}) %collective-permute-start.66) | collective-permute-done | bytes 589856 | tf_op jit(solution)/shard_map/ppermute | solution.py:1013
  1198.2 57.5 %attention_backward.5 = (f32[3,2048,64]{2,1,0:T(8,128)}, bf16[3,4096,64]{2,1,0:T(8,128)(2,1)}, bf16[3,4096,64]{2,1,0:T(8,128)(2,1)}) custom-call(s32[32]{0:T(128)} %copy-done.112, s32[8]{0:T(128)} %copy-done.123, bf16[9,2048,64]{2,1,0:T(8,128)(2,1)} %get-tuple-element.340.q_ref, bf16[9,2048,64]{2,1,0:T(8,128)(2,1)} %get-tuple-element.502.g_ref, ...), custom_call_target="tpu_custom_call" | custom-call | flops 32212254720 | bytes 25165824 | tf_op jit(solution)/shard_map/attention_backward/pallas_call | solution.py:795
  1313.8 15.3 unproject.2
  1333.2 15.2 unproject.3
  1374.4 17.0 %collective-permute-done.86 = bf16[128,2304]{1,0:T(8,128)(2,1)} collective-permute-done((bf16[128,2304]{1,0:T(8,128)(2,1)}, bf16[128,2304]{1,0:T(8,128)(2,1)}, u32[]{:S(2)}, u32[]{:S(2)}) %collective-permute-start.86) | collective-permute-done | bytes 589856 | tf_op jit(solution)/shard_map/ppermute | solution.py:959
  1416.0 20.7 %collective-permute-done.89 = bf16[64,2304]{1,0:T(8,128)(2,1)} collective-permute-done((bf16[64,2304]{1,0:T(8,128)(2,1)}, bf16[64,2304]{1,0:T(8,128)(2,1)}, u32[]{:S(2)}, u32[]{:S(2)}) %collective-permute-start.89) | collective-permute-done | bytes 294944 | tf_op jit(solution)/shard_map/ppermute | solution.py:1013
  1436.7 12.8 collective-permute-done.90
  (802 shorter events, 938.6 us)
Async XLA Ops:
  7.2 176.5 %all-gather.15.cloned.1.call-start = ((), (), s32[]{:S(2)}) async-start(), calls=%async_computation.19 | async-start | bytes 10321920 | tf_op jit(solution)/shard_map/all_gather | solution.py:1084
  99.3 274.5 %all-gather.7.cloned.1.call-start = ((), (), s32[]{:S(2)}) async-start(), calls=%async_computation.8 | async-start | bytes 2985984 | tf_op jit(solution)/shard_map/all_gather | solution.py:1086
  218.1 258.5 %all-gather.9.cloned.1.call-start = ((), (), s32[]{:S(2)}) async-start(), calls=%async_computation.9 | async-start | bytes 7630848 | tf_op jit(solution)/shard_map/all_gather | solution.py:1131
  310.6 220.0 %all-gather.11.cloned.1.call-start = ((), (), s32[]{:S(2)}) async-start(), calls=%async_computation.10 | async-start | bytes 7630848 | tf_op jit(solution)/shard_map/all_gather | solution.py:1131
  313.8 229.2 %all-gather.13.cloned.1.call-start = ((), (), s32[]{:S(2)}) async-start(), calls=%async_computation.11 | async-start | bytes 7630848 | tf_op jit(solution)/shard_map/all_gather | solution.py:1131
  385.4 67.0 %collective-permute-start.31 = (bf16[256,2304]{1,0:T(8,128)(2,1)}, bf16[256,2304]{1,0:T(8,128)(2,1)}, u32[]{:S(2)}, u32[]{:S(2)}) collective-permute-start(bf16[256,2304]{1,0:T(8,128)(2,1)} %slice.537), channel_id=1, source_target_pairs={{0,8},{8,0},{16,24},{24,16},{1,9},{9,1},{17,25},{25,17},{2,10},{10... | collective-permute-start | bytes 3538952 | tf_op jit(solution)/shard_map/ppermute | solution.py:959
  388.1 64.3 %collective-permute-start.32 = (bf16[256,2304]{1,0:T(8,128)(2,1)}, bf16[256,2304]{1,0:T(8,128)(2,1)}, u32[]{:S(2)}, u32[]{:S(2)}) collective-permute-start(bf16[256,2304]{1,0:T(8,128)(2,1)} %slice.538), channel_id=1, source_target_pairs={{0,16},{8,24},{16,0},{24,8},{1,17},{9,25},{17,1},{25,9},{2,18},{10... | collective-permute-start | bytes 3538952 | tf_op jit(solution)/shard_map/ppermute | solution.py:959
  425.3 456.8 %reduce-scatter.8.cloned.1.call-start = ((), (), s32[]{:S(2)}) async-start(), calls=%async_computation.12 | async-start | bytes 7630848 | tf_op jit(solution)/shard_map/reduce_scatter | solution.py:1205
  734.5 208.2 %reduce-scatter.10.cloned.1.call-start = ((), (), s32[]{:S(2)}) async-start(), calls=%async_computation.13 | async-start | bytes 7630848 | tf_op jit(solution)/shard_map/reduce_scatter | solution.py:1205
  779.3 233.3 %reduce-scatter.12.cloned.1.call-start = ((), (), s32[]{:S(2)}) async-start(), calls=%async_computation.14 | async-start | bytes 7630848 | tf_op jit(solution)/shard_map/reduce_scatter | solution.py:1205
  823.2 189.5 %reduce-scatter.14.cloned.1.call-start = ((), (), s32[]{:S(2)}) async-start(), calls=%async_computation.15 | async-start | bytes 2985984 | tf_op jit(solution)/shard_map/reduce_scatter | solution.py:1205
  942.8 326.6 %reduce-scatter.16.cloned.1.call-start = ((), (), s32[]{:S(2)}) async-start(), calls=%async_computation.16 | async-start | bytes 3686400 | tf_op jit(solution)/shard_map/reduce_scatter | solution.py:1236
  946.6 66.0 %collective-permute-start.63 = (bf16[512,2304]{1,0:T(8,128)(2,1)}, bf16[512,2304]{1,0:T(8,128)(2,1)}, u32[]{:S(2)}, u32[]{:S(2)}) collective-permute-start(bf16[512,2304]{1,0:T(8,128)(2,1)} %pad_maximum_fusion.17), channel_id=1, source_target_pairs={{0,8},{8,0},{16,24},{24,16},{1,9},{9,1},{17,25},{25,17},{2,10},{10... | collective-permute-start | bytes 7077896 | tf_op jit(solution)/shard_map/ppermute | solution.py:959
  1034.7 74.0 %collective-permute-start.65 = (bf16[128,2304]{1,0:T(8,128)(2,1)}, bf16[128,2304]{1,0:T(8,128)(2,1)S(1)}, u32[]{:S(2)}, u32[]{:S(2)}) collective-permute-start(bf16[128,2304]{1,0:T(8,128)(2,1)} %get-tuple-element.722), channel_id=1, source_target_pairs={{0,2},{2,0},{4,6},{6,4},{1,3},{3,1},{5,7},{7,5},{8,10},{10,8},{12,... | collective-permute-start | bytes 1769480 | tf_op jit(solution)/shard_map/ppermute | solution.py:1013
  1038.8 115.5 %collective-permute-start.68 = (bf16[2048,384]{1,0:T(8,128)(2,1)}, bf16[2048,384]{1,0:T(8,128)(2,1)S(1)}, u32[]{:S(2)}, u32[]{:S(2)}) collective-permute-start(bf16[2048,384]{1,0:T(8,128)(2,1)} %get-tuple-element.484), channel_id=1, source_target_pairs={{0,1},{1,0},{2,3},{3,2},{4,5},{5,4},{6,7},{7,6},{8,9},{9,8},{10,11... | collective-permute-start | bytes 4718600 | tf_op jit(solution)/shard_map/ppermute | solution.py:1245
  1039.1 62.6 %collective-permute-start.76 = (bf16[3,184,576]{2,1,0:T(8,128)(2,1)S(1)}, bf16[3,184,576]{2,1,0:T(8,128)(2,1)S(1)}, u32[]{:S(2)}, u32[]{:S(2)}) collective-permute-start(bf16[3,184,576]{2,1,0:T(8,128)(2,1)S(1)} %get-tuple-element.694), channel_id=1, source_target_pairs={{0,24},{8,16},{16,8},{24,0},{1,25},{9,17},{17,9},{25,1},{2,26},{10... | collective-permute-start | bytes 1907720 | tf_op jit(solution)/shard_map/ppermute | solution.py:1013
  1039.5 64.5 %collective-permute-start.75 = (bf16[3,184,576]{2,1,0:T(8,128)(2,1)S(1)}, bf16[3,184,576]{2,1,0:T(8,128)(2,1)S(1)}, u32[]{:S(2)}, u32[]{:S(2)}) collective-permute-start(bf16[3,184,576]{2,1,0:T(8,128)(2,1)S(1)} %get-tuple-element.695), channel_id=1, source_target_pairs={{0,16},{8,24},{16,0},{24,8},{1,17},{9,25},{17,1},{25,9},{2,18},{10... | collective-permute-start | bytes 1907720 | tf_op jit(solution)/shard_map/ppermute | solution.py:1013
  1041.5 64.1 %collective-permute-start.74 = (bf16[3,184,576]{2,1,0:T(8,128)(2,1)S(1)}, bf16[3,184,576]{2,1,0:T(8,128)(2,1)S(1)}, u32[]{:S(2)}, u32[]{:S(2)}) collective-permute-start(bf16[3,184,576]{2,1,0:T(8,128)(2,1)S(1)} %get-tuple-element.696), channel_id=1, source_target_pairs={{0,8},{8,0},{16,24},{24,16},{1,9},{9,1},{17,25},{25,17},{2,10},{10... | collective-permute-start | bytes 1907720 | tf_op jit(solution)/shard_map/ppermute | solution.py:1013
  1191.0 311.8 %reduce-scatter.18.cloned.1.call-start = ((), (), s32[]{:S(2)}) async-start(), calls=%async_computation.17 | async-start | bytes 3686400 | tf_op jit(solution)/shard_map/reduce_scatter | solution.py:1236
  1194.0 72.4 %collective-permute-start.79 = (bf16[128,2304]{1,0:T(8,128)(2,1)}, bf16[128,2304]{1,0:T(8,128)(2,1)S(1)}, u32[]{:S(2)}, u32[]{:S(2)}) collective-permute-start(bf16[128,2304]{1,0:T(8,128)(2,1)} %get-tuple-element.717), channel_id=1, source_target_pairs={{0,24},{8,16},{16,8},{24,0},{1,25},{9,17},{17,9},{25,1},{2,26},{10... | collective-permute-start | bytes 1769480 | tf_op jit(solution)/shard_map/ppermute | solution.py:1013
  1195.6 70.7 %collective-permute-start.78 = (bf16[128,2304]{1,0:T(8,128)(2,1)}, bf16[128,2304]{1,0:T(8,128)(2,1)}, u32[]{:S(2)}, u32[]{:S(2)}) collective-permute-start(bf16[128,2304]{1,0:T(8,128)(2,1)} %get-tuple-element.718), channel_id=1, source_target_pairs={{0,16},{8,24},{16,0},{24,8},{1,17},{9,25},{17,1},{25,9},{2,18},{10... | collective-permute-start | bytes 1769480 | tf_op jit(solution)/shard_map/ppermute | solution.py:1013
  1196.3 70.0 %collective-permute-start.77 = (bf16[128,2304]{1,0:T(8,128)(2,1)}, bf16[128,2304]{1,0:T(8,128)(2,1)}, u32[]{:S(2)}, u32[]{:S(2)}) collective-permute-start(bf16[128,2304]{1,0:T(8,128)(2,1)} %get-tuple-element.719), channel_id=1, source_target_pairs={{0,8},{8,0},{16,24},{24,16},{1,9},{9,1},{17,25},{25,17},{2,10},{10... | collective-permute-start | bytes 1769480 | tf_op jit(solution)/shard_map/ppermute | solution.py:1013
  1197.5 71.9 %collective-permute-start.80 = (bf16[2048,384]{1,0:T(8,128)(2,1)}, bf16[2048,384]{1,0:T(8,128)(2,1)}, u32[]{:S(2)}, u32[]{:S(2)}) collective-permute-start(bf16[2048,384]{1,0:T(8,128)(2,1)} %get-tuple-element.510), channel_id=1, source_target_pairs={{0,1},{1,0},{2,3},{3,2},{4,5},{5,4},{6,7},{7,6},{8,9},{9,8},{10,11... | collective-permute-start | bytes 4718600 | tf_op jit(solution)/shard_map/ppermute | solution.py:1245
  1333.2 169.6 %reduce-scatter.20.cloned.1.call-start = ((), (), s32[]{:S(2)}) async-start(), calls=%async_computation.18 | async-start | bytes 3686400 | tf_op jit(solution)/shard_map/reduce_scatter | solution.py:1236
  (224 other events, 4395.7 us)
Sparse Core Ops, SparseCore 0:
  98.6 84.9 all-gather.14
  218.2 44.3 all-gather.6
  310.7 65.5 all-gather.8
  377.8 67.4 all-gather.10
  446.7 67.4 all-gather.12
  733.8 75.1 reduce-scatter.7
  811.3 73.0 reduce-scatter.9
  886.7 73.0 reduce-scatter.11
  962.1 35.2 reduce-scatter.13
  1191.2 37.4 reduce-scatter.15
  1333.3 37.0 reduce-scatter.17
  1409.9 76.4 reduce-scatter.19

commit v3 on v2

--- a/solution.py
+++ b/solution.py
@@ -23,9 +23,10 @@
 PART = NH * HDIM
 GROUP = 3
 GPART = GROUP * HDIM
+QB_BACK = 512
 QB = 256
 KB = 1024
-KB_FWD = 512
+KB_FWD = 1024
 HEAD_STEP = 9
 NT = (((1,), (1,)), ((), ()))
 NN = (((1,), (0,)), ((), ()))
@@ -508,11 +509,11 @@
 
 
 def sort_kernel(order_ref, *refs):
-    k_ref, v_ref, kt_ref, vt_ref = refs[8:]
-    first = pl.program_id(0) * 4
-    for j in range(4):
+    k_ref, v_ref, kt_ref, vt_ref = refs[16:]
+    first = pl.program_id(0) * 8
+    for j in range(8):
         from_mine = order_ref[first + j] < 32
-        tile = jnp.where(from_mine, refs[j][0], refs[4 + j][0])
+        tile = jnp.where(from_mine, refs[j][0], refs[8 + j][0])
         rows = slice(j * BLK, (j + 1) * BLK)
         for h in range(NH):
             v_ref[h, rows, :] = tile[:, h * HDIM : (h + 1) * HDIM]
@@ -525,49 +526,51 @@
 def sort_keys(order, mine, theirs):
     count = order.shape[0]
     shape = (1, BLK, 2 * PART)
-    near = lambda j: pl.BlockSpec(shape, lambda i, o: (jnp.minimum(o[i * 4 + j], 31), 0, 0))
-    far = lambda j: pl.BlockSpec(shape, lambda i, o: (jnp.maximum(o[i * 4 + j] - 32, 0), 0, 0))
+    near = lambda j: pl.BlockSpec(shape, lambda i, o: (jnp.minimum(o[i * 8 + j], 31), 0, 0))
+    far = lambda j: pl.BlockSpec(shape, lambda i, o: (jnp.maximum(o[i * 8 + j] - 32, 0), 0, 0))
     return pl.pallas_call(
         sort_kernel,
         out_shape=[jax.ShapeDtypeStruct((NH, count * BLK, HDIM), BF)] * 2
         + [jax.ShapeDtypeStruct((NH, HDIM, count * BLK), BF)] * 2,
         grid_spec=pltpu.PrefetchScalarGridSpec(
             num_scalar_prefetch=1,
-            grid=(count // 4,),
-            in_specs=[near(j) for j in range(4)] + [far(j) for j in range(4)],
-            out_specs=[pl.BlockSpec((NH, 4 * BLK, HDIM), lambda i, o: (0, i, 0))] * 2
-            + [pl.BlockSpec((NH, HDIM, 4 * BLK), lambda i, o: (0, 0, i))] * 2,
+            grid=(count // 8,),
+            in_specs=[near(j) for j in range(8)] + [far(j) for j in range(8)],
+            out_specs=[pl.BlockSpec((NH, 8 * BLK, HDIM), lambda i, o: (0, i, 0))] * 2
+            + [pl.BlockSpec((NH, HDIM, 8 * BLK), lambda i, o: (0, 0, i))] * 2,
         ),
         compiler_params=room(),
         cost_estimate=cost(0, 64 * count * BLK * PART),
         name="sort_keys",
-    )(order, *([mine.reshape(32, BLK, 2 * PART)] * 4), *([theirs.reshape(32, BLK, 2 * PART)] * 4))
+    )(order, *([mine.reshape(32, BLK, 2 * PART)] * 8), *([theirs.reshape(32, BLK, 2 * PART)] * 8))
 
 
 def lane_tile(vals):
-    lane = lax.broadcasted_iota(jnp.int32, (1, QB), 1)
-    out = jnp.full((1, QB), vals[3], jnp.int32)
-    for j in (2, 1, 0):
+    shape = (1, len(vals) * BLK)
+    lane = lax.broadcasted_iota(jnp.int32, shape, 1)
+    out = jnp.full(shape, vals[-1], jnp.int32)
+    for j in range(len(vals) - 2, -1, -1):
         out = jnp.where(lane < (j + 1) * BLK, vals[j], out)
     return out, lane & (BLK - 1)
 
 
-def block_facts(tiles_ref, len_ref, block, step):
+def block_facts(tiles_ref, len_ref, block, step, size):
     half_tiles = PLEN // BLK
-    t = [tiles_ref[block * 4 + j] for j in range(4)]
+    count = size // BLK
+    t = [tiles_ref[block * count + j] for j in range(count)]
     tile, within = lane_tile(t)
     qpos = tile * BLK + within
-    tmax = jnp.maximum(jnp.maximum(t[0], t[1]), jnp.maximum(t[2], t[3]))
-    tmin = jnp.minimum(jnp.minimum(t[0], t[1]), jnp.minimum(t[2], t[3]))
+    tmax = functools.reduce(jnp.maximum, t)
+    tmin = functools.reduce(jnp.minimum, t)
     per = step // BLK
     is_cont = t[0] >= half_tiles
     n_all = jnp.where(is_cont, PLEN // step, tmax // per + 1)
     n_free = jnp.where(is_cont, PLEN // step, tmin // per)
-    conts = [jnp.maximum(t[j] - half_tiles, 0) // 4 for j in range(4)]
-    lens = lane_tile([len_ref[conts[j]] for j in range(4)])[0]
+    conts = [jnp.maximum(v - half_tiles, 0) // 4 for v in t]
+    lens = lane_tile([len_ref[v] for v in conts])[0]
     qin = qpos - PLEN - lane_tile(conts)[0] * CLEN
-    starts = [pl.multiple_of(PLEN + conts[j] * CLEN, CLEN) for j in range(4)]
-    kin = lax.broadcasted_iota(jnp.int32, (CLEN, QB), 0)
+    starts = [pl.multiple_of(PLEN + v * CLEN, CLEN) for v in conts]
+    kin = lax.broadcasted_iota(jnp.int32, (CLEN, size), 0)
     seen = lambda: (kin <= qin) & (kin < lens)
     return qpos, is_cont, n_all, n_free, starts, seen
 
@@ -576,7 +579,9 @@
     tiles_ref, len_ref, q_ref, k_ref, vt_sc, o_ref, lse_ref, mx_ref, ot_sc, shift
 ):
     block = pl.program_id(0) + shift
-    qpos, is_cont, n_all, n_free, starts, seen = block_facts(tiles_ref, len_ref, block, KB_FWD)
+    qpos, is_cont, n_all, n_free, starts, seen = block_facts(
+        tiles_ref, len_ref, block, KB_FWD, QB
+    )
 
     def heads(group, carry):
         hs = [group * HEAD_STEP + j for j in range(HEAD_STEP)]
@@ -684,19 +689,27 @@
 
 
 def delta_kernel(*refs):
-    w_ref, o_ref, gh_ref, delta_ref, x_sc = refs[10:]
-    fetch_rows(refs[:10], x_sc)
-    grad = mul(x_sc[...], w_ref[...], NT).astype(BF)
+    w_ref, o_ref, gh_ref, delta_ref, gw_ref, x_sc = refs[10:]
+    step = pl.program_id(0)
+    rows = pl.ds(pl.multiple_of(step * QB, QB), QB)
+    fetch_rows(refs[:10], x_sc.at[rows, :])
+    grad = mul(x_sc[rows, :], w_ref[...], NT).astype(BF)
     for h in range(NH):
         gh_ref[h] = grad[:, h * HDIM : (h + 1) * HDIM]
-    prod = grad.astype(F32) * o_ref[...].astype(F32)
+    prod = grad.astype(F32) * o_ref[rows, :].astype(F32)
+    high = prod.astype(BF)
+    low = (prod - high.astype(F32)).astype(BF)
     row = lax.broadcasted_iota(jnp.int32, (16, PART), 0)
     col = lax.broadcasted_iota(jnp.int32, (16, PART), 1)
-    pick = jnp.where(col // HDIM == row, 1.0, 0.0)
-    total = lax.dot_general(
-        pick, prod, NT, preferred_element_type=F32, precision=lax.Precision.HIGHEST
-    )
+    pick_head = jnp.where(col // HDIM == row, 1.0, 0.0).astype(BF)
+    total = mul(pick_head, high, NT) + mul(pick_head, low, NT)
     delta_ref[0] = total[:NH]
+
+    @pl.when(step == pl.num_programs(0) - 1)
+    def _():
+        for k in range(3):
+            cols = slice(k * 768, (k + 1) * 768)
+            gw_ref[:, cols] = mul(o_ref[...], x_sc[:, cols], TN).astype(BF)
 
 
 def attention_delta(grad_branch, w_out, attended):
@@ -707,15 +720,17 @@
         out_shape=[
             jax.ShapeDtypeStruct((NH, rows, HDIM), BF),
             jax.ShapeDtypeStruct((count, NH, QB), F32),
+            jax.ShapeDtypeStruct((PART, width), BF),
         ],
         grid=(count,),
         in_specs=[whole(v.shape) for v in grad_branch]
-        + [whole((PART, width)), pl.BlockSpec((QB, PART), lambda i: (i, 0))],
+        + [whole((PART, width)), whole((rows, PART))],
         out_specs=[
             pl.BlockSpec((NH, QB, HDIM), lambda i: (0, i, 0)),
             pl.BlockSpec((1, NH, QB), lambda i: (i, 0, 0)),
+            pl.BlockSpec((PART, width), lambda i: (0, 0)),
         ],
-        scratch_shapes=[pltpu.VMEM((QB, width), BF)],
+        scratch_shapes=[pltpu.VMEM((rows, width), BF)],
         compiler_params=room(),
         cost_estimate=cost(2 * rows * width * PART, 2 * rows * width),
         name="attention_delta",
@@ -734,11 +749,16 @@
         dk_ref[...] = jnp.zeros_like(dk_ref)
         dv_ref[...] = jnp.zeros_like(dv_ref)
 
-    qpos, is_cont, n_all, n_free, starts, seen = block_facts(tiles_ref, len_ref, block, KB)
+    qpos, is_cont, n_all, n_free, starts, seen = block_facts(
+        tiles_ref, len_ref, block, KB, QB_BACK
+    )
     q = q_ref[0]
     g = g_ref[0]
-    lse = lse_ref[0, pl.ds(h, 1), :]
-    delta = delta_ref[0, pl.ds(h, 1), :]
+    stat = lambda ref: jnp.concatenate(
+        [ref[j, pl.ds(h, 1), :] for j in range(QB_BACK // QB)], axis=1
+    )
+    lse = stat(lse_ref)
+    delta = stat(delta_ref)
 
     def step(kb, dqt, masked):
         base = pl.multiple_of(kb * KB, KB)
@@ -746,7 +766,7 @@
         s = mul(k_ref[0, rows, :], q, NT)
         dp = mul(v_ref[0, rows, :], g, NT)
         if masked:
-            kpos = base + lax.broadcasted_iota(jnp.int32, (KB, QB), 0)
+            kpos = base + lax.broadcasted_iota(jnp.int32, (KB, QB_BACK), 0)
             s = jnp.where(kpos <= qpos, s, masked_value)
         p = jnp.exp(s - lse)
         ds = (p * (dp - delta)).astype(BF)
@@ -754,7 +774,7 @@
         dk_ref[rows, :] += mul(ds, q)
         return dqt + mul(kt_ref[0, :, rows], ds)
 
-    dqt = jnp.zeros((HDIM, QB), F32)
+    dqt = jnp.zeros((HDIM, QB_BACK), F32)
     dqt = lax.fori_loop(0, n_free, functools.partial(step, masked=False), dqt)
     dqt = lax.fori_loop(n_free, n_all, functools.partial(step, masked=True), dqt)
     dq_ref[0] = dqt.T * HDIM ** (-0.5)
@@ -762,15 +782,15 @@
     @pl.when(is_cont)
     def _():
         part = lambda x, j: x[j * BLK : (j + 1) * BLK]
-        rows = [pl.ds(starts[j], CLEN) for j in range(4)]
-        s = jnp.concatenate([mul(k_ref[0, rows[j], :], part(q, j), NT) for j in range(4)], axis=1)
+        rows = [pl.ds(starts[j], CLEN) for j in range(QB_BACK // BLK)]
+        s = jnp.concatenate([mul(k_ref[0, rows[j], :], part(q, j), NT) for j in range(QB_BACK // BLK)], axis=1)
         s = jnp.where(seen(), s, masked_value)
         p = jnp.exp(s - lse)
-        dp = jnp.concatenate([mul(v_ref[0, rows[j], :], part(g, j), NT) for j in range(4)], axis=1)
+        dp = jnp.concatenate([mul(v_ref[0, rows[j], :], part(g, j), NT) for j in range(QB_BACK // BLK)], axis=1)
         ds = (p * (dp - delta)).astype(BF)
         pb = p.astype(BF)
         dq = []
-        for j in range(4):
+        for j in range(QB_BACK // BLK):
             cols = slice(j * BLK, (j + 1) * BLK)
             dv_ref[rows[j], :] += mul(pb[:, cols], part(g, j))
             dk_ref[rows[j], :] += mul(ds[:, cols], part(q, j))
@@ -785,11 +805,11 @@
 
 def attention_backward(tiles, lengths, queries, grads, log_total, row_delta, keys, values, keys_t, group):
     rows = queries.shape[1]
-    count = rows // QB
+    count = rows // QB_BACK
     span = keys.shape[1]
     first = group * GROUP
-    row = pl.BlockSpec((1, QB, HDIM), lambda h, i, a, b: (h + first, i, 0))
-    stat = pl.BlockSpec((1, NH, QB), lambda h, i, a, b: (i, 0, 0))
+    row = pl.BlockSpec((1, QB_BACK, HDIM), lambda h, i, a, b: (h + first, i, 0))
+    stat = pl.BlockSpec((QB_BACK // QB, NH, QB), lambda h, i, a, b: (i, 0, 0))
     full = pl.BlockSpec((1, span, HDIM), lambda h, i, a, b: (h + first, 0, 0))
     out = pl.BlockSpec((1, span, HDIM), lambda h, i, a, b: (h, 0, 0))
     return pl.pallas_call(
@@ -811,7 +831,7 @@
                 full,
                 pl.BlockSpec((1, HDIM, span), lambda h, i, a, b: (h + first, 0, 0)),
             ],
-            out_specs=[pl.BlockSpec((1, QB, HDIM), lambda h, i, a, b: (h, i, 0)), out, out],
+            out_specs=[pl.BlockSpec((1, QB_BACK, HDIM), lambda h, i, a, b: (h, i, 0)), out, out],
             scratch_shapes=[pltpu.VMEM((span, HDIM), F32)] * 2,
         ),
         compiler_params=room(),
@@ -821,44 +841,44 @@
 
 
 def restore_kernel(tiles_ref, *refs):
-    mine_ref, theirs_ref = refs[8:]
+    mine_ref, theirs_ref = refs[16:]
 
     def write(out_ref):
-        for j in range(4):
+        for j in range(8):
             rows = slice(j * BLK, (j + 1) * BLK)
             for h in range(GROUP):
                 cols = slice(h * HDIM, (h + 1) * HDIM)
-                out_ref[rows, cols] = refs[4 + j][h]
+                out_ref[rows, cols] = refs[8 + j][h]
                 out_ref[rows, GPART + h * HDIM : GPART + (h + 1) * HDIM] = refs[j][h]
 
-    @pl.when(pl.program_id(0) < 8)
+    @pl.when(pl.program_id(0) < 4)
     def _():
         write(theirs_ref)
 
-    @pl.when(pl.program_id(0) >= 8)
+    @pl.when(pl.program_id(0) >= 4)
     def _():
         write(mine_ref)
 
 
 def restore_keys(tiles, grad_k, grad_v):
-    spec = lambda j: pl.BlockSpec((GROUP, BLK, HDIM), lambda i, o: (0, o[i * 4 + j], 0))
-    shape = (4 * BLK, 2 * GPART)
+    spec = lambda j: pl.BlockSpec((GROUP, BLK, HDIM), lambda i, o: (0, o[i * 8 + j], 0))
+    shape = (8 * BLK, 2 * GPART)
     return pl.pallas_call(
         restore_kernel,
         out_shape=[jax.ShapeDtypeStruct((32 * BLK, 2 * GPART), BF)] * 2,
         grid_spec=pltpu.PrefetchScalarGridSpec(
             num_scalar_prefetch=1,
-            grid=(16,),
-            in_specs=[spec(j) for j in range(4)] * 2,
+            grid=(8,),
+            in_specs=[spec(j) for j in range(8)] * 2,
             out_specs=[
-                pl.BlockSpec(shape, lambda i, o: (jnp.maximum(i - 8, 0), 0)),
-                pl.BlockSpec(shape, lambda i, o: (jnp.minimum(i, 7), 0)),
+                pl.BlockSpec(shape, lambda i, o: (jnp.maximum(i - 4, 0), 0)),
+                pl.BlockSpec(shape, lambda i, o: (jnp.minimum(i, 3), 0)),
             ],
         ),
         compiler_params=room(),
         cost_estimate=cost(0, 64 * 64 * BLK * GPART),
         name="restore_keys",
-    )(tiles, *([grad_k] * 4), *([grad_v] * 4))
+    )(tiles, *([grad_k] * 8), *([grad_v] * 8))
 
 
 def unturn_kernel(dq_ref, mine_ref, theirs_ref, cos_ref, sin_ref, g_ref, y_sc):
@@ -875,7 +895,7 @@
 
 def unturn(grad_q, mine, theirs, cosine, sine_vals):
     rows = mine.shape[0]
-    size = 2 * QB
+    size = QB
     row = lambda n: pl.BlockSpec((size, n), lambda i: (i, 0))
     return pl.pallas_call(
         unturn_kernel,
@@ -888,7 +908,7 @@
             row(128),
             row(128),
         ],
-        out_specs=row(3 * GPART),
+        out_specs=pl.BlockSpec((size, 3 * GPART), lambda i: (i % 4 * 2 + i // 4, 0)),
         scratch_shapes=[pltpu.VMEM((size, 2 * GPART), F32)],
         compiler_params=room(),
         cost_estimate=cost(0, 20 * rows * GPART),
@@ -913,14 +933,13 @@
 
 def unproject(parts, w_all, chunk):
     rows = parts[0].shape[0] // 2
-    shift = chunk * (rows // QB)
     full = w_all.shape
     width = full[0] * full[1] * (full[2] - 8)
     return pl.pallas_call(
         unproject_kernel,
         out_shape=jax.ShapeDtypeStruct((rows, width), BF),
         grid=(rows // QB,),
-        in_specs=[pl.BlockSpec((QB, 3 * GPART), lambda i: (i + shift, 0))] * 3
+        in_specs=[pl.BlockSpec((QB, 3 * GPART), lambda i: (i * 2 + chunk, 0))] * 3
         + [pl.BlockSpec(full, lambda i: (0, 0, 0, 0), pipeline_mode=pl.Buffered(1))],
         out_specs=pl.BlockSpec((QB, width), lambda i: (i, 0)),
         scratch_shapes=[
@@ -931,6 +950,32 @@
         cost_estimate=cost(2 * rows * width * 3 * PART, 4 * rows * width),
         name="unproject",
     )(*parts, w_all)
+
+
+def finish_kernel(a_ref, bc_ref, wq_ref, wk_ref, wv_ref, gain_ref, q_ref, k_ref, v_ref, sum_ref):
+    thin = gain_ref.shape[0]
+    gain = gain_ref[...]
+    total = jnp.zeros((thin, 1), F32)
+    for p in range(4):
+        for g, (ref, first) in enumerate(((a_ref, 0), (bc_ref, 0), (bc_ref, PART))):
+            cols = slice(p * PART + g * GPART, p * PART + (g + 1) * GPART)
+            for n, (w, out) in enumerate(((wq_ref, q_ref), (wk_ref, k_ref), (wv_ref, v_ref))):
+                part = slice(first + n * GPART, first + (n + 1) * GPART)
+                grad = ref[p, :thin, part].astype(F32)
+                out[:, cols] = grad * gain
+                total += jnp.sum(grad * w[:, cols].astype(F32), axis=1, keepdims=True)
+    sum_ref[...] = jnp.broadcast_to(total, sum_ref.shape)
+
+
+def finish(parts, weights, gain):
+    thin, width = weights[0].shape
+    return pl.pallas_call(
+        finish_kernel,
+        out_shape=[jax.ShapeDtypeStruct((thin, width), F32)] * 3
+        + [jax.ShapeDtypeStruct((thin, 128), F32)],
+        compiler_params=room(),
+        name="finish",
+    )(*parts, *weights, gain)
 
 
 def split_tiles(rows):
@@ -1121,7 +1166,7 @@
         project(pieces, w_qkv, cosine, sine_vals),
         cross(parts_of(quarters(grad_out))),
     )
-    normed = joined(in_chunks(pieces))
+    normed = joined(pieces)
     theirs = lax.ppermute(mine, "c", [(0, 1), (1, 0)])
     sorted_kv, grad_out, stacked = meet(
         sort_keys(order, mine, theirs), hop_on(grad_out), stacked
@@ -1208,12 +1253,11 @@
     grad_resid = [back_a[1], back_b[1]]
 
     grad_pieces, branch_ffn, grad_gate = meet(grad_pieces, branch_ffn, sum_rows(grad_gate))
-    (grad_heads, row_delta), far, grad_up = meet(
+    (grad_heads, row_delta, grad_w_part), far, grad_up = meet(
         attention_delta(grad_pieces, w_out, attended),
         scatter_far_both(branch_ffn),
         sum_rows(grad_up),
     )
-    grad_w_part = mul(attended, joined(grad_pieces), TN).astype(BF)
 
     far_order = jnp.concatenate([tiles_far, tiles])
     gain_rows = grad_gain_two.astype(BF).reshape(4, 8, 1, thin).transpose(1, 0, 2, 3)
@@ -1244,13 +1288,13 @@
         maxima = jnp.maximum(maxima, lax.ppermute(maxima, name, pairs))
     trade = lambda v: lax.ppermute(v, "c", [(0, 1), (1, 0)])
     grad_heads, grad_w_part = meet(grad_heads, grad_w_part)
-    part_a, grad_heads, near, grad_down, grad_w_output = meet(
+    part_a, grad_heads, near, grad_down = meet(
         back_group(0, grad_heads),
         grad_heads,
         scatter_near_both(branch_ffn, far),
         sum_rows(grad_down),
-        sum_rows(grad_w_part),
-    )
+    )
+    grad_w_output = sum_rows(grad_w_part)
     part_a = restore(part_a)
     states = (state_a, state_b)
     output = []
@@ -1262,13 +1306,12 @@
     ffn_grads = jnp.stack([grad_gate, grad_up, grad_down])
     ffn_grads = ffn_grads.reshape(3, share, 4, PART).transpose(2, 0, 1, 3)
     output, grad_heads, part_a, ffn_grads = meet(output, grad_heads, part_a, ffn_grads)
-    part_b, grad_heads, hops, far_a, maxima, ffn_grads = meet(
+    part_b, grad_heads, hops, far_a, grad_w_output = meet(
         back_group(1, grad_heads),
         grad_heads,
         hop_back(output),
         trade(part_a[2]),
-        maxima,
-        cross_whole(ffn_grads),
+        grad_w_output,
     )
     part_b = restore(part_b)
     grads_a = unturn(part_a[0], part_a[1], far_a, cosine, sine_vals)
@@ -1282,17 +1325,18 @@
     )
     part_c = restore(part_c)
     grads_b = unturn(part_b[0], part_b[1], far_b, cosine, sine_vals)
-    weights_b, far_c = meet(weight_part(grads_b), trade(part_c[2]))
+    weights_b, far_c, ffn_grads = meet(
+        weight_part(grads_b), trade(part_c[2]), cross_whole(ffn_grads)
+    )
     output = joined(output)
     weights_b = sum_line(weights_b)
     grads_c = unturn(part_c[0], part_c[1], far_c, cosine, sine_vals)
     grads = (grads_a, grads_b, grads_c)
-    rest_a, grads = meet(unproject(grads, w_qkv, 0), grads)
-    rest_b, far_a, grads_c = meet(unproject(grads, w_qkv, 1), scatter_far(rest_a), grads[2])
-    weights_c, near_a, far_b = meet(
-        weight_part(grads_c), scatter_near(rest_a, far_a), scatter_far(rest_b)
-    )
+    rest_a, grads, weights_a = meet(unproject(grads, w_qkv, 0), grads, cross_whole(weights_a))
+    weights_c, far_a, grads = meet(weight_part(grads[2]), scatter_far(rest_a), grads)
     weights_c = sum_line(weights_c)
+    rest_b, near_a = meet(unproject(grads, w_qkv, 1), scatter_near(rest_a, far_a))
+    far_b = scatter_far(rest_b)
 
     def first_back(k, total):
         grad_first = inverse_one[k] * total - residual[k] * inverse_one[k] ** 3 * jnp.mean(
@@ -1300,20 +1344,19 @@
         )
         return (grad_resid[k] + grad_first).astype(BF)
 
+    hop_a = hop_back(first_back(0, scatter_sum(rest_a, near_a)))
     near_b = scatter_near(rest_b, far_b)
-    hop_a, near_b = meet(hop_back(first_back(0, scatter_sum(rest_a, near_a))), near_b)
+    hop_a, near_b = meet(hop_a, near_b)
     hop_b, hop_a = meet(hop_back(first_back(1, scatter_sum(rest_b, near_b))), hop_out(hop_a))
     grad_input = join_tiles([jnp.stack(hop_a), jnp.stack(hop_out(hop_b))]).astype(F32)
     ffn_grads = ffn_grads.astype(F32)
     ffn_grads = jnp.concatenate([ffn_grads[k, :, :n] for k, n in enumerate(sizes)], axis=1)
-    proj = over("p", jnp.concatenate([weights_a, weights_b, weights_c], axis=2)).astype(F32)
-    grad_ffn_gain = jnp.sum(proj[:, thin, :thin], axis=0)
-    proj = proj[:, :thin].reshape(4, thin, 3, 3, GPART).transpose(3, 1, 0, 2, 4)
-    proj = proj.reshape(3, thin, width)
-    grad_attn_gain = sum(
-        jnp.sum(w.astype(F32) * proj[k], axis=1) for k, w in enumerate((w_query, w_key, w_value))
-    )
-    proj = proj * gain_f[None, :, None]
+    grad_ffn_gain = jnp.sum(weights_a[:, thin, :thin].astype(F32), axis=0)
+    weights_bc = over("p", jnp.concatenate([weights_b, weights_c], axis=2))
+    proj = finish(
+        (weights_a, weights_bc), (w_query, w_key, w_value), gain_f[:, None]
+    )
+    grad_attn_gain = proj[3][:, 0]
 
     limit_value = clip_threshold[0].astype(F32)
     clip_factor = jnp.sqrt(limit_value / jnp.maximum(maxima, limit_value))

time: 1580 us -> 1430 us (0.905)
  waiting for transfers between devices: 353 us -> 282 us
  local copies, waits for them, and re-layouts: 200 us -> 161 us
  starting transfers between devices: 147 us -> 125 us
    ppermute x39 -> x42, waiting for transfers between devices: 218 us -> 148 us  [swap_blocks(): lax.ppermute(pieces[r], name, [(k, k ^ r) for k in range(4)])]
    pallas_call x3, Pallas kernels: 172 us -> 155 us  [attention_backward(): pl.pallas_call(functools.partial(backward_kernel, first=first), out_shape...]
    unnamed x297 -> x249, local copies, waits for them, and re-layouts: 65 us -> 48.6 us
    dot_general x24 -> x23, matrix products: 269 us -> 257 us  [mul(): return lax.dot_general(left, right, dims, preferred_element_type=F32)]
    ppermute x39 -> x42, starting transfers between devices: 56.9 us -> 55.7 us  [swap_blocks(): lax.ppermute(pieces[r], name, [(k, k ^ r) for k in range(4)])]
  transfers between devices with their start and end apart: 115 -> 118, of which waited for: 42 -> 44; matrix products, arithmetic and copies ran while one was open for 34% -> 38% of each run, Pallas kernels for 23% -> 28%
where the time goes in v3:
time: 1430 us; the launch traced here: 1420 us
  Pallas kernels  409 us (29%)
  waiting for transfers between devices  282 us (20%)
  matrix products  257 us (18%)
  other arithmetic  163 us (11%)
  local copies, waits for them, and re-layouts  161 us (11%)
  starting transfers between devices  125 us (9%)
  between operations  17.1 us (1%)
    dot_general x23, matrix products, mul(): return lax.dot_general(left, right, dims, preferred_element_type=F32)  257 us
    pallas_call x3, Pallas kernels, attention_backward(): pl.pallas_call(functools.partial(backward_kernel, first=first), out_shape...  155 us
    ppermute x42, waiting for transfers between devices, swap_blocks(): lax.ppermute(pieces[r], name, [(k, k ^ r) for k in range(4)])  148 us
    ppermute x52, waiting for transfers between devices, flip(): return lax.ppermute(values, 'p', [(k, k ^ mask) for k in range(4)])  113 us
    pallas_call x3, Pallas kernels, attention_forward(): pl.pallas_call(functools.partial(forward_kernel, shift=shift), out_shape=...  92 us
    ppermute x52, starting transfers between devices, flip(): return lax.ppermute(values, 'p', [(k, k ^ mask) for k in range(4)])  57 us
    ppermute x42, starting transfers between devices, swap_blocks(): lax.ppermute(pieces[r], name, [(k, k ^ r) for k in range(4)])  55.7 us
    unnamed x249, local copies, waits for them, and re-layouts  48.6 us
  transfers between devices with their start and end apart: 118, of which 44 were waited for; matrix products, arithmetic and copies ran while one was open for 38% of the time, Pallas kernels for 28%

profile of v3, /device:TPU:8, one launch (start us, length us, event | category | flops | bytes accessed | tf_op | source)
XLA Modules:
  0.0 1416.0 jit_solution(2863732209287864557)
XLA Ops:
  27.2 12.7 collective-permute-done.3
  55.9 12.7 collective-permute-done.8
  68.6 19.7 %collective-permute-done.9 = bf16[128,2304]{1,0:T(8,128)(2,1)S(1)} collective-permute-done((bf16[128,2304]{1,0:T(8,128)(2,1)S(1)}, bf16[128,2304]{1,0:T(8,128)(2,1)S(1)}, u32[]{:S(2)}, u32[]{:S(2)}) %collective-permute-start.9) | collective-permute-done | bytes 589856 | tf_op jit(solution)/shard_map/ppermute | solution.py:1058
  114.6 40.5 %collective-permute-done.12.refs_2_ = bf16[512,2304]{1,0:T(8,128)(2,1)} collective-permute-done((bf16[512,2304]{1,0:T(8,128)(2,1)}, bf16[512,2304]{1,0:T(8,128)(2,1)}, u32[]{:S(2)}, u32[]{:S(2)}) %collective-permute-start.12) | collective-permute-done | bytes 2359328 | tf_op jit(solution)/shard_map/ppermute | solution.py:1004
  167.4 13.1 collective-permute-done.13.refs_3_
  190.3 27.7 %project.1 = (bf16[9,2048,64]{2,1,0:T(8,128)(2,1)}, bf16[2048,1152]{1,0:T(8,128)(2,1)}) custom-call(bf16[512,2304]{1,0:T(8,128)(2,1)} %pad_maximum_fusion.13.refs_0_, bf16[512,2304]{1,0:T(8,128)(2,1)} %collective-permute-done.11.refs_1_, bf16[512,2304]{1,0:T(8,128)(2,1)} %collective-permute-done.12.refs_2_, ...), custom_call_target="tpu_custom_call" | custom-call | flops 16307453952 | bytes 29196288 | tf_op jit(solution)/shard_map/project/pallas_call | solution.py:487
  268.6 19.9 %sort_keys.1 = (bf16[9,4096,64]{2,1,0:T(8,128)(2,1)}, bf16[9,4096,64]{2,1,0:T(8,128)(2,1)}, bf16[9,64,4096]{2,1,0:T(8,128)(2,1)}, bf16[9,64,4096]{2,1,0:T(8,128)(2,1)}) custom-call(s32[64]{0:T(128)} %select_reduce_fusion.order_ref, bf16[32,64,1152]{2,1,0:T(8,128)(2,1)} %bitcast.326, bf16[32,64,1152]{2,1,0:T(8,128)(2,1)} %bitcast.327, ...), custom_call_target="tpu_custom_call" | custom-call | bytes 150994944 | tf_op jit(solution)/shard_map/sort_keys/pallas_call | solution.py:531
  292.5 14.5 %collective-permute-done.21 = bf16[128,2304]{1,0:T(8,128)(2,1)} collective-permute-done((bf16[128,2304]{1,0:T(8,128)(2,1)}, bf16[128,2304]{1,0:T(8,128)(2,1)}, u32[]{:S(2)}, u32[]{:S(2)}) %collective-permute-start.21) | collective-permute-done | bytes 589856 | tf_op jit(solution)/shard_map/ppermute | solution.py:1058
  327.6 42.3 %attention_forward.3 = (bf16[1024,576]{1,0:T(8,128)(2,1)}, f32[4,9,256]{2,1,0:T(8,128)}, f32[4,9,256]{2,1,0:T(8,128)}) custom-call(s32[32]{0:T(128)} %copy-done.92, s32[8]{0:T(128)} %copy-done.105, bf16[9,2048,64]{2,1,0:T(8,128)(2,1)} %get-tuple-element.346.q_ref, bf16[9,4096,64]{2,1,0:T(8,128)(2,1)} %get-tuple-element.335.k_ref, ...), custom_call_target="tpu_custom_call" | custom-call | flops 24159191040 | bytes 37748736 | tf_op jit(solution)/shard_map/attention_forward/pallas_call | solution.py:667
  386.6 24.1 %attention_forward.5 = (bf16[512,576]{1,0:T(8,128)(2,1)}, f32[2,9,256]{2,1,0:T(8,128)}, f32[2,9,256]{2,1,0:T(8,128)}) custom-call(s32[32]{0:T(128)} %copy-done.92, s32[8]{0:T(128)} %copy-done.105, bf16[9,2048,64]{2,1,0:T(8,128)(2,1)} %get-tuple-element.346.q_ref, bf16[9,4096,64]{2,1,0:T(8,128)(2,1)} %get-tuple-element.335.k_ref, ...), custom_call_target="tpu_custom_call" | custom-call | flops 12079595520 | bytes 37748736 | tf_op jit(solution)/shard_map/attention_forward/pallas_call | solution.py:667
  423.2 25.6 %attention_forward.4 = (bf16[512,576]{1,0:T(8,128)(2,1)}, f32[2,9,256]{2,1,0:T(8,128)}, f32[2,9,256]{2,1,0:T(8,128)}) custom-call(s32[32]{0:T(128)} %copy-done.92, s32[8]{0:T(128)} %copy-done.105, bf16[9,2048,64]{2,1,0:T(8,128)(2,1)} %get-tuple-element.346.q_ref, bf16[9,4096,64]{2,1,0:T(8,128)(2,1)} %get-tuple-element.335.k_ref, ...), custom_call_target="tpu_custom_call" | custom-call | flops 12079595520 | bytes 37748736 | tf_op jit(solution)/shard_map/attention_forward/pallas_call | solution.py:667
  472.4 12.6 fusion.62
  606.0 12.5 fusion.72
  631.8 12.7 fusion.68
  672.8 13.1 fusion.70
  698.4 14.2 %fusion.71 = f32[1472,2304]{1,0:T(8,128)} fusion(bf16[1024,1472]{0,1:T(8,128)(2,1)S(1)} %copy-done.40, bf16[1024,2304]{1,0:T(8,128)(2,1)} %copy-done.73), kind=kOutput, calls=%fused_computation.350 | convolution fusion | flops 6945767424 | bytes 21299200 | tf_op jit(solution)/shard_map/dot_general | solution.py:409
  736.7 12.7 fusion.74
  805.8 12.6 convolution_convert_fusion.3
  889.7 27.1 %attention_delta.1 = (bf16[9,2048,64]{2,1,0:T(8,128)(2,1)}, f32[8,9,256]{2,1,0:T(8,128)}, bf16[576,2304]{1,0:T(8,128)(2,1)}) custom-call(bf16[256,2304]{1,0:T(8,128)(2,1)} %get-tuple-element.445.refs_0_, bf16[256,2304]{1,0:T(8,128)(2,1)} %collective-permute-done.49.refs_1_, bf16[256,2304]{1,0:T(8,128)(2,1)} %collective-permute-done.50.refs_2_, ...), custom_call_target="tpu_custom_call" | custom-call | flops 5435817984 | bytes 9437184 | tf_op jit(solution)/shard_map/attention_delta/pallas_call | solution.py:718
  929.2 51.7 %attention_backward.3 = (f32[3,2048,64]{2,1,0:T(8,128)}, bf16[3,4096,64]{2,1,0:T(8,128)(2,1)}, bf16[3,4096,64]{2,1,0:T(8,128)(2,1)}) custom-call(s32[32]{0:T(128)} %copy-done.92, s32[8]{0:T(128)} %copy-done.105, bf16[9,2048,64]{2,1,0:T(8,128)(2,1)} %get-tuple-element.346.q_ref, bf16[9,2048,64]{2,1,0:T(8,128)(2,1)} %get-tuple-element.506.g_ref, ...), custom_call_target="tpu_custom_call" | custom-call | flops 32212254720 | bytes 25165824 | tf_op jit(solution)/shard_map/attention_backward/pallas_call | solution.py:815
  1005.4 51.6 %attention_backward.4 = (f32[3,2048,64]{2,1,0:T(8,128)}, bf16[3,4096,64]{2,1,0:T(8,128)(2,1)}, bf16[3,4096,64]{2,1,0:T(8,128)(2,1)}) custom-call(s32[32]{0:T(128)} %copy-done.92, s32[8]{0:T(128)} %copy-done.105, bf16[9,2048,64]{2,1,0:T(8,128)(2,1)} %get-tuple-element.346.q_ref, bf16[9,2048,64]{2,1,0:T(8,128)(2,1)} %get-tuple-element.506.g_ref, ...), custom_call_target="tpu_custom_call" | custom-call | flops 32212254720 | bytes 25165824 | tf_op jit(solution)/shard_map/attention_backward/pallas_call | solution.py:815
  1105.8 51.8 %attention_backward.5 = (f32[3,2048,64]{2,1,0:T(8,128)}, bf16[3,4096,64]{2,1,0:T(8,128)(2,1)}, bf16[3,4096,64]{2,1,0:T(8,128)(2,1)}) custom-call(s32[32]{0:T(128)} %copy-done.92, s32[8]{0:T(128)} %copy-done.105, bf16[9,2048,64]{2,1,0:T(8,128)(2,1)} %get-tuple-element.346.q_ref, bf16[9,2048,64]{2,1,0:T(8,128)(2,1)} %get-tuple-element.506.g_ref, ...), custom_call_target="tpu_custom_call" | custom-call | flops 32212254720 | bytes 25165824 | tf_op jit(solution)/shard_map/attention_backward/pallas_call | solution.py:815
  1211.8 15.3 %unproject.2 = bf16[1024,2304]{1,0:T(8,128)(2,1)} custom-call(bf16[2048,576]{1,0:T(8,128)(2,1)} %unturn.3.a_ref, bf16[2048,576]{1,0:T(8,128)(2,1)} %unturn.4.b_ref, bf16[2048,576]{1,0:T(8,128)(2,1)} %unturn.5.c_ref, bf16[8,4,80,1728]{3,2,1,0:T(8,128)(2,1)} %bitcast.408), custom_call_target="tpu_custom_call" | custom-call | flops 8153726976 | bytes 9437184 | tf_op jit(solution)/shard_map/unproject/pallas_call | solution.py:938
  1263.4 15.5 %unproject.3 = bf16[1024,2304]{1,0:T(8,128)(2,1)} custom-call(bf16[2048,576]{1,0:T(8,128)(2,1)} %unturn.3.a_ref, bf16[2048,576]{1,0:T(8,128)(2,1)} %unturn.4.b_ref, bf16[2048,576]{1,0:T(8,128)(2,1)} %unturn.5.c_ref, bf16[8,4,80,1728]{3,2,1,0:T(8,128)(2,1)} %bitcast.409), custom_call_target="tpu_custom_call" | custom-call | flops 8153726976 | bytes 9437184 | tf_op jit(solution)/shard_map/unproject/pallas_call | solution.py:938
  (749 shorter events, 842.6 us)
Async XLA Ops:
  7.2 176.5 %all-gather.15.cloned.1.call-start = ((), (), s32[]{:S(2)}) async-start(), calls=%async_computation.19 | async-start | bytes 10321920 | tf_op jit(solution)/shard_map/all_gather | solution.py:1129
  99.3 272.1 %all-gather.7.cloned.1.call-start = ((), (), s32[]{:S(2)}) async-start(), calls=%async_computation.8 | async-start | bytes 2985984 | tf_op jit(solution)/shard_map/all_gather | solution.py:1131
  218.1 254.3 %all-gather.9.cloned.1.call-start = ((), (), s32[]{:S(2)}) async-start(), calls=%async_computation.9 | async-start | bytes 7630848 | tf_op jit(solution)/shard_map/all_gather | solution.py:1176
  310.4 219.8 %all-gather.11.cloned.1.call-start = ((), (), s32[]{:S(2)}) async-start(), calls=%async_computation.10 | async-start | bytes 7630848 | tf_op jit(solution)/shard_map/all_gather | solution.py:1176
  313.6 229.0 %all-gather.13.cloned.1.call-start = ((), (), s32[]{:S(2)}) async-start(), calls=%async_computation.11 | async-start | bytes 7630848 | tf_op jit(solution)/shard_map/all_gather | solution.py:1176
  384.1 64.7 %collective-permute-start.31 = (bf16[256,2304]{1,0:T(8,128)(2,1)}, bf16[256,2304]{1,0:T(8,128)(2,1)}, u32[]{:S(2)}, u32[]{:S(2)}) collective-permute-start(bf16[256,2304]{1,0:T(8,128)(2,1)} %slice.503), channel_id=1, source_target_pairs={{0,8},{8,0},{16,24},{24,16},{1,9},{9,1},{17,25},{25,17},{2,10},{10... | collective-permute-start | bytes 3538952 | tf_op jit(solution)/shard_map/ppermute | solution.py:1004
  385.7 63.1 %collective-permute-start.32 = (bf16[256,2304]{1,0:T(8,128)(2,1)}, bf16[256,2304]{1,0:T(8,128)(2,1)}, u32[]{:S(2)}, u32[]{:S(2)}) collective-permute-start(bf16[256,2304]{1,0:T(8,128)(2,1)} %slice.504), channel_id=1, source_target_pairs={{0,16},{8,24},{16,0},{24,8},{1,17},{9,25},{17,1},{25,9},{2,18},{10... | collective-permute-start | bytes 3538952 | tf_op jit(solution)/shard_map/ppermute | solution.py:1004
  423.2 439.9 %reduce-scatter.8.cloned.1.call-start = ((), (), s32[]{:S(2)}) async-start(), calls=%async_computation.12 | async-start | bytes 7630848 | tf_op jit(solution)/shard_map/reduce_scatter | solution.py:1250
  736.6 180.3 %reduce-scatter.10.cloned.1.call-start = ((), (), s32[]{:S(2)}) async-start(), calls=%async_computation.13 | async-start | bytes 7630848 | tf_op jit(solution)/shard_map/reduce_scatter | solution.py:1250
  782.4 198.5 %reduce-scatter.12.cloned.1.call-start = ((), (), s32[]{:S(2)}) async-start(), calls=%async_computation.14 | async-start | bytes 7630848 | tf_op jit(solution)/shard_map/reduce_scatter | solution.py:1250
  819.4 239.4 %reduce-scatter.14.cloned.1.call-start = ((), (), s32[]{:S(2)}) async-start(), calls=%async_computation.15 | async-start | bytes 2985984 | tf_op jit(solution)/shard_map/reduce_scatter | solution.py:1250
  920.4 60.5 %collective-permute-start.63 = (bf16[512,2304]{1,0:T(8,128)(2,1)}, bf16[512,2304]{1,0:T(8,128)(2,1)}, u32[]{:S(2)}, u32[]{:S(2)}) collective-permute-start(bf16[512,2304]{1,0:T(8,128)(2,1)} %pad_maximum_fusion.18), channel_id=1, source_target_pairs={{0,8},{8,0},{16,24},{24,16},{1,9},{9,1},{17,25},{25,17},{2,10},{10... | collective-permute-start | bytes 7077896 | tf_op jit(solution)/shard_map/ppermute | solution.py:1004
  924.6 56.4 %collective-permute-start.64 = (bf16[512,2304]{1,0:T(8,128)(2,1)}, bf16[512,2304]{1,0:T(8,128)(2,1)}, u32[]{:S(2)}, u32[]{:S(2)}) collective-permute-start(bf16[512,2304]{1,0:T(8,128)(2,1)} %pad_maximum_fusion.19), channel_id=1, source_target_pairs={{0,16},{8,24},{16,0},{24,8},{1,17},{9,25},{17,1},{25,9},{2,18},{10... | collective-permute-start | bytes 7077896 | tf_op jit(solution)/shard_map/ppermute | solution.py:1004
  929.2 230.9 %reduce-scatter.16.cloned.1.call-start = ((), (), s32[]{:S(2)}) async-start(), calls=%async_computation.16 | async-start | bytes 3686400 | tf_op jit(solution)/shard_map/reduce_scatter | solution.py:1280
  998.3 58.7 %collective-permute-start.65 = (bf16[128,2304]{1,0:T(8,128)(2,1)S(1)}, bf16[128,2304]{1,0:T(8,128)(2,1)S(1)}, u32[]{:S(2)}, u32[]{:S(2)}) collective-permute-start(bf16[128,2304]{1,0:T(8,128)(2,1)S(1)} %get-tuple-element.733), channel_id=1, source_target_pairs={{0,2},{2,0},{4,6},{6,4},{1,3},{3,1},{5,7},{7,5},{8,10},{10,8},{12,... | collective-permute-start | bytes 1769480 | tf_op jit(solution)/shard_map/ppermute | solution.py:1058
  1000.4 57.8 %collective-permute-start.66 = (bf16[128,2304]{1,0:T(8,128)(2,1)S(1)}, bf16[128,2304]{1,0:T(8,128)(2,1)S(1)}, u32[]{:S(2)}, u32[]{:S(2)}) collective-permute-start(bf16[128,2304]{1,0:T(8,128)(2,1)S(1)} %get-tuple-element.732), channel_id=1, source_target_pairs={{0,4},{2,6},{4,0},{6,2},{1,5},{3,7},{5,1},{7,3},{8,12},{10,14},{12... | collective-permute-start | bytes 1769480 | tf_op jit(solution)/shard_map/ppermute | solution.py:1058
  1000.4 58.4 %collective-permute-start.67 = (bf16[128,2304]{1,0:T(8,128)(2,1)S(1)}, bf16[128,2304]{1,0:T(8,128)(2,1)}, u32[]{:S(2)}, u32[]{:S(2)}) collective-permute-start(bf16[128,2304]{1,0:T(8,128)(2,1)S(1)} %get-tuple-element.731), channel_id=1, source_target_pairs={{0,6},{2,4},{4,2},{6,0},{1,7},{3,5},{5,3},{7,1},{8,14},{10,12},{12... | collective-permute-start | bytes 1769480 | tf_op jit(solution)/shard_map/ppermute | solution.py:1058
  1001.9 56.8 %collective-permute-start.68 = (bf16[2048,384]{1,0:T(8,128)(2,1)S(1)}, bf16[2048,384]{1,0:T(8,128)(2,1)S(1)}, u32[]{:S(2)}, u32[]{:S(2)}) collective-permute-start(bf16[2048,384]{1,0:T(8,128)(2,1)S(1)} %copy-done.100), channel_id=1, source_target_pairs={{0,1},{1,0},{2,3},{3,2},{4,5},{5,4},{6,7},{7,6},{8,9},{9,8},{10,11... | collective-permute-start | bytes 4718600 | tf_op jit(solution)/shard_map/ppermute | solution.py:1289
  1003.6 92.6 %collective-permute-start.76 = (bf16[3,184,576]{2,1,0:T(8,128)(2,1)}, bf16[3,184,576]{2,1,0:T(8,128)(2,1)}, u32[]{:S(2)}, u32[]{:S(2)}) collective-permute-start(bf16[3,184,576]{2,1,0:T(8,128)(2,1)} %get-tuple-element.705), channel_id=1, source_target_pairs={{0,24},{8,16},{16,8},{24,0},{1,25},{9,17},{17,9},{25,1},{2,26},{10... | collective-permute-start | bytes 1907720 | tf_op jit(solution)/shard_map/ppermute | solution.py:1058
  1094.0 290.2 %reduce-scatter.18.cloned.1.call-start = ((), (), s32[]{:S(2)}) async-start(), calls=%async_computation.17 | async-start | bytes 3686400 | tf_op jit(solution)/shard_map/reduce_scatter | solution.py:1280
  1102.3 56.2 %collective-permute-start.71 = (bf16[128,2304]{1,0:T(8,128)(2,1)S(1)}, bf16[128,2304]{1,0:T(8,128)(2,1)S(1)}, u32[]{:S(2)}, u32[]{:S(2)}) collective-permute-start(bf16[128,2304]{1,0:T(8,128)(2,1)S(1)} %get-tuple-element.728), channel_id=1, source_target_pairs={{0,24},{8,16},{16,8},{24,0},{1,25},{9,17},{17,9},{25,1},{2,26},{10... | collective-permute-start | bytes 1769480 | tf_op jit(solution)/shard_map/ppermute | solution.py:1058
  1104.1 54.4 %collective-permute-start.70 = (bf16[128,2304]{1,0:T(8,128)(2,1)S(1)}, bf16[128,2304]{1,0:T(8,128)(2,1)S(1)}, u32[]{:S(2)}, u32[]{:S(2)}) collective-permute-start(bf16[128,2304]{1,0:T(8,128)(2,1)S(1)} %get-tuple-element.729), channel_id=1, source_target_pairs={{0,16},{8,24},{16,0},{24,8},{1,17},{9,25},{17,1},{25,9},{2,18},{10... | collective-permute-start | bytes 1769480 | tf_op jit(solution)/shard_map/ppermute | solution.py:1058
  1105.8 54.2 %collective-permute-start.72 = (bf16[2048,384]{1,0:T(8,128)(2,1)}, bf16[2048,384]{1,0:T(8,128)(2,1)S(1)}, u32[]{:S(2)}, u32[]{:S(2)}) collective-permute-start(bf16[2048,384]{1,0:T(8,128)(2,1)} %get-tuple-element.514), channel_id=1, source_target_pairs={{0,1},{1,0},{2,3},{3,2},{4,5},{5,4},{6,7},{7,6},{8,9},{9,8},{10,11... | collective-permute-start | bytes 4718600 | tf_op jit(solution)/shard_map/ppermute | solution.py:1289
  1203.3 180.9 %reduce-scatter.20.cloned.1.call-start = ((), (), s32[]{:S(2)}) async-start(), calls=%async_computation.18 | async-start | bytes 3686400 | tf_op jit(solution)/shard_map/reduce_scatter | solution.py:1280
  (210 other events, 3788.7 us)
Sparse Core Ops, SparseCore 0:
  98.6 84.9 all-gather.14
  218.3 44.3 all-gather.6
  310.5 65.7 all-gather.8
  377.8 67.4 all-gather.10
  446.7 67.4 all-gather.12
  736.7 69.8 reduce-scatter.7
  808.9 73.0 reduce-scatter.9
  884.3 73.0 reduce-scatter.11
  959.7 35.3 reduce-scatter.13
  1094.1 37.3 reduce-scatter.15
  1203.4 36.5 reduce-scatter.17
  1263.5 36.6 reduce-scatter.19

commit v4 on v3

--- a/solution.py
+++ b/solution.py
@@ -457,7 +457,7 @@
 
 
 def project_kernel(*refs):
-    w_ref, cos_ref, sin_ref, q_ref, kv_ref, w_sc, x_sc = refs[5:]
+    w_ref, cos_ref, sin_ref, q_ref, kv_ref, x_sc, w_sc = refs[5:]
     thin = w_sc.shape[0] // 32
     fetch_rows(refs[:5], x_sc)
 
@@ -489,6 +489,7 @@
         out_shape=[
             jax.ShapeDtypeStruct((NH, rows, HDIM), BF),
             jax.ShapeDtypeStruct((rows, 2 * PART), BF),
+            jax.ShapeDtypeStruct((rows, width), BF),
         ],
         grid=(rows // QB,),
         in_specs=[whole(v.shape) for v in normed]
@@ -500,8 +501,9 @@
         out_specs=[
             pl.BlockSpec((NH, QB, HDIM), lambda i: (0, i, 0)),
             pl.BlockSpec((QB, 2 * PART), lambda i: (i, 0)),
+            pl.BlockSpec((QB, width), lambda i: (i % 4 * 2 + i // 4, 0)),
         ],
-        scratch_shapes=[pltpu.VMEM((width, full[3]), BF), pltpu.VMEM((QB, width), BF)],
+        scratch_shapes=[pltpu.VMEM((width, full[3]), BF)],
         compiler_params=room(),
         cost_estimate=cost(2 * rows * width * full[3], 2 * (rows * width + width * full[3] + rows * 5 * PART)),
         name="project",
@@ -1162,11 +1164,10 @@
         ]
 
     pieces, w_qkv, grad_out = meet(pieces, w_qkv, cotangent)
-    (queries, mine), grad_out = meet(
+    (queries, mine, normed), grad_out = meet(
         project(pieces, w_qkv, cosine, sine_vals),
         cross(parts_of(quarters(grad_out))),
     )
-    normed = joined(pieces)
     theirs = lax.ppermute(mine, "c", [(0, 1), (1, 0)])
     sorted_kv, grad_out, stacked = meet(
         sort_keys(order, mine, theirs), hop_on(grad_out), stacked
@@ -1261,7 +1262,20 @@
 
     far_order = jnp.concatenate([tiles_far, tiles])
     gain_rows = grad_gain_two.astype(BF).reshape(4, 8, 1, thin).transpose(1, 0, 2, 3)
-    gain_rows = jnp.pad(gain_rows, ((0, 0), (0, 0), (0, 7), (0, 3 * GPART - thin)))
+    peak = jnp.max(peaks, axis=(0, 2))
+    peak_high = lax.reduce_precision(peak, 8, 7)
+    peak_rows = jnp.stack([peak_high.astype(BF), (peak - peak_high).astype(BF)])
+    mine_slot = (jnp.arange(8) == depth * 2 + core)[None, :, None]
+    peak_rows = jnp.where(mine_slot, peak_rows[:, None, :], 0).reshape(2, 8 * NH)
+    widen = lambda v: jnp.pad(v, ((0, 0), (0, 0), (0, 0), (0, 3 * GPART - v.shape[3])))
+    gain_rows = jnp.concatenate(
+        [
+            widen(gain_rows),
+            widen(jnp.broadcast_to(peak_rows, (8, 4, 2, 8 * NH))),
+            jnp.zeros((8, 4, 5, 3 * GPART), BF),
+        ],
+        axis=2,
+    )
 
     def back_group(g, grads):
         return attention_backward(
@@ -1280,19 +1294,13 @@
         proj = lax.psum_scatter(proj, line, scatter_dimension=0, tiled=True)
         return proj.reshape(4, thin + 8, 3 * GPART)
 
-    maxima = jnp.where(
-        jnp.arange(4)[:, None] == plane, jnp.max(peaks, axis=(0, 2))[None, :], masked_value
-    ).reshape(HEADS)
-    for name, mask, size in (("c", 1, 2), ("p", 1, 4), ("p", 2, 4), ("z", 1, 4), ("z", 2, 4)):
-        pairs = [(k, k ^ mask) for k in range(size)]
-        maxima = jnp.maximum(maxima, lax.ppermute(maxima, name, pairs))
     trade = lambda v: lax.ppermute(v, "c", [(0, 1), (1, 0)])
     grad_heads, grad_w_part = meet(grad_heads, grad_w_part)
-    part_a, grad_heads, near, grad_down = meet(
+    grad_down = sum_rows(grad_down)
+    part_a, grad_heads, near = meet(
         back_group(0, grad_heads),
         grad_heads,
         scatter_near_both(branch_ffn, far),
-        sum_rows(grad_down),
     )
     grad_w_output = sum_rows(grad_w_part)
     part_a = restore(part_a)
@@ -1303,36 +1311,40 @@
         total = scatter_sum(v, [w[k * size : (k + 1) * size] for w in near])
         output.append(quarters((state[0] + branch_scale * total).astype(BF)))
     output = join_tiles(output)
-    ffn_grads = jnp.stack([grad_gate, grad_up, grad_down])
-    ffn_grads = ffn_grads.reshape(3, share, 4, PART).transpose(2, 0, 1, 3)
-    output, grad_heads, part_a, ffn_grads = meet(output, grad_heads, part_a, ffn_grads)
-    part_b, grad_heads, hops, far_a, grad_w_output = meet(
+    output, grad_heads, part_a = meet(output, grad_heads, part_a)
+    part_b, grad_heads, hops, far_a, grad_down = meet(
         back_group(1, grad_heads),
         grad_heads,
         hop_back(output),
         trade(part_a[2]),
-        grad_w_output,
-    )
+        grad_down,
+    )
+    ffn_grads = jnp.stack([grad_gate, grad_up, grad_down])
+    ffn_grads = ffn_grads.reshape(3, share, 4, PART).transpose(2, 0, 1, 3)
     part_b = restore(part_b)
     grads_a = unturn(part_a[0], part_a[1], far_a, cosine, sine_vals)
     weights_a = weight_part(grads_a)
-    grad_heads, weights_a, hops, part_b = meet(grad_heads, weights_a, hops, part_b)
-    part_c, output, far_b, weights_a = meet(
+    grad_heads, weights_a, hops, part_b, ffn_grads = meet(
+        grad_heads, weights_a, hops, part_b, ffn_grads
+    )
+    part_c, output, far_b, weights_a, grad_w_output = meet(
         back_group(2, grad_heads),
         hop_out(hops),
         trade(part_b[2]),
         sum_line(weights_a),
-    )
-    part_c = restore(part_c)
+        grad_w_output,
+    )
+    part_c, far_b = meet(restore(part_c), far_b)
     grads_b = unturn(part_b[0], part_b[1], far_b, cosine, sine_vals)
     weights_b, far_c, ffn_grads = meet(
         weight_part(grads_b), trade(part_c[2]), cross_whole(ffn_grads)
     )
     output = joined(output)
-    weights_b = sum_line(weights_b)
     grads_c = unturn(part_c[0], part_c[1], far_c, cosine, sine_vals)
     grads = (grads_a, grads_b, grads_c)
-    rest_a, grads, weights_a = meet(unproject(grads, w_qkv, 0), grads, cross_whole(weights_a))
+    rest_a, grads, weights_a, weights_b = meet(
+        unproject(grads, w_qkv, 0), grads, cross_whole(weights_a), sum_line(weights_b)
+    )
     weights_c, far_a, grads = meet(weight_part(grads[2]), scatter_far(rest_a), grads)
     weights_c = sum_line(weights_c)
     rest_b, near_a = meet(unproject(grads, w_qkv, 1), scatter_near(rest_a, far_a))
@@ -1358,6 +1370,8 @@
     )
     grad_attn_gain = proj[3][:, 0]
 
+    maxima = jnp.sum(weights_a[:, thin + 1 : thin + 3, : 8 * NH].astype(F32), axis=1)
+    maxima = jnp.max(maxima.reshape(4, 8, NH), axis=1).reshape(HEADS)
     limit_value = clip_threshold[0].astype(F32)
     clip_factor = jnp.sqrt(limit_value / jnp.maximum(maxima, limit_value))
     column_factor = jnp.repeat(clip_factor, HDIM)

time: 1430 us -> 1440 us (level)
  waiting for transfers between devices: 282 us -> 337 us
  local copies, waits for them, and re-layouts: 161 us -> 131 us
    ppermute x42, waiting for transfers between devices: 148 us -> 198 us  [swap_blocks(): lax.ppermute(pieces[r], name, [(k, k ^ r) for k in range(4)])]
    unnamed x249 -> x269, local copies, waits for them, and re-layouts: 48.6 us -> 30.3 us
  transfers between devices with their start and end apart: 118 -> 113, of which waited for: 44 -> 50; matrix products, arithmetic and copies ran while one was open for 38% -> 34% of each run, Pallas kernels for 28% -> 28%
where the time goes in v4:
time: 1440 us; the launch traced here: 1430 us
  Pallas kernels  410 us (28%)
  waiting for transfers between devices  337 us (23%)
  matrix products  258 us (18%)
  other arithmetic  154 us (11%)
  local copies, waits for them, and re-layouts  131 us (9%)
  starting transfers between devices  123 us (9%)
  between operations  17.4 us (1%)
    dot_general x23, matrix products, mul(): return lax.dot_general(left, right, dims, preferred_element_type=F32)  258 us
    ppermute x42, waiting for transfers between devices, swap_blocks(): lax.ppermute(pieces[r], name, [(k, k ^ r) for k in range(4)])  198 us
    pallas_call x3, Pallas kernels, attention_backward(): pl.pallas_call(functools.partial(backward_kernel, first=first), out_shape...  155 us
    ppermute x52, waiting for transfers between devices, flip(): return lax.ppermute(values, 'p', [(k, k ^ mask) for k in range(4)])  119 us
    pallas_call x3, Pallas kernels, attention_forward(): pl.pallas_call(functools.partial(forward_kernel, shift=shift), out_shape=...  92.3 us
    ppermute x52, starting transfers between devices, flip(): return lax.ppermute(values, 'p', [(k, k ^ mask) for k in range(4)])  57.2 us
    ppermute x42, starting transfers between devices, swap_blocks(): lax.ppermute(pieces[r], name, [(k, k ^ r) for k in range(4)])  56.7 us
    pallas_call x2, Pallas kernels, unproject(): pl.pallas_call(unproject_kernel, out_shape=jax.ShapeDtypeStruct((rows, wi...  30.9 us
  transfers between devices with their start and end apart: 113, of which 50 were waited for; matrix products, arithmetic and copies ran while one was open for 34% of the time, Pallas kernels for 28%

profile of v4, /device:TPU:8, one launch (start us, length us, event | category | flops | bytes accessed | tf_op | source)
XLA Modules:
  0.0 1430.2 jit_solution(678557986671495225)
XLA Ops:
  27.2 12.7 collective-permute-done.3
  55.9 12.7 collective-permute-done.8
  68.6 19.7 %collective-permute-done.9 = bf16[128,2304]{1,0:T(8,128)(2,1)S(1)} collective-permute-done((bf16[128,2304]{1,0:T(8,128)(2,1)S(1)}, bf16[128,2304]{1,0:T(8,128)(2,1)S(1)}, u32[]{:S(2)}, u32[]{:S(2)}) %collective-permute-start.9) | collective-permute-done | bytes 589856 | tf_op jit(solution)/shard_map/ppermute | solution.py:1060
  114.0 41.0 %collective-permute-done.12.refs_2_ = bf16[512,2304]{1,0:T(8,128)(2,1)} collective-permute-done((bf16[512,2304]{1,0:T(8,128)(2,1)}, bf16[512,2304]{1,0:T(8,128)(2,1)}, u32[]{:S(2)}, u32[]{:S(2)}) %collective-permute-start.12) | collective-permute-done | bytes 2359328 | tf_op jit(solution)/shard_map/ppermute | solution.py:1006
  167.3 13.0 collective-permute-done.13.refs_3_
  190.2 28.3 %project.1 = (bf16[9,2048,64]{2,1,0:T(8,128)(2,1)}, bf16[2048,1152]{1,0:T(8,128)(2,1)}, bf16[2048,2304]{1,0:T(8,128)(2,1)}) custom-call(bf16[512,2304]{1,0:T(8,128)(2,1)} %pad_maximum_fusion.13.refs_0_, bf16[512,2304]{1,0:T(8,128)(2,1)} %collective-permute-done.11.refs_1_, bf16[512,2304]{1,0:T(8,128)(2,1)} %collective-permute-done.12.refs_2_, ...), custom_call_target="tpu_custom_call" | custom-call | flops 16307453952 | bytes 29196288 | tf_op jit(solution)/shard_map/project/pallas_call | solution.py:487
  269.3 19.5 %sort_keys.1 = (bf16[9,4096,64]{2,1,0:T(8,128)(2,1)}, bf16[9,4096,64]{2,1,0:T(8,128)(2,1)}, bf16[9,64,4096]{2,1,0:T(8,128)(2,1)}, bf16[9,64,4096]{2,1,0:T(8,128)(2,1)}) custom-call(s32[64]{0:T(128)} %select_reduce_fusion.order_ref, bf16[32,64,1152]{2,1,0:T(8,128)(2,1)} %bitcast.329, bf16[32,64,1152]{2,1,0:T(8,128)(2,1)} %bitcast.330, ...), custom_call_target="tpu_custom_call" | custom-call | bytes 150994944 | tf_op jit(solution)/shard_map/sort_keys/pallas_call | solution.py:533
  293.1 14.5 %collective-permute-done.21 = bf16[128,2304]{1,0:T(8,128)(2,1)} collective-permute-done((bf16[128,2304]{1,0:T(8,128)(2,1)}, bf16[128,2304]{1,0:T(8,128)(2,1)}, u32[]{:S(2)}, u32[]{:S(2)}) %collective-permute-start.21) | collective-permute-done | bytes 589856 | tf_op jit(solution)/shard_map/ppermute | solution.py:1060
  328.1 42.3 %attention_forward.3 = (bf16[1024,576]{1,0:T(8,128)(2,1)}, f32[4,9,256]{2,1,0:T(8,128)}, f32[4,9,256]{2,1,0:T(8,128)}) custom-call(s32[32]{0:T(128)} %copy-done.102, s32[8]{0:T(128)} %copy-done.115, bf16[9,2048,64]{2,1,0:T(8,128)(2,1)} %get-tuple-element.354.q_ref, bf16[9,4096,64]{2,1,0:T(8,128)(2,1)} %get-tuple-element.343.k_ref, ...), custom_call_target="tpu_custom_call" | custom-call | flops 24159191040 | bytes 37748736 | tf_op jit(solution)/shard_map/attention_forward/pallas_call | solution.py:669
  386.9 24.2 %attention_forward.5 = (bf16[512,576]{1,0:T(8,128)(2,1)}, f32[2,9,256]{2,1,0:T(8,128)}, f32[2,9,256]{2,1,0:T(8,128)}) custom-call(s32[32]{0:T(128)} %copy-done.102, s32[8]{0:T(128)} %copy-done.115, bf16[9,2048,64]{2,1,0:T(8,128)(2,1)} %get-tuple-element.354.q_ref, bf16[9,4096,64]{2,1,0:T(8,128)(2,1)} %get-tuple-element.343.k_ref, ...), custom_call_target="tpu_custom_call" | custom-call | flops 12079595520 | bytes 37748736 | tf_op jit(solution)/shard_map/attention_forward/pallas_call | solution.py:669
  423.6 25.8 %attention_forward.4 = (bf16[512,576]{1,0:T(8,128)(2,1)}, f32[2,9,256]{2,1,0:T(8,128)}, f32[2,9,256]{2,1,0:T(8,128)}) custom-call(s32[32]{0:T(128)} %copy-done.102, s32[8]{0:T(128)} %copy-done.115, bf16[9,2048,64]{2,1,0:T(8,128)(2,1)} %get-tuple-element.354.q_ref, bf16[9,4096,64]{2,1,0:T(8,128)(2,1)} %get-tuple-element.343.k_ref, ...), custom_call_target="tpu_custom_call" | custom-call | flops 12079595520 | bytes 37748736 | tf_op jit(solution)/shard_map/attention_forward/pallas_call | solution.py:669
  472.8 12.6 fusion.63
  606.8 12.5 fusion.73
  632.6 12.8 fusion.69
  673.5 13.3 fusion.71
  699.2 14.3 fusion.72
  737.3 12.7 fusion.75
  851.6 26.8 %attention_delta.1 = (bf16[9,2048,64]{2,1,0:T(8,128)(2,1)}, f32[8,9,256]{2,1,0:T(8,128)}, bf16[576,2304]{1,0:T(8,128)(2,1)}) custom-call(bf16[256,2304]{1,0:T(8,128)(2,1)} %get-tuple-element.453.refs_0_, bf16[256,2304]{1,0:T(8,128)(2,1)} %collective-permute-done.49.refs_1_, bf16[256,2304]{1,0:T(8,128)(2,1)} %collective-permute-done.50.refs_2_, ...), custom_call_target="tpu_custom_call" | custom-call | flops 5435817984 | bytes 9437184 | tf_op jit(solution)/shard_map/attention_delta/pallas_call | solution.py:720
  895.2 52.0 %attention_backward.3 = (f32[3,2048,64]{2,1,0:T(8,128)}, bf16[3,4096,64]{2,1,0:T(8,128)(2,1)}, bf16[3,4096,64]{2,1,0:T(8,128)(2,1)}) custom-call(s32[32]{0:T(128)} %copy-done.102, s32[8]{0:T(128)} %copy-done.115, bf16[9,2048,64]{2,1,0:T(8,128)(2,1)} %get-tuple-element.354.q_ref, bf16[9,2048,64]{2,1,0:T(8,128)(2,1)} %get-tuple-element.517.g_ref, ...), custom_call_target="tpu_custom_call" | custom-call | flops 32212254720 | bytes 25165824 | tf_op jit(solution)/shard_map/attention_backward/pallas_call | solution.py:817
  965.8 51.4 %attention_backward.4 = (f32[3,2048,64]{2,1,0:T(8,128)}, bf16[3,4096,64]{2,1,0:T(8,128)(2,1)}, bf16[3,4096,64]{2,1,0:T(8,128)(2,1)}) custom-call(s32[32]{0:T(128)} %copy-done.102, s32[8]{0:T(128)} %copy-done.115, bf16[9,2048,64]{2,1,0:T(8,128)(2,1)} %get-tuple-element.354.q_ref, bf16[9,2048,64]{2,1,0:T(8,128)(2,1)} %get-tuple-element.517.g_ref, ...), custom_call_target="tpu_custom_call" | custom-call | flops 32212254720 | bytes 25165824 | tf_op jit(solution)/shard_map/attention_backward/pallas_call | solution.py:817
  1017.3 22.8 %collective-permute-done.67 = bf16[128,2304]{1,0:T(8,128)(2,1)} collective-permute-done((bf16[128,2304]{1,0:T(8,128)(2,1)}, bf16[128,2304]{1,0:T(8,128)(2,1)}, u32[]{:S(2)}, u32[]{:S(2)}) %collective-permute-start.67) | collective-permute-done | bytes 589856 | tf_op jit(solution)/shard_map/ppermute | solution.py:1060
  1086.8 51.8 %attention_backward.5 = (f32[3,2048,64]{2,1,0:T(8,128)}, bf16[3,4096,64]{2,1,0:T(8,128)(2,1)}, bf16[3,4096,64]{2,1,0:T(8,128)(2,1)}) custom-call(s32[32]{0:T(128)} %copy-done.102, s32[8]{0:T(128)} %copy-done.115, bf16[9,2048,64]{2,1,0:T(8,128)(2,1)} %get-tuple-element.354.q_ref, bf16[9,2048,64]{2,1,0:T(8,128)(2,1)} %get-tuple-element.517.g_ref, ...), custom_call_target="tpu_custom_call" | custom-call | flops 32212254720 | bytes 25165824 | tf_op jit(solution)/shard_map/attention_backward/pallas_call | solution.py:817
  1221.2 15.4 %unproject.2 = bf16[1024,2304]{1,0:T(8,128)(2,1)} custom-call(bf16[2048,576]{1,0:T(8,128)(2,1)} %unturn.3.a_ref, bf16[2048,576]{1,0:T(8,128)(2,1)} %unturn.4.b_ref, bf16[2048,576]{1,0:T(8,128)(2,1)} %unturn.5.c_ref, bf16[8,4,80,1728]{3,2,1,0:T(8,128)(2,1)} %bitcast.417), custom_call_target="tpu_custom_call" | custom-call | flops 8153726976 | bytes 9437184 | tf_op jit(solution)/shard_map/unproject/pallas_call | solution.py:940
  1287.5 15.5 %unproject.3 = bf16[1024,2304]{1,0:T(8,128)(2,1)} custom-call(bf16[2048,576]{1,0:T(8,128)(2,1)} %unturn.3.a_ref, bf16[2048,576]{1,0:T(8,128)(2,1)} %unturn.4.b_ref, bf16[2048,576]{1,0:T(8,128)(2,1)} %unturn.5.c_ref, bf16[8,4,80,1728]{3,2,1,0:T(8,128)(2,1)} %bitcast.418), custom_call_target="tpu_custom_call" | custom-call | flops 8153726976 | bytes 9437184 | tf_op jit(solution)/shard_map/unproject/pallas_call | solution.py:940
  (766 shorter events, 845.1 us)
Async XLA Ops:
  7.2 176.5 %all-gather.15.cloned.1.call-start = ((), (), s32[]{:S(2)}) async-start(), calls=%async_computation.19 | async-start | bytes 10321920 | tf_op jit(solution)/shard_map/all_gather | solution.py:1131
  99.3 272.5 %all-gather.7.cloned.1.call-start = ((), (), s32[]{:S(2)}) async-start(), calls=%async_computation.8 | async-start | bytes 2985984 | tf_op jit(solution)/shard_map/all_gather | solution.py:1133
  218.6 254.2 %all-gather.9.cloned.1.call-start = ((), (), s32[]{:S(2)}) async-start(), calls=%async_computation.9 | async-start | bytes 7630848 | tf_op jit(solution)/shard_map/all_gather | solution.py:1177
  311.1 219.6 %all-gather.11.cloned.1.call-start = ((), (), s32[]{:S(2)}) async-start(), calls=%async_computation.10 | async-start | bytes 7630848 | tf_op jit(solution)/shard_map/all_gather | solution.py:1177
  314.3 228.8 %all-gather.13.cloned.1.call-start = ((), (), s32[]{:S(2)}) async-start(), calls=%async_computation.11 | async-start | bytes 7630848 | tf_op jit(solution)/shard_map/all_gather | solution.py:1177
  384.4 64.9 %collective-permute-start.31 = (bf16[256,2304]{1,0:T(8,128)(2,1)}, bf16[256,2304]{1,0:T(8,128)(2,1)}, u32[]{:S(2)}, u32[]{:S(2)}) collective-permute-start(bf16[256,2304]{1,0:T(8,128)(2,1)} %slice.506), channel_id=1, source_target_pairs={{0,8},{8,0},{16,24},{24,16},{1,9},{9,1},{17,25},{25,17},{2,10},{10... | collective-permute-start | bytes 3538952 | tf_op jit(solution)/shard_map/ppermute | solution.py:1006
  386.1 63.3 %collective-permute-start.32 = (bf16[256,2304]{1,0:T(8,128)(2,1)}, bf16[256,2304]{1,0:T(8,128)(2,1)}, u32[]{:S(2)}, u32[]{:S(2)}) collective-permute-start(bf16[256,2304]{1,0:T(8,128)(2,1)} %slice.507), channel_id=1, source_target_pairs={{0,16},{8,24},{16,0},{24,8},{1,17},{9,25},{17,1},{25,9},{2,18},{10... | collective-permute-start | bytes 3538952 | tf_op jit(solution)/shard_map/ppermute | solution.py:1006
  423.5 413.8 %reduce-scatter.8.cloned.1.call-start = ((), (), s32[]{:S(2)}) async-start(), calls=%async_computation.12 | async-start | bytes 7630848 | tf_op jit(solution)/shard_map/reduce_scatter | solution.py:1251
  737.3 145.8 %reduce-scatter.10.cloned.1.call-start = ((), (), s32[]{:S(2)}) async-start(), calls=%async_computation.13 | async-start | bytes 7630848 | tf_op jit(solution)/shard_map/reduce_scatter | solution.py:1251
  782.6 234.6 %reduce-scatter.12.cloned.1.call-start = ((), (), s32[]{:S(2)}) async-start(), calls=%async_computation.14 | async-start | bytes 7630848 | tf_op jit(solution)/shard_map/reduce_scatter | solution.py:1251
  818.3 342.8 %reduce-scatter.16.cloned.1.call-start = ((), (), s32[]{:S(2)}) async-start(), calls=%async_computation.16 | async-start | bytes 2985984 | tf_op jit(solution)/shard_map/reduce_scatter | solution.py:1251
  886.5 60.7 %collective-permute-start.63 = (bf16[512,2304]{1,0:T(8,128)(2,1)}, bf16[512,2304]{1,0:T(8,128)(2,1)}, u32[]{:S(2)}, u32[]{:S(2)}) collective-permute-start(bf16[512,2304]{1,0:T(8,128)(2,1)} %pad_maximum_fusion.18), channel_id=1, source_target_pairs={{0,8},{8,0},{16,24},{24,16},{1,9},{9,1},{17,25},{25,17},{2,10},{10... | collective-permute-start | bytes 7077896 | tf_op jit(solution)/shard_map/ppermute | solution.py:1006
  891.5 55.7 %collective-permute-start.64 = (bf16[512,2304]{1,0:T(8,128)(2,1)}, bf16[512,2304]{1,0:T(8,128)(2,1)}, u32[]{:S(2)}, u32[]{:S(2)}) collective-permute-start(bf16[512,2304]{1,0:T(8,128)(2,1)} %pad_maximum_fusion.19), channel_id=1, source_target_pairs={{0,16},{8,24},{16,0},{24,8},{1,17},{9,25},{17,1},{25,9},{2,18},{10... | collective-permute-start | bytes 7077896 | tf_op jit(solution)/shard_map/ppermute | solution.py:1006
  895.1 266.0 %reduce-scatter.14.cloned.1.call-start = ((), (), s32[]{:S(2)}) async-start(), calls=%async_computation.15 | async-start | bytes 3686400 | tf_op jit(solution)/shard_map/reduce_scatter | solution.py:1294
  961.0 56.3 %collective-permute-start.65 = (bf16[128,2304]{1,0:T(8,128)(2,1)}, bf16[128,2304]{1,0:T(8,128)(2,1)S(1)}, u32[]{:S(2)}, u32[]{:S(2)}) collective-permute-start(bf16[128,2304]{1,0:T(8,128)(2,1)} %get-tuple-element.745), channel_id=1, source_target_pairs={{0,2},{2,0},{4,6},{6,4},{1,3},{3,1},{5,7},{7,5},{8,10},{10,8},{12,... | collective-permute-start | bytes 1769480 | tf_op jit(solution)/shard_map/ppermute | solution.py:1060
  964.3 75.7 %collective-permute-start.67 = (bf16[128,2304]{1,0:T(8,128)(2,1)}, bf16[128,2304]{1,0:T(8,128)(2,1)}, u32[]{:S(2)}, u32[]{:S(2)}) collective-permute-start(bf16[128,2304]{1,0:T(8,128)(2,1)} %get-tuple-element.743), channel_id=1, source_target_pairs={{0,6},{2,4},{4,2},{6,0},{1,7},{3,5},{5,3},{7,1},{8,14},{10,12},{12... | collective-permute-start | bytes 1769480 | tf_op jit(solution)/shard_map/ppermute | solution.py:1060
  965.8 74.3 %collective-permute-start.68 = (bf16[2048,384]{1,0:T(8,128)(2,1)}, bf16[2048,384]{1,0:T(8,128)(2,1)S(1)}, u32[]{:S(2)}, u32[]{:S(2)}) collective-permute-start(bf16[2048,384]{1,0:T(8,128)(2,1)} %get-tuple-element.495), channel_id=1, source_target_pairs={{0,1},{1,0},{2,3},{3,2},{4,5},{5,4},{6,7},{7,6},{8,9},{9,8},{10,11... | collective-permute-start | bytes 4718600 | tf_op jit(solution)/shard_map/ppermute | solution.py:1297
  1080.0 156.7 %reduce-scatter.18.cloned.1.call-start = ((), (), s32[]{:S(2)}) async-start(), calls=%async_computation.17 | async-start | bytes 3686400 | tf_op jit(solution)/shard_map/reduce_scatter | solution.py:1294
  1082.9 55.7 %collective-permute-start.71 = (bf16[128,2304]{1,0:T(8,128)(2,1)S(1)}, bf16[128,2304]{1,0:T(8,128)(2,1)S(1)}, u32[]{:S(2)}, u32[]{:S(2)}) collective-permute-start(bf16[128,2304]{1,0:T(8,128)(2,1)S(1)} %get-tuple-element.740), channel_id=1, source_target_pairs={{0,24},{8,16},{16,8},{24,0},{1,25},{9,17},{17,9},{25,1},{2,26},{10... | collective-permute-start | bytes 1769480 | tf_op jit(solution)/shard_map/ppermute | solution.py:1060
  1082.9 57.3 %collective-permute-start.70 = (bf16[128,2304]{1,0:T(8,128)(2,1)}, bf16[128,2304]{1,0:T(8,128)(2,1)}, u32[]{:S(2)}, u32[]{:S(2)}) collective-permute-start(bf16[128,2304]{1,0:T(8,128)(2,1)} %get-tuple-element.741), channel_id=1, source_target_pairs={{0,16},{8,24},{16,0},{24,8},{1,17},{9,25},{17,1},{25,9},{2,18},{10... | collective-permute-start | bytes 1769480 | tf_op jit(solution)/shard_map/ppermute | solution.py:1060
  1084.4 57.7 %collective-permute-start.69 = (bf16[128,2304]{1,0:T(8,128)(2,1)}, bf16[128,2304]{1,0:T(8,128)(2,1)}, u32[]{:S(2)}, u32[]{:S(2)}) collective-permute-start(bf16[128,2304]{1,0:T(8,128)(2,1)} %get-tuple-element.742), channel_id=1, source_target_pairs={{0,8},{8,0},{16,24},{24,16},{1,9},{9,1},{17,25},{25,17},{2,10},{10... | collective-permute-start | bytes 1769480 | tf_op jit(solution)/shard_map/ppermute | solution.py:1060
  1086.4 74.7 %collective-permute-start.72 = (bf16[2048,384]{1,0:T(8,128)(2,1)}, bf16[2048,384]{1,0:T(8,128)(2,1)}, u32[]{:S(2)}, u32[]{:S(2)}) collective-permute-start(bf16[2048,384]{1,0:T(8,128)(2,1)} %get-tuple-element.525), channel_id=1, source_target_pairs={{0,1},{1,0},{2,3},{3,2},{4,5},{5,4},{6,7},{7,6},{8,9},{9,8},{10,11... | collective-permute-start | bytes 4718600 | tf_op jit(solution)/shard_map/ppermute | solution.py:1297
  1086.7 58.3 %collective-permute-start.76 = (bf16[3,184,576]{2,1,0:T(8,128)(2,1)S(1)}, bf16[3,184,576]{2,1,0:T(8,128)(2,1)S(1)}, u32[]{:S(2)}, u32[]{:S(2)}) collective-permute-start(bf16[3,184,576]{2,1,0:T(8,128)(2,1)S(1)} %get-tuple-element.717), channel_id=1, source_target_pairs={{0,24},{8,16},{16,8},{24,0},{1,25},{9,17},{17,9},{25,1},{2,26},{10... | collective-permute-start | bytes 1907720 | tf_op jit(solution)/shard_map/ppermute | solution.py:1060
  1196.9 201.7 %reduce-scatter.20.cloned.1.call-start = ((), (), s32[]{:S(2)}) async-start(), calls=%async_computation.18 | async-start | bytes 3686400 | tf_op jit(solution)/shard_map/reduce_scatter | solution.py:1294
  (217 other events, 3869.6 us)
Sparse Core Ops, SparseCore 0:
  98.6 84.9 all-gather.14
  218.7 44.3 all-gather.6
  311.2 65.5 all-gather.8
  378.2 67.4 all-gather.10
  447.2 67.4 all-gather.12
  737.4 70.1 reduce-scatter.7
  809.8 73.1 reduce-scatter.9
  885.3 73.0 reduce-scatter.11
  960.7 80.3 reduce-scatter.15
  1080.1 35.4 reduce-scatter.13
  1197.0 36.5 reduce-scatter.17
  1287.6 37.8 reduce-scatter.19

commit v5 on v4

--- a/solution.py
+++ b/solution.py
@@ -1253,13 +1253,12 @@
     grad_gain_two = back_a[0] + back_b[0]
     grad_resid = [back_a[1], back_b[1]]
 
-    grad_pieces, branch_ffn, grad_gate = meet(grad_pieces, branch_ffn, sum_rows(grad_gate))
-    (grad_heads, row_delta, grad_w_part), far, grad_up = meet(
+    grad_pieces, branch_ffn = meet(grad_pieces, branch_ffn)
+    (grad_heads, row_delta, grad_w_part), far, grad_gate = meet(
         attention_delta(grad_pieces, w_out, attended),
         scatter_far_both(branch_ffn),
-        sum_rows(grad_up),
-    )
-
+        sum_rows(grad_gate),
+    )
     far_order = jnp.concatenate([tiles_far, tiles])
     gain_rows = grad_gain_two.astype(BF).reshape(4, 8, 1, thin).transpose(1, 0, 2, 3)
     peak = jnp.max(peaks, axis=(0, 2))
@@ -1297,10 +1296,11 @@
     trade = lambda v: lax.ppermute(v, "c", [(0, 1), (1, 0)])
     grad_heads, grad_w_part = meet(grad_heads, grad_w_part)
     grad_down = sum_rows(grad_down)
-    part_a, grad_heads, near = meet(
+    part_a, grad_heads, near, grad_up = meet(
         back_group(0, grad_heads),
         grad_heads,
         scatter_near_both(branch_ffn, far),
+        sum_rows(grad_up),
     )
     grad_w_output = sum_rows(grad_w_part)
     part_a = restore(part_a)
@@ -1327,27 +1327,27 @@
     grad_heads, weights_a, hops, part_b, ffn_grads = meet(
         grad_heads, weights_a, hops, part_b, ffn_grads
     )
-    part_c, output, far_b, weights_a, grad_w_output = meet(
-        back_group(2, grad_heads),
-        hop_out(hops),
-        trade(part_b[2]),
-        sum_line(weights_a),
-        grad_w_output,
-    )
+    part_c, output, far_b = meet(back_group(2, grad_heads), hop_out(hops), trade(part_b[2]))
+    weights_a = sum_line(weights_a)
     part_c, far_b = meet(restore(part_c), far_b)
     grads_b = unturn(part_b[0], part_b[1], far_b, cosine, sine_vals)
     weights_b, far_c, ffn_grads = meet(
         weight_part(grads_b), trade(part_c[2]), cross_whole(ffn_grads)
     )
     output = joined(output)
-    grads_c = unturn(part_c[0], part_c[1], far_c, cosine, sine_vals)
+    grads_c, weights_a = meet(
+        unturn(part_c[0], part_c[1], far_c, cosine, sine_vals), weights_a
+    )
     grads = (grads_a, grads_b, grads_c)
-    rest_a, grads, weights_a, weights_b = meet(
-        unproject(grads, w_qkv, 0), grads, cross_whole(weights_a), sum_line(weights_b)
-    )
+    rest_a, grads, weights_a = meet(unproject(grads, w_qkv, 0), grads, cross_whole(weights_a))
     weights_c, far_a, grads = meet(weight_part(grads[2]), scatter_far(rest_a), grads)
     weights_c = sum_line(weights_c)
-    rest_b, near_a = meet(unproject(grads, w_qkv, 1), scatter_near(rest_a, far_a))
+    rest_b, near_a, weights_b, grad_w_output = meet(
+        unproject(grads, w_qkv, 1),
+        scatter_near(rest_a, far_a),
+        sum_line(weights_b),
+        grad_w_output,
+    )
     far_b = scatter_far(rest_b)
 
     def first_back(k, total):

time: 1440 us -> 1430 us (level)
  waiting for transfers between devices: 337 us -> 304 us
    ppermute x42, waiting for transfers between devices: 198 us -> 173 us  [swap_blocks(): lax.ppermute(pieces[r], name, [(k, k ^ r) for k in range(4)])]
    unnamed x269 -> x251, local copies, waits for them, and re-layouts: 30.3 us -> 34.6 us
  transfers between devices with their start and end apart: 113 -> 113, of which waited for: 50 -> 46; matrix products, arithmetic and copies ran while one was open for 34% -> 35% of each run, Pallas kernels for 28% -> 27%
where the time goes in v5:
time: 1430 us; the launch traced here: 1410 us
  Pallas kernels  405 us (28%)
  waiting for transfers between devices  304 us (21%)
  matrix products  258 us (18%)
  other arithmetic  159 us (11%)
  local copies, waits for them, and re-layouts  144 us (10%)
  starting transfers between devices  124 us (9%)
  between operations  17.1 us (1%)
    dot_general x23, matrix products, mul(): return lax.dot_general(left, right, dims, preferred_element_type=F32)  258 us
    ppermute x42, waiting for transfers between devices, swap_blocks(): lax.ppermute(pieces[r], name, [(k, k ^ r) for k in range(4)])  173 us
    pallas_call x3, Pallas kernels, attention_backward(): pl.pallas_call(functools.partial(backward_kernel, first=first), out_shape...  155 us
    ppermute x52, waiting for transfers between devices, flip(): return lax.ppermute(values, 'p', [(k, k ^ mask) for k in range(4)])  117 us
    pallas_call x3, Pallas kernels, attention_forward(): pl.pallas_call(functools.partial(forward_kernel, shift=shift), out_shape=...  88.3 us
    ppermute x52, starting transfers between devices, flip(): return lax.ppermute(values, 'p', [(k, k ^ mask) for k in range(4)])  59.9 us
    ppermute x42, starting transfers between devices, swap_blocks(): lax.ppermute(pieces[r], name, [(k, k ^ r) for k in range(4)])  54.6 us
    unnamed x251, local copies, waits for them, and re-layouts  34.6 us
  transfers between devices with their start and end apart: 113, of which 46 were waited for; matrix products, arithmetic and copies ran while one was open for 35% of the time, Pallas kernels for 27%

profile of v5, /device:TPU:8, one launch (start us, length us, event | category | flops | bytes accessed | tf_op | source)
XLA Modules:
  0.0 1411.2 jit_solution(13889811781978851870)
XLA Ops:
  27.2 12.7 collective-permute-done.3
  55.9 12.7 collective-permute-done.8
  68.6 19.7 %collective-permute-done.9 = bf16[128,2304]{1,0:T(8,128)(2,1)S(1)} collective-permute-done((bf16[128,2304]{1,0:T(8,128)(2,1)S(1)}, bf16[128,2304]{1,0:T(8,128)(2,1)S(1)}, u32[]{:S(2)}, u32[]{:S(2)}) %collective-permute-start.9) | collective-permute-done | bytes 589856 | tf_op jit(solution)/shard_map/ppermute | solution.py:1060
  114.0 41.0 %collective-permute-done.12.refs_2_ = bf16[512,2304]{1,0:T(8,128)(2,1)} collective-permute-done((bf16[512,2304]{1,0:T(8,128)(2,1)}, bf16[512,2304]{1,0:T(8,128)(2,1)}, u32[]{:S(2)}, u32[]{:S(2)}) %collective-permute-start.12) | collective-permute-done | bytes 2359328 | tf_op jit(solution)/shard_map/ppermute | solution.py:1006
  167.4 13.0 collective-permute-done.13.refs_3_
  190.2 28.3 %project.1 = (bf16[9,2048,64]{2,1,0:T(8,128)(2,1)}, bf16[2048,1152]{1,0:T(8,128)(2,1)}, bf16[2048,2304]{1,0:T(8,128)(2,1)}) custom-call(bf16[512,2304]{1,0:T(8,128)(2,1)} %pad_maximum_fusion.13.refs_0_, bf16[512,2304]{1,0:T(8,128)(2,1)} %collective-permute-done.11.refs_1_, bf16[512,2304]{1,0:T(8,128)(2,1)} %collective-permute-done.12.refs_2_, ...), custom_call_target="tpu_custom_call" | custom-call | flops 16307453952 | bytes 29196288 | tf_op jit(solution)/shard_map/project/pallas_call | solution.py:487
  269.1 19.5 %sort_keys.1 = (bf16[9,4096,64]{2,1,0:T(8,128)(2,1)}, bf16[9,4096,64]{2,1,0:T(8,128)(2,1)}, bf16[9,64,4096]{2,1,0:T(8,128)(2,1)}, bf16[9,64,4096]{2,1,0:T(8,128)(2,1)}) custom-call(s32[64]{0:T(128)} %select_reduce_fusion.order_ref, bf16[32,64,1152]{2,1,0:T(8,128)(2,1)} %bitcast.329, bf16[32,64,1152]{2,1,0:T(8,128)(2,1)} %bitcast.330, ...), custom_call_target="tpu_custom_call" | custom-call | bytes 150994944 | tf_op jit(solution)/shard_map/sort_keys/pallas_call | solution.py:533
  293.0 14.5 %collective-permute-done.21 = bf16[128,2304]{1,0:T(8,128)(2,1)} collective-permute-done((bf16[128,2304]{1,0:T(8,128)(2,1)}, bf16[128,2304]{1,0:T(8,128)(2,1)}, u32[]{:S(2)}, u32[]{:S(2)}) %collective-permute-start.21) | collective-permute-done | bytes 589856 | tf_op jit(solution)/shard_map/ppermute | solution.py:1060
  328.1 42.3 %attention_forward.3 = (bf16[1024,576]{1,0:T(8,128)(2,1)}, f32[4,9,256]{2,1,0:T(8,128)}, f32[4,9,256]{2,1,0:T(8,128)}) custom-call(s32[32]{0:T(128)} %copy-done.94, s32[8]{0:T(128)} %copy-done.107, bf16[9,2048,64]{2,1,0:T(8,128)(2,1)} %get-tuple-element.355.q_ref, bf16[9,4096,64]{2,1,0:T(8,128)(2,1)} %get-tuple-element.344.k_ref, ...), custom_call_target="tpu_custom_call" | custom-call | flops 24159191040 | bytes 37748736 | tf_op jit(solution)/shard_map/attention_forward/pallas_call | solution.py:669
  387.1 20.4 %attention_forward.5 = (bf16[512,576]{1,0:T(8,128)(2,1)}, f32[2,9,256]{2,1,0:T(8,128)}, f32[2,9,256]{2,1,0:T(8,128)}) custom-call(s32[32]{0:T(128)} %copy-done.94, s32[8]{0:T(128)} %copy-done.107, bf16[9,2048,64]{2,1,0:T(8,128)(2,1)} %get-tuple-element.355.q_ref, bf16[9,4096,64]{2,1,0:T(8,128)(2,1)} %get-tuple-element.344.k_ref, ...), custom_call_target="tpu_custom_call" | custom-call | flops 12079595520 | bytes 37748736 | tf_op jit(solution)/shard_map/attention_forward/pallas_call | solution.py:669
  423.7 25.6 %attention_forward.4 = (bf16[512,576]{1,0:T(8,128)(2,1)}, f32[2,9,256]{2,1,0:T(8,128)}, f32[2,9,256]{2,1,0:T(8,128)}) custom-call(s32[32]{0:T(128)} %copy-done.94, s32[8]{0:T(128)} %copy-done.107, bf16[9,2048,64]{2,1,0:T(8,128)(2,1)} %get-tuple-element.355.q_ref, bf16[9,4096,64]{2,1,0:T(8,128)(2,1)} %get-tuple-element.344.k_ref, ...), custom_call_target="tpu_custom_call" | custom-call | flops 12079595520 | bytes 37748736 | tf_op jit(solution)/shard_map/attention_forward/pallas_call | solution.py:669
  473.0 12.6 fusion.63
  632.3 12.7 fusion.69
  673.2 13.2 fusion.71
  698.8 14.2 %fusion.72 = f32[1472,2304]{1,0:T(8,128)} fusion(bf16[1024,1472]{0,1:T(8,128)(2,1)S(1)} %copy-done.39, bf16[1024,2304]{1,0:T(8,128)(2,1)} %copy-done.72), kind=kOutput, calls=%fused_computation.356 | convolution fusion | flops 6945767424 | bytes 21299200 | tf_op jit(solution)/shard_map/dot_general | solution.py:409
  736.9 12.7 fusion.75
  814.1 13.3 convolution_convert_fusion.3
  857.6 26.7 %attention_delta.1 = (bf16[9,2048,64]{2,1,0:T(8,128)(2,1)}, f32[8,9,256]{2,1,0:T(8,128)}, bf16[576,2304]{1,0:T(8,128)(2,1)}) custom-call(bf16[256,2304]{1,0:T(8,128)(2,1)} %get-tuple-element.453.refs_0_, bf16[256,2304]{1,0:T(8,128)(2,1)} %collective-permute-done.49.refs_1_, bf16[256,2304]{1,0:T(8,128)(2,1)} %collective-permute-done.50.refs_2_, ...), custom_call_target="tpu_custom_call" | custom-call | flops 5435817984 | bytes 9437184 | tf_op jit(solution)/shard_map/attention_delta/pallas_call | solution.py:720
  897.0 51.7 %attention_backward.3 = (f32[3,2048,64]{2,1,0:T(8,128)}, bf16[3,4096,64]{2,1,0:T(8,128)(2,1)}, bf16[3,4096,64]{2,1,0:T(8,128)(2,1)}) custom-call(s32[32]{0:T(128)} %copy-done.94, s32[8]{0:T(128)} %copy-done.107, bf16[9,2048,64]{2,1,0:T(8,128)(2,1)} %get-tuple-element.355.q_ref, bf16[9,2048,64]{2,1,0:T(8,128)(2,1)} %get-tuple-element.518.g_ref, ...), custom_call_target="tpu_custom_call" | custom-call | flops 32212254720 | bytes 25165824 | tf_op jit(solution)/shard_map/attention_backward/pallas_call | solution.py:817
  966.0 51.4 %attention_backward.4 = (f32[3,2048,64]{2,1,0:T(8,128)}, bf16[3,4096,64]{2,1,0:T(8,128)(2,1)}, bf16[3,4096,64]{2,1,0:T(8,128)(2,1)}) custom-call(s32[32]{0:T(128)} %copy-done.94, s32[8]{0:T(128)} %copy-done.107, bf16[9,2048,64]{2,1,0:T(8,128)(2,1)} %get-tuple-element.355.q_ref, bf16[9,2048,64]{2,1,0:T(8,128)(2,1)} %get-tuple-element.518.g_ref, ...), custom_call_target="tpu_custom_call" | custom-call | flops 32212254720 | bytes 25165824 | tf_op jit(solution)/shard_map/attention_backward/pallas_call | solution.py:817
  1074.0 51.6 %attention_backward.5 = (f32[3,2048,64]{2,1,0:T(8,128)}, bf16[3,4096,64]{2,1,0:T(8,128)(2,1)}, bf16[3,4096,64]{2,1,0:T(8,128)(2,1)}) custom-call(s32[32]{0:T(128)} %copy-done.94, s32[8]{0:T(128)} %copy-done.107, bf16[9,2048,64]{2,1,0:T(8,128)(2,1)} %get-tuple-element.355.q_ref, bf16[9,2048,64]{2,1,0:T(8,128)(2,1)} %get-tuple-element.518.g_ref, ...), custom_call_target="tpu_custom_call" | custom-call | flops 32212254720 | bytes 25165824 | tf_op jit(solution)/shard_map/attention_backward/pallas_call | solution.py:817
  1130.2 13.6 collective-permute-done.75
  1204.9 15.4 %unproject.2 = bf16[1024,2304]{1,0:T(8,128)(2,1)} custom-call(bf16[2048,576]{1,0:T(8,128)(2,1)} %unturn.3.a_ref, bf16[2048,576]{1,0:T(8,128)(2,1)} %unturn.4.b_ref, bf16[2048,576]{1,0:T(8,128)(2,1)} %unturn.5.c_ref, bf16[8,4,80,1728]{3,2,1,0:T(8,128)(2,1)} %bitcast.413), custom_call_target="tpu_custom_call" | custom-call | flops 8153726976 | bytes 9437184 | tf_op jit(solution)/shard_map/unproject/pallas_call | solution.py:940
  1271.4 15.5 %unproject.3 = bf16[1024,2304]{1,0:T(8,128)(2,1)} custom-call(bf16[2048,576]{1,0:T(8,128)(2,1)} %unturn.3.a_ref, bf16[2048,576]{1,0:T(8,128)(2,1)} %unturn.4.b_ref, bf16[2048,576]{1,0:T(8,128)(2,1)} %unturn.5.c_ref, bf16[8,4,80,1728]{3,2,1,0:T(8,128)(2,1)} %bitcast.414), custom_call_target="tpu_custom_call" | custom-call | flops 8153726976 | bytes 9437184 | tf_op jit(solution)/shard_map/unproject/pallas_call | solution.py:940
  (747 shorter events, 839.8 us)
Async XLA Ops:
  7.2 176.5 %all-gather.15.cloned.1.call-start = ((), (), s32[]{:S(2)}) async-start(), calls=%async_computation.19 | async-start | bytes 10321920 | tf_op jit(solution)/shard_map/all_gather | solution.py:1131
  99.3 272.6 %all-gather.7.cloned.1.call-start = ((), (), s32[]{:S(2)}) async-start(), calls=%async_computation.8 | async-start | bytes 2985984 | tf_op jit(solution)/shard_map/all_gather | solution.py:1133
  218.6 254.4 %all-gather.9.cloned.1.call-start = ((), (), s32[]{:S(2)}) async-start(), calls=%async_computation.9 | async-start | bytes 7630848 | tf_op jit(solution)/shard_map/all_gather | solution.py:1177
  311.0 219.7 %all-gather.11.cloned.1.call-start = ((), (), s32[]{:S(2)}) async-start(), calls=%async_computation.10 | async-start | bytes 7630848 | tf_op jit(solution)/shard_map/all_gather | solution.py:1177
  314.2 228.9 %all-gather.13.cloned.1.call-start = ((), (), s32[]{:S(2)}) async-start(), calls=%async_computation.11 | async-start | bytes 7630848 | tf_op jit(solution)/shard_map/all_gather | solution.py:1177
  384.6 64.7 %collective-permute-start.31 = (bf16[256,2304]{1,0:T(8,128)(2,1)}, bf16[256,2304]{1,0:T(8,128)(2,1)}, u32[]{:S(2)}, u32[]{:S(2)}) collective-permute-start(bf16[256,2304]{1,0:T(8,128)(2,1)} %slice.506), channel_id=1, source_target_pairs={{0,8},{8,0},{16,24},{24,16},{1,9},{9,1},{17,25},{25,17},{2,10},{10... | collective-permute-start | bytes 3538952 | tf_op jit(solution)/shard_map/ppermute | solution.py:1006
  386.3 63.0 %collective-permute-start.32 = (bf16[256,2304]{1,0:T(8,128)(2,1)}, bf16[256,2304]{1,0:T(8,128)(2,1)}, u32[]{:S(2)}, u32[]{:S(2)}) collective-permute-start(bf16[256,2304]{1,0:T(8,128)(2,1)} %slice.507), channel_id=1, source_target_pairs={{0,16},{8,24},{16,0},{24,8},{1,17},{9,25},{17,1},{25,9},{2,18},{10... | collective-permute-start | bytes 3538952 | tf_op jit(solution)/shard_map/ppermute | solution.py:1006
  423.6 460.7 %reduce-scatter.8.cloned.1.call-start = ((), (), s32[]{:S(2)}) async-start(), calls=%async_computation.12 | async-start | bytes 7630848 | tf_op jit(solution)/shard_map/reduce_scatter | solution.py:1251
  736.8 211.9 %reduce-scatter.10.cloned.1.call-start = ((), (), s32[]{:S(2)}) async-start(), calls=%async_computation.13 | async-start | bytes 7630848 | tf_op jit(solution)/shard_map/reduce_scatter | solution.py:1251
  782.1 239.1 %reduce-scatter.12.cloned.1.call-start = ((), (), s32[]{:S(2)}) async-start(), calls=%async_computation.14 | async-start | bytes 7630848 | tf_op jit(solution)/shard_map/reduce_scatter | solution.py:1251
  844.8 355.4 %reduce-scatter.14.cloned.1.call-start = ((), (), s32[]{:S(2)}) async-start(), calls=%async_computation.15 | async-start | bytes 3686400 | tf_op jit(solution)/shard_map/reduce_scatter | solution.py:1293
  887.9 60.8 %collective-permute-start.63 = (bf16[512,2304]{1,0:T(8,128)(2,1)}, bf16[512,2304]{1,0:T(8,128)(2,1)}, u32[]{:S(2)}, u32[]{:S(2)}) collective-permute-start(bf16[512,2304]{1,0:T(8,128)(2,1)} %pad_maximum_fusion.18), channel_id=1, source_target_pairs={{0,8},{8,0},{16,24},{24,16},{1,9},{9,1},{17,25},{25,17},{2,10},{10... | collective-permute-start | bytes 7077896 | tf_op jit(solution)/shard_map/ppermute | solution.py:1006
  893.2 55.5 %collective-permute-start.64 = (bf16[512,2304]{1,0:T(8,128)(2,1)}, bf16[512,2304]{1,0:T(8,128)(2,1)}, u32[]{:S(2)}, u32[]{:S(2)}) collective-permute-start(bf16[512,2304]{1,0:T(8,128)(2,1)} %pad_maximum_fusion.19), channel_id=1, source_target_pairs={{0,16},{8,24},{16,0},{24,8},{1,17},{9,25},{17,1},{25,9},{2,18},{10... | collective-permute-start | bytes 7077896 | tf_op jit(solution)/shard_map/ppermute | solution.py:1006
  962.5 58.7 %collective-permute-start.65 = (bf16[128,2304]{1,0:T(8,128)(2,1)}, bf16[128,2304]{1,0:T(8,128)(2,1)}, u32[]{:S(2)}, u32[]{:S(2)}) collective-permute-start(bf16[128,2304]{1,0:T(8,128)(2,1)} %get-tuple-element.747), channel_id=1, source_target_pairs={{0,2},{2,0},{4,6},{6,4},{1,3},{3,1},{5,7},{7,5},{8,10},{10,8},{12,... | collective-permute-start | bytes 1769480 | tf_op jit(solution)/shard_map/ppermute | solution.py:1060
  962.5 58.7 %collective-permute-start.66 = (bf16[128,2304]{1,0:T(8,128)(2,1)}, bf16[128,2304]{1,0:T(8,128)(2,1)}, u32[]{:S(2)}, u32[]{:S(2)}) collective-permute-start(bf16[128,2304]{1,0:T(8,128)(2,1)} %get-tuple-element.746), channel_id=1, source_target_pairs={{0,4},{2,6},{4,0},{6,2},{1,5},{3,7},{5,1},{7,3},{8,12},{10,14},{12... | collective-permute-start | bytes 1769480 | tf_op jit(solution)/shard_map/ppermute | solution.py:1060
  962.5 58.7 %collective-permute-start.67 = (bf16[128,2304]{1,0:T(8,128)(2,1)}, bf16[128,2304]{1,0:T(8,128)(2,1)}, u32[]{:S(2)}, u32[]{:S(2)}) collective-permute-start(bf16[128,2304]{1,0:T(8,128)(2,1)} %get-tuple-element.745), channel_id=1, source_target_pairs={{0,6},{2,4},{4,2},{6,0},{1,7},{3,5},{5,3},{7,1},{8,14},{10,12},{12... | collective-permute-start | bytes 1769480 | tf_op jit(solution)/shard_map/ppermute | solution.py:1060
  1061.1 225.7 %reduce-scatter.18.cloned.1.call-start = ((), (), s32[]{:S(2)}) async-start(), calls=%async_computation.17 | async-start | bytes 2985984 | tf_op jit(solution)/shard_map/reduce_scatter | solution.py:1251
  1064.3 222.6 %reduce-scatter.16.cloned.1.call-start = ((), (), s32[]{:S(2)}) async-start(), calls=%async_computation.16 | async-start | bytes 3686400 | tf_op jit(solution)/shard_map/reduce_scatter | solution.py:1293
  1067.3 58.3 %collective-permute-start.71 = (bf16[128,2304]{1,0:T(8,128)(2,1)}, bf16[128,2304]{1,0:T(8,128)(2,1)S(1)}, u32[]{:S(2)}, u32[]{:S(2)}) collective-permute-start(bf16[128,2304]{1,0:T(8,128)(2,1)} %get-tuple-element.742), channel_id=1, source_target_pairs={{0,24},{8,16},{16,8},{24,0},{1,25},{9,17},{17,9},{25,1},{2,26},{10... | collective-permute-start | bytes 1769480 | tf_op jit(solution)/shard_map/ppermute | solution.py:1060
  1069.1 58.1 %collective-permute-start.70 = (bf16[128,2304]{1,0:T(8,128)(2,1)}, bf16[128,2304]{1,0:T(8,128)(2,1)}, u32[]{:S(2)}, u32[]{:S(2)}) collective-permute-start(bf16[128,2304]{1,0:T(8,128)(2,1)} %get-tuple-element.743), channel_id=1, source_target_pairs={{0,16},{8,24},{16,0},{24,8},{1,17},{9,25},{17,1},{25,9},{2,18},{10... | collective-permute-start | bytes 1769480 | tf_op jit(solution)/shard_map/ppermute | solution.py:1060
  1070.5 56.9 %collective-permute-start.69 = (bf16[128,2304]{1,0:T(8,128)(2,1)}, bf16[128,2304]{1,0:T(8,128)(2,1)}, u32[]{:S(2)}, u32[]{:S(2)}) collective-permute-start(bf16[128,2304]{1,0:T(8,128)(2,1)} %get-tuple-element.744), channel_id=1, source_target_pairs={{0,8},{8,0},{16,24},{24,16},{1,9},{9,1},{17,25},{25,17},{2,10},{10... | collective-permute-start | bytes 1769480 | tf_op jit(solution)/shard_map/ppermute | solution.py:1060
  1070.8 77.0 %collective-permute-start.72 = (bf16[2048,384]{1,0:T(8,128)(2,1)}, bf16[2048,384]{1,0:T(8,128)(2,1)S(1)}, u32[]{:S(2)}, u32[]{:S(2)}) collective-permute-start(bf16[2048,384]{1,0:T(8,128)(2,1)} %get-tuple-element.526), channel_id=1, source_target_pairs={{0,1},{1,0},{2,3},{3,2},{4,5},{5,4},{6,7},{7,6},{8,9},{9,8},{10,11... | collective-permute-start | bytes 4718600 | tf_op jit(solution)/shard_map/ppermute | solution.py:1296
  1072.2 58.0 %collective-permute-start.76 = (bf16[3,184,576]{2,1,0:T(8,128)(2,1)}, bf16[3,184,576]{2,1,0:T(8,128)(2,1)S(1)}, u32[]{:S(2)}, u32[]{:S(2)}) collective-permute-start(bf16[3,184,576]{2,1,0:T(8,128)(2,1)} %get-tuple-element.719), channel_id=1, source_target_pairs={{0,24},{8,16},{16,8},{24,0},{1,25},{9,17},{17,9},{25,1},{2,26},{10... | collective-permute-start | bytes 1907720 | tf_op jit(solution)/shard_map/ppermute | solution.py:1060
  1188.8 191.4 %reduce-scatter.20.cloned.1.call-start = ((), (), s32[]{:S(2)}) async-start(), calls=%async_computation.18 | async-start | bytes 3686400 | tf_op jit(solution)/shard_map/reduce_scatter | solution.py:1293
  (208 other events, 3706.5 us)
Sparse Core Ops, SparseCore 0:
  98.6 84.9 all-gather.14
  218.7 44.4 all-gather.6
  311.1 65.7 all-gather.8
  378.4 67.4 all-gather.10
  447.3 67.4 all-gather.12
  736.9 70.1 reduce-scatter.7
  809.4 73.0 reduce-scatter.9
  884.8 77.9 reduce-scatter.11
  1061.2 36.5 reduce-scatter.13
  1100.1 36.4 reduce-scatter.17
  1189.0 35.8 reduce-scatter.15
  1271.5 35.3 reduce-scatter.19

commit v6 on v5

--- a/solution.py
+++ b/solution.py
@@ -1327,13 +1327,13 @@
     grad_heads, weights_a, hops, part_b, ffn_grads = meet(
         grad_heads, weights_a, hops, part_b, ffn_grads
     )
-    part_c, output, far_b = meet(back_group(2, grad_heads), hop_out(hops), trade(part_b[2]))
+    part_c, hops, ffn_grads, far_b = meet(
+        back_group(2, grad_heads), hops, cross_whole(ffn_grads), trade(part_b[2])
+    )
     weights_a = sum_line(weights_a)
     part_c, far_b = meet(restore(part_c), far_b)
     grads_b = unturn(part_b[0], part_b[1], far_b, cosine, sine_vals)
-    weights_b, far_c, ffn_grads = meet(
-        weight_part(grads_b), trade(part_c[2]), cross_whole(ffn_grads)
-    )
+    weights_b, far_c, output = meet(weight_part(grads_b), trade(part_c[2]), hop_out(hops))
     output = joined(output)
     grads_c, weights_a = meet(
         unturn(part_c[0], part_c[1], far_c, cosine, sine_vals), weights_a

time: 1430 us -> 1430 us (level)
    unnamed x251 -> x247, local copies, waits for them, and re-layouts: 34.6 us -> 33.9 us
where the time goes in v6:
time: 1430 us; the launch traced here: 1420 us
  Pallas kernels  409 us (29%)
  waiting for transfers between devices  306 us (21%)
  matrix products  258 us (18%)
  other arithmetic  157 us (11%)
  local copies, waits for them, and re-layouts  141 us (10%)
  starting transfers between devices  129 us (9%)
  between operations  17.1 us (1%)
    dot_general x23, matrix products, mul(): return lax.dot_general(left, right, dims, preferred_element_type=F32)  258 us
    ppermute x42, waiting for transfers between devices, swap_blocks(): lax.ppermute(pieces[r], name, [(k, k ^ r) for k in range(4)])  167 us
    pallas_call x3, Pallas kernels, attention_backward(): pl.pallas_call(functools.partial(backward_kernel, first=first), out_shape...  155 us
    ppermute x52, waiting for transfers between devices, flip(): return lax.ppermute(values, 'p', [(k, k ^ mask) for k in range(4)])  123 us
    pallas_call x3, Pallas kernels, attention_forward(): pl.pallas_call(functools.partial(forward_kernel, shift=shift), out_shape=...  92 us
    ppermute x42, starting transfers between devices, swap_blocks(): lax.ppermute(pieces[r], name, [(k, k ^ r) for k in range(4)])  63.9 us
    ppermute x52, starting transfers between devices, flip(): return lax.ppermute(values, 'p', [(k, k ^ mask) for k in range(4)])  56.3 us
    unnamed x247, local copies, waits for them, and re-layouts  33.9 us
  transfers between devices with their start and end apart: 113, of which 46 were waited for; matrix products, arithmetic and copies ran while one was open for 35% of the time, Pallas kernels for 27%

profile of v6, /device:TPU:8, one launch (start us, length us, event | category | flops | bytes accessed | tf_op | source)
XLA Modules:
  0.0 1417.4 jit_solution(3003755177076522674)
XLA Ops:
  27.2 12.7 collective-permute-done.1
  55.9 12.7 collective-permute-done.6
  68.6 19.7 %collective-permute-done.7 = bf16[128,2304]{1,0:T(8,128)(2,1)S(1)} collective-permute-done((bf16[128,2304]{1,0:T(8,128)(2,1)S(1)}, bf16[128,2304]{1,0:T(8,128)(2,1)S(1)}, u32[]{:S(2)}, u32[]{:S(2)}) %collective-permute-start.7) | collective-permute-done | bytes 589856 | tf_op jit(solution)/shard_map/ppermute | solution.py:1060
  114.0 41.0 %collective-permute-done.10.refs_2_ = bf16[512,2304]{1,0:T(8,128)(2,1)} collective-permute-done((bf16[512,2304]{1,0:T(8,128)(2,1)}, bf16[512,2304]{1,0:T(8,128)(2,1)}, u32[]{:S(2)}, u32[]{:S(2)}) %collective-permute-start.10) | collective-permute-done | bytes 2359328 | tf_op jit(solution)/shard_map/ppermute | solution.py:1006
  167.4 13.0 collective-permute-done.11.refs_3_
  190.2 28.3 %project.1 = (bf16[9,2048,64]{2,1,0:T(8,128)(2,1)}, bf16[2048,1152]{1,0:T(8,128)(2,1)}, bf16[2048,2304]{1,0:T(8,128)(2,1)}) custom-call(bf16[512,2304]{1,0:T(8,128)(2,1)} %pad_maximum_fusion.13.refs_0_, bf16[512,2304]{1,0:T(8,128)(2,1)} %collective-permute-done.9.refs_1_, bf16[512,2304]{1,0:T(8,128)(2,1)} %collective-permute-done.10.refs_2_, ...), custom_call_target="tpu_custom_call" | custom-call | flops 16307453952 | bytes 29196288 | tf_op jit(solution)/shard_map/project/pallas_call | solution.py:487
  269.1 19.2 %sort_keys.1 = (bf16[9,4096,64]{2,1,0:T(8,128)(2,1)}, bf16[9,4096,64]{2,1,0:T(8,128)(2,1)}, bf16[9,64,4096]{2,1,0:T(8,128)(2,1)}, bf16[9,64,4096]{2,1,0:T(8,128)(2,1)}) custom-call(s32[64]{0:T(128)} %select_reduce_fusion.order_ref, bf16[32,64,1152]{2,1,0:T(8,128)(2,1)} %bitcast.329, bf16[32,64,1152]{2,1,0:T(8,128)(2,1)} %bitcast.330, ...), custom_call_target="tpu_custom_call" | custom-call | bytes 150994944 | tf_op jit(solution)/shard_map/sort_keys/pallas_call | solution.py:533
  293.0 14.5 %collective-permute-done.21 = bf16[128,2304]{1,0:T(8,128)(2,1)} collective-permute-done((bf16[128,2304]{1,0:T(8,128)(2,1)}, bf16[128,2304]{1,0:T(8,128)(2,1)}, u32[]{:S(2)}, u32[]{:S(2)}) %collective-permute-start.21) | collective-permute-done | bytes 589856 | tf_op jit(solution)/shard_map/ppermute | solution.py:1060
  328.1 42.3 %attention_forward.3 = (bf16[1024,576]{1,0:T(8,128)(2,1)}, f32[4,9,256]{2,1,0:T(8,128)}, f32[4,9,256]{2,1,0:T(8,128)}) custom-call(s32[32]{0:T(128)} %copy-done.94, s32[8]{0:T(128)} %copy-done.107, bf16[9,2048,64]{2,1,0:T(8,128)(2,1)} %get-tuple-element.360.q_ref, bf16[9,4096,64]{2,1,0:T(8,128)(2,1)} %get-tuple-element.349.k_ref, ...), custom_call_target="tpu_custom_call" | custom-call | flops 24159191040 | bytes 37748736 | tf_op jit(solution)/shard_map/attention_forward/pallas_call | solution.py:669
  387.0 24.1 %attention_forward.5 = (bf16[512,576]{1,0:T(8,128)(2,1)}, f32[2,9,256]{2,1,0:T(8,128)}, f32[2,9,256]{2,1,0:T(8,128)}) custom-call(s32[32]{0:T(128)} %copy-done.94, s32[8]{0:T(128)} %copy-done.107, bf16[9,2048,64]{2,1,0:T(8,128)(2,1)} %get-tuple-element.360.q_ref, bf16[9,4096,64]{2,1,0:T(8,128)(2,1)} %get-tuple-element.349.k_ref, ...), custom_call_target="tpu_custom_call" | custom-call | flops 12079595520 | bytes 37748736 | tf_op jit(solution)/shard_map/attention_forward/pallas_call | solution.py:669
  423.7 25.6 %attention_forward.4 = (bf16[512,576]{1,0:T(8,128)(2,1)}, f32[2,9,256]{2,1,0:T(8,128)}, f32[2,9,256]{2,1,0:T(8,128)}) custom-call(s32[32]{0:T(128)} %copy-done.94, s32[8]{0:T(128)} %copy-done.107, bf16[9,2048,64]{2,1,0:T(8,128)(2,1)} %get-tuple-element.360.q_ref, bf16[9,4096,64]{2,1,0:T(8,128)(2,1)} %get-tuple-element.349.k_ref, ...), custom_call_target="tpu_custom_call" | custom-call | flops 12079595520 | bytes 37748736 | tf_op jit(solution)/shard_map/attention_forward/pallas_call | solution.py:669
  472.9 12.6 fusion.63
  606.6 12.5 fusion.73
  632.3 12.7 fusion.69
  673.2 13.2 fusion.71
  698.8 14.2 %fusion.72 = f32[1472,2304]{1,0:T(8,128)} fusion(bf16[1024,1472]{0,1:T(8,128)(2,1)S(1)} %copy-done.36, bf16[1024,2304]{1,0:T(8,128)(2,1)} %copy-done.70), kind=kOutput, calls=%fused_computation.356 | convolution fusion | flops 6945767424 | bytes 21299200 | tf_op jit(solution)/shard_map/dot_general | solution.py:409
  737.1 12.7 fusion.75
  814.4 12.8 convolution_convert_fusion.3
  857.6 26.7 %attention_delta.1 = (bf16[9,2048,64]{2,1,0:T(8,128)(2,1)}, f32[8,9,256]{2,1,0:T(8,128)}, bf16[576,2304]{1,0:T(8,128)(2,1)}) custom-call(bf16[256,2304]{1,0:T(8,128)(2,1)} %get-tuple-element.458.refs_0_, bf16[256,2304]{1,0:T(8,128)(2,1)} %collective-permute-done.49.refs_1_, bf16[256,2304]{1,0:T(8,128)(2,1)} %collective-permute-done.50.refs_2_, ...), custom_call_target="tpu_custom_call" | custom-call | flops 5435817984 | bytes 9437184 | tf_op jit(solution)/shard_map/attention_delta/pallas_call | solution.py:720
  897.1 51.7 %attention_backward.3 = (f32[3,2048,64]{2,1,0:T(8,128)}, bf16[3,4096,64]{2,1,0:T(8,128)(2,1)}, bf16[3,4096,64]{2,1,0:T(8,128)(2,1)}) custom-call(s32[32]{0:T(128)} %copy-done.94, s32[8]{0:T(128)} %copy-done.107, bf16[9,2048,64]{2,1,0:T(8,128)(2,1)} %get-tuple-element.360.q_ref, bf16[9,2048,64]{2,1,0:T(8,128)(2,1)} %get-tuple-element.524.g_ref, ...), custom_call_target="tpu_custom_call" | custom-call | flops 32212254720 | bytes 25165824 | tf_op jit(solution)/shard_map/attention_backward/pallas_call | solution.py:817
  972.4 51.4 %attention_backward.4 = (f32[3,2048,64]{2,1,0:T(8,128)}, bf16[3,4096,64]{2,1,0:T(8,128)(2,1)}, bf16[3,4096,64]{2,1,0:T(8,128)(2,1)}) custom-call(s32[32]{0:T(128)} %copy-done.94, s32[8]{0:T(128)} %copy-done.107, bf16[9,2048,64]{2,1,0:T(8,128)(2,1)} %get-tuple-element.360.q_ref, bf16[9,2048,64]{2,1,0:T(8,128)(2,1)} %get-tuple-element.524.g_ref, ...), custom_call_target="tpu_custom_call" | custom-call | flops 32212254720 | bytes 25165824 | tf_op jit(solution)/shard_map/attention_backward/pallas_call | solution.py:817
  1075.3 51.8 %attention_backward.5 = (f32[3,2048,64]{2,1,0:T(8,128)}, bf16[3,4096,64]{2,1,0:T(8,128)(2,1)}, bf16[3,4096,64]{2,1,0:T(8,128)(2,1)}) custom-call(s32[32]{0:T(128)} %copy-done.94, s32[8]{0:T(128)} %copy-done.107, bf16[9,2048,64]{2,1,0:T(8,128)(2,1)} %get-tuple-element.360.q_ref, bf16[9,2048,64]{2,1,0:T(8,128)(2,1)} %get-tuple-element.524.g_ref, ...), custom_call_target="tpu_custom_call" | custom-call | flops 32212254720 | bytes 25165824 | tf_op jit(solution)/shard_map/attention_backward/pallas_call | solution.py:817
  1216.4 15.4 %unproject.2 = bf16[1024,2304]{1,0:T(8,128)(2,1)} custom-call(bf16[2048,576]{1,0:T(8,128)(2,1)} %unturn.3.a_ref, bf16[2048,576]{1,0:T(8,128)(2,1)} %unturn.4.b_ref, bf16[2048,576]{1,0:T(8,128)(2,1)} %unturn.5.c_ref, bf16[8,4,80,1728]{3,2,1,0:T(8,128)(2,1)} %bitcast.411), custom_call_target="tpu_custom_call" | custom-call | flops 8153726976 | bytes 9437184 | tf_op jit(solution)/shard_map/unproject/pallas_call | solution.py:940
  1274.7 15.5 %unproject.3 = bf16[1024,2304]{1,0:T(8,128)(2,1)} custom-call(bf16[2048,576]{1,0:T(8,128)(2,1)} %unturn.3.a_ref, bf16[2048,576]{1,0:T(8,128)(2,1)} %unturn.4.b_ref, bf16[2048,576]{1,0:T(8,128)(2,1)} %unturn.5.c_ref, bf16[8,4,80,1728]{3,2,1,0:T(8,128)(2,1)} %bitcast.412), custom_call_target="tpu_custom_call" | custom-call | flops 8153726976 | bytes 9437184 | tf_op jit(solution)/shard_map/unproject/pallas_call | solution.py:940
  (742 shorter events, 844.2 us)
Async XLA Ops:
  7.2 176.5 %all-gather.15.cloned.1.call-start = ((), (), s32[]{:S(2)}) async-start(), calls=%async_computation.19 | async-start | bytes 10321920 | tf_op jit(solution)/shard_map/all_gather | solution.py:1131
  99.3 272.6 %all-gather.7.cloned.1.call-start = ((), (), s32[]{:S(2)}) async-start(), calls=%async_computation.8 | async-start | bytes 2985984 | tf_op jit(solution)/shard_map/all_gather | solution.py:1133
  218.6 254.3 %all-gather.9.cloned.1.call-start = ((), (), s32[]{:S(2)}) async-start(), calls=%async_computation.9 | async-start | bytes 7630848 | tf_op jit(solution)/shard_map/all_gather | solution.py:1177
  310.9 219.8 %all-gather.11.cloned.1.call-start = ((), (), s32[]{:S(2)}) async-start(), calls=%async_computation.10 | async-start | bytes 7630848 | tf_op jit(solution)/shard_map/all_gather | solution.py:1177
  314.1 229.0 %all-gather.13.cloned.1.call-start = ((), (), s32[]{:S(2)}) async-start(), calls=%async_computation.11 | async-start | bytes 7630848 | tf_op jit(solution)/shard_map/all_gather | solution.py:1177
  384.5 64.7 %collective-permute-start.31 = (bf16[256,2304]{1,0:T(8,128)(2,1)}, bf16[256,2304]{1,0:T(8,128)(2,1)}, u32[]{:S(2)}, u32[]{:S(2)}) collective-permute-start(bf16[256,2304]{1,0:T(8,128)(2,1)} %slice.506), channel_id=1, source_target_pairs={{0,8},{8,0},{16,24},{24,16},{1,9},{9,1},{17,25},{25,17},{2,10},{10... | collective-permute-start | bytes 3538952 | tf_op jit(solution)/shard_map/ppermute | solution.py:1006
  386.2 63.1 %collective-permute-start.32 = (bf16[256,2304]{1,0:T(8,128)(2,1)}, bf16[256,2304]{1,0:T(8,128)(2,1)}, u32[]{:S(2)}, u32[]{:S(2)}) collective-permute-start(bf16[256,2304]{1,0:T(8,128)(2,1)} %slice.507), channel_id=1, source_target_pairs={{0,16},{8,24},{16,0},{24,8},{1,17},{9,25},{17,1},{25,9},{2,18},{10... | collective-permute-start | bytes 3538952 | tf_op jit(solution)/shard_map/ppermute | solution.py:1006
  423.6 460.7 %reduce-scatter.8.cloned.1.call-start = ((), (), s32[]{:S(2)}) async-start(), calls=%async_computation.12 | async-start | bytes 7630848 | tf_op jit(solution)/shard_map/reduce_scatter | solution.py:1251
  737.0 211.8 %reduce-scatter.10.cloned.1.call-start = ((), (), s32[]{:S(2)}) async-start(), calls=%async_computation.13 | async-start | bytes 7630848 | tf_op jit(solution)/shard_map/reduce_scatter | solution.py:1251
  782.5 245.0 %reduce-scatter.12.cloned.1.call-start = ((), (), s32[]{:S(2)}) async-start(), calls=%async_computation.14 | async-start | bytes 7630848 | tf_op jit(solution)/shard_map/reduce_scatter | solution.py:1251
  844.9 366.9 %reduce-scatter.14.cloned.1.call-start = ((), (), s32[]{:S(2)}) async-start(), calls=%async_computation.15 | async-start | bytes 3686400 | tf_op jit(solution)/shard_map/reduce_scatter | solution.py:1293
  887.9 60.9 %collective-permute-start.63 = (bf16[512,2304]{1,0:T(8,128)(2,1)}, bf16[512,2304]{1,0:T(8,128)(2,1)}, u32[]{:S(2)}, u32[]{:S(2)}) collective-permute-start(bf16[512,2304]{1,0:T(8,128)(2,1)} %pad_maximum_fusion.18), channel_id=1, source_target_pairs={{0,8},{8,0},{16,24},{24,16},{1,9},{9,1},{17,25},{25,17},{2,10},{10... | collective-permute-start | bytes 7077896 | tf_op jit(solution)/shard_map/ppermute | solution.py:1006
  893.0 55.8 %collective-permute-start.64 = (bf16[512,2304]{1,0:T(8,128)(2,1)}, bf16[512,2304]{1,0:T(8,128)(2,1)}, u32[]{:S(2)}, u32[]{:S(2)}) collective-permute-start(bf16[512,2304]{1,0:T(8,128)(2,1)} %pad_maximum_fusion.19), channel_id=1, source_target_pairs={{0,16},{8,24},{16,0},{24,8},{1,17},{9,25},{17,1},{25,9},{2,18},{10... | collective-permute-start | bytes 7077896 | tf_op jit(solution)/shard_map/ppermute | solution.py:1006
  962.7 64.8 %collective-permute-start.65 = (bf16[128,2304]{1,0:T(8,128)(2,1)}, bf16[128,2304]{1,0:T(8,128)(2,1)}, u32[]{:S(2)}, u32[]{:S(2)}) collective-permute-start(bf16[128,2304]{1,0:T(8,128)(2,1)} %get-tuple-element.755), channel_id=1, source_target_pairs={{0,2},{2,0},{4,6},{6,4},{1,3},{3,1},{5,7},{7,5},{8,10},{10,8},{12,... | collective-permute-start | bytes 1769480 | tf_op jit(solution)/shard_map/ppermute | solution.py:1060
  962.7 64.8 %collective-permute-start.66 = (bf16[128,2304]{1,0:T(8,128)(2,1)}, bf16[128,2304]{1,0:T(8,128)(2,1)}, u32[]{:S(2)}, u32[]{:S(2)}) collective-permute-start(bf16[128,2304]{1,0:T(8,128)(2,1)} %get-tuple-element.754), channel_id=1, source_target_pairs={{0,4},{2,6},{4,0},{6,2},{1,5},{3,7},{5,1},{7,3},{8,12},{10,14},{12... | collective-permute-start | bytes 1769480 | tf_op jit(solution)/shard_map/ppermute | solution.py:1060
  971.8 55.7 %collective-permute-start.67 = (bf16[128,2304]{1,0:T(8,128)(2,1)}, bf16[128,2304]{1,0:T(8,128)(2,1)}, u32[]{:S(2)}, u32[]{:S(2)}) collective-permute-start(bf16[128,2304]{1,0:T(8,128)(2,1)} %get-tuple-element.753), channel_id=1, source_target_pairs={{0,6},{2,4},{4,2},{6,0},{1,7},{3,5},{5,3},{7,1},{8,14},{10,12},{12... | collective-permute-start | bytes 1769480 | tf_op jit(solution)/shard_map/ppermute | solution.py:1060
  972.4 55.2 %collective-permute-start.68 = (bf16[2048,384]{1,0:T(8,128)(2,1)}, bf16[2048,384]{1,0:T(8,128)(2,1)S(1)}, u32[]{:S(2)}, u32[]{:S(2)}) collective-permute-start(bf16[2048,384]{1,0:T(8,128)(2,1)} %get-tuple-element.501), channel_id=1, source_target_pairs={{0,1},{1,0},{2,3},{3,2},{4,5},{5,4},{6,7},{7,6},{8,9},{9,8},{10,11... | collective-permute-start | bytes 4718600 | tf_op jit(solution)/shard_map/ppermute | solution.py:1296
  1067.4 222.8 %reduce-scatter.18.cloned.1.call-start = ((), (), s32[]{:S(2)}) async-start(), calls=%async_computation.17 | async-start | bytes 2985984 | tf_op jit(solution)/shard_map/reduce_scatter | solution.py:1251
  1070.6 225.8 %reduce-scatter.16.cloned.1.call-start = ((), (), s32[]{:S(2)}) async-start(), calls=%async_computation.16 | async-start | bytes 3686400 | tf_op jit(solution)/shard_map/reduce_scatter | solution.py:1293
  1071.8 55.3 %collective-permute-start.71 = (bf16[3,184,576]{2,1,0:T(8,128)(2,1)}, bf16[3,184,576]{2,1,0:T(8,128)(2,1)S(1)}, u32[]{:S(2)}, u32[]{:S(2)}) collective-permute-start(bf16[3,184,576]{2,1,0:T(8,128)(2,1)} %get-tuple-element.727), channel_id=1, source_target_pairs={{0,24},{8,16},{16,8},{24,0},{1,25},{9,17},{17,9},{25,1},{2,26},{10... | collective-permute-start | bytes 1907720 | tf_op jit(solution)/shard_map/ppermute | solution.py:1060
  1072.8 54.3 %collective-permute-start.70 = (bf16[3,184,576]{2,1,0:T(8,128)(2,1)S(1)}, bf16[3,184,576]{2,1,0:T(8,128)(2,1)S(1)}, u32[]{:S(2)}, u32[]{:S(2)}) collective-permute-start(bf16[3,184,576]{2,1,0:T(8,128)(2,1)S(1)} %get-tuple-element.728), channel_id=1, source_target_pairs={{0,16},{8,24},{16,0},{24,8},{1,17},{9,25},{17,1},{25,9},{2,18},{10... | collective-permute-start | bytes 1907720 | tf_op jit(solution)/shard_map/ppermute | solution.py:1060
  1073.6 53.5 %collective-permute-start.69 = (bf16[3,184,576]{2,1,0:T(8,128)(2,1)S(1)}, bf16[3,184,576]{2,1,0:T(8,128)(2,1)S(1)}, u32[]{:S(2)}, u32[]{:S(2)}) collective-permute-start(bf16[3,184,576]{2,1,0:T(8,128)(2,1)S(1)} %get-tuple-element.729), channel_id=1, source_target_pairs={{0,8},{8,0},{16,24},{24,16},{1,9},{9,1},{17,25},{25,17},{2,10},{10... | collective-permute-start | bytes 1907720 | tf_op jit(solution)/shard_map/ppermute | solution.py:1060
  1075.2 54.9 %collective-permute-start.72 = (bf16[2048,384]{1,0:T(8,128)(2,1)}, bf16[2048,384]{1,0:T(8,128)(2,1)S(1)}, u32[]{:S(2)}, u32[]{:S(2)}) collective-permute-start(bf16[2048,384]{1,0:T(8,128)(2,1)} %get-tuple-element.533), channel_id=1, source_target_pairs={{0,1},{1,0},{2,3},{3,2},{4,5},{5,4},{6,7},{7,6},{8,9},{9,8},{10,11... | collective-permute-start | bytes 4718600 | tf_op jit(solution)/shard_map/ppermute | solution.py:1296
  1203.2 182.7 %reduce-scatter.20.cloned.1.call-start = ((), (), s32[]{:S(2)}) async-start(), calls=%async_computation.18 | async-start | bytes 3686400 | tf_op jit(solution)/shard_map/reduce_scatter | solution.py:1293
  (206 other events, 3637.0 us)
Sparse Core Ops, SparseCore 0:
  98.6 84.9 all-gather.14
  218.7 44.4 all-gather.6
  311.1 65.7 all-gather.8
  378.3 67.4 all-gather.10
  447.3 67.4 all-gather.12
  737.1 73.3 reduce-scatter.7
  812.9 73.0 reduce-scatter.9
  888.3 83.8 reduce-scatter.11
  1067.5 38.2 reduce-scatter.13
  1108.0 36.8 reduce-scatter.17
  1203.3 38.1 reduce-scatter.15
  1274.8 38.4 reduce-scatter.19

commit v7 on v5

--- a/solution.py
+++ b/solution.py
@@ -1361,6 +1361,7 @@
     hop_a, near_b = meet(hop_a, near_b)
     hop_b, hop_a = meet(hop_back(first_back(1, scatter_sum(rest_b, near_b))), hop_out(hop_a))
     grad_input = join_tiles([jnp.stack(hop_a), jnp.stack(hop_out(hop_b))]).astype(F32)
+    ffn_grads, late = after((ffn_grads, weights_a), rest_b)
     ffn_grads = ffn_grads.astype(F32)
     ffn_grads = jnp.concatenate([ffn_grads[k, :, :n] for k, n in enumerate(sizes)], axis=1)
     grad_ffn_gain = jnp.sum(weights_a[:, thin, :thin].astype(F32), axis=0)
@@ -1370,7 +1371,7 @@
     )
     grad_attn_gain = proj[3][:, 0]
 
-    maxima = jnp.sum(weights_a[:, thin + 1 : thin + 3, : 8 * NH].astype(F32), axis=1)
+    maxima = jnp.sum(late[:, thin + 1 : thin + 3, : 8 * NH].astype(F32), axis=1)
     maxima = jnp.max(maxima.reshape(4, 8, NH), axis=1).reshape(HEADS)
     limit_value = clip_threshold[0].astype(F32)
     clip_factor = jnp.sqrt(limit_value / jnp.maximum(maxima, limit_value))

time: 1430 us -> 1430 us (level)
  waiting for transfers between devices: 304 us -> 280 us
    ppermute x42, waiting for transfers between devices: 173 us -> 145 us  [swap_blocks(): lax.ppermute(pieces[r], name, [(k, k ^ r) for k in range(4)])]
    unnamed x251 -> x255, local copies, waits for them, and re-layouts: 34.6 us -> 36.3 us
  transfers between devices with their start and end apart: 113 -> 113, of which waited for: 46 -> 43; matrix products, arithmetic and copies ran while one was open for 35% -> 37% of each run, Pallas kernels for 27% -> 27%
where the time goes in v7:
time: 1430 us; the launch traced here: 1410 us
  Pallas kernels  409 us (29%)
  waiting for transfers between devices  280 us (20%)
  matrix products  258 us (18%)
  other arithmetic  169 us (12%)
  local copies, waits for them, and re-layouts  155 us (11%)
  starting transfers between devices  122 us (9%)
  between operations  17.1 us (1%)
    dot_general x23, matrix products, mul(): return lax.dot_general(left, right, dims, preferred_element_type=F32)  258 us
    pallas_call x3, Pallas kernels, attention_backward(): pl.pallas_call(functools.partial(backward_kernel, first=first), out_shape...  155 us
    ppermute x42, waiting for transfers between devices, swap_blocks(): lax.ppermute(pieces[r], name, [(k, k ^ r) for k in range(4)])  145 us
    ppermute x52, waiting for transfers between devices, flip(): return lax.ppermute(values, 'p', [(k, k ^ mask) for k in range(4)])  122 us
    pallas_call x3, Pallas kernels, attention_forward(): pl.pallas_call(functools.partial(forward_kernel, shift=shift), out_shape=...  91.7 us
    ppermute x42, starting transfers between devices, swap_blocks(): lax.ppermute(pieces[r], name, [(k, k ^ r) for k in range(4)])  58 us
    ppermute x52, starting transfers between devices, flip(): return lax.ppermute(values, 'p', [(k, k ^ mask) for k in range(4)])  54.9 us
    unnamed x255, local copies, waits for them, and re-layouts  36.3 us
  transfers between devices with their start and end apart: 113, of which 43 were waited for; matrix products, arithmetic and copies ran while one was open for 37% of the time, Pallas kernels for 27%

profile of v7, /device:TPU:8, one launch (start us, length us, event | category | flops | bytes accessed | tf_op | source)
XLA Modules:
  0.0 1409.8 jit_solution(1576384013512880417)
XLA Ops:
  27.2 12.7 collective-permute-done.3
  55.9 12.7 collective-permute-done.8
  68.6 19.7 %collective-permute-done.9 = bf16[128,2304]{1,0:T(8,128)(2,1)S(1)} collective-permute-done((bf16[128,2304]{1,0:T(8,128)(2,1)S(1)}, bf16[128,2304]{1,0:T(8,128)(2,1)S(1)}, u32[]{:S(2)}, u32[]{:S(2)}) %collective-permute-start.9) | collective-permute-done | bytes 589856 | tf_op jit(solution)/shard_map/ppermute | solution.py:1060
  114.0 41.0 %collective-permute-done.12.refs_2_ = bf16[512,2304]{1,0:T(8,128)(2,1)} collective-permute-done((bf16[512,2304]{1,0:T(8,128)(2,1)}, bf16[512,2304]{1,0:T(8,128)(2,1)}, u32[]{:S(2)}, u32[]{:S(2)}) %collective-permute-start.12) | collective-permute-done | bytes 2359328 | tf_op jit(solution)/shard_map/ppermute | solution.py:1006
  167.3 13.0 collective-permute-done.13.refs_3_
  190.2 28.3 %project.1 = (bf16[9,2048,64]{2,1,0:T(8,128)(2,1)}, bf16[2048,1152]{1,0:T(8,128)(2,1)}, bf16[2048,2304]{1,0:T(8,128)(2,1)}) custom-call(bf16[512,2304]{1,0:T(8,128)(2,1)} %pad_maximum_fusion.13.refs_0_, bf16[512,2304]{1,0:T(8,128)(2,1)} %collective-permute-done.11.refs_1_, bf16[512,2304]{1,0:T(8,128)(2,1)} %collective-permute-done.12.refs_2_, ...), custom_call_target="tpu_custom_call" | custom-call | flops 16307453952 | bytes 29196288 | tf_op jit(solution)/shard_map/project/pallas_call | solution.py:487
  269.1 19.5 %sort_keys.1 = (bf16[9,4096,64]{2,1,0:T(8,128)(2,1)}, bf16[9,4096,64]{2,1,0:T(8,128)(2,1)}, bf16[9,64,4096]{2,1,0:T(8,128)(2,1)}, bf16[9,64,4096]{2,1,0:T(8,128)(2,1)}) custom-call(s32[64]{0:T(128)} %select_reduce_fusion.order_ref, bf16[32,64,1152]{2,1,0:T(8,128)(2,1)} %bitcast.329, bf16[32,64,1152]{2,1,0:T(8,128)(2,1)} %bitcast.330, ...), custom_call_target="tpu_custom_call" | custom-call | bytes 150994944 | tf_op jit(solution)/shard_map/sort_keys/pallas_call | solution.py:533
  293.0 14.5 %collective-permute-done.21 = bf16[128,2304]{1,0:T(8,128)(2,1)} collective-permute-done((bf16[128,2304]{1,0:T(8,128)(2,1)}, bf16[128,2304]{1,0:T(8,128)(2,1)}, u32[]{:S(2)}, u32[]{:S(2)}) %collective-permute-start.21) | collective-permute-done | bytes 589856 | tf_op jit(solution)/shard_map/ppermute | solution.py:1060
  328.2 42.0 %attention_forward.3 = (bf16[1024,576]{1,0:T(8,128)(2,1)}, f32[4,9,256]{2,1,0:T(8,128)}, f32[4,9,256]{2,1,0:T(8,128)}) custom-call(s32[32]{0:T(128)} %copy-done.96, s32[8]{0:T(128)} %copy-done.109, bf16[9,2048,64]{2,1,0:T(8,128)(2,1)} %get-tuple-element.357.q_ref, bf16[9,4096,64]{2,1,0:T(8,128)(2,1)} %get-tuple-element.346.k_ref, ...), custom_call_target="tpu_custom_call" | custom-call | flops 24159191040 | bytes 37748736 | tf_op jit(solution)/shard_map/attention_forward/pallas_call | solution.py:669
  387.1 24.1 %attention_forward.5 = (bf16[512,576]{1,0:T(8,128)(2,1)}, f32[2,9,256]{2,1,0:T(8,128)}, f32[2,9,256]{2,1,0:T(8,128)}) custom-call(s32[32]{0:T(128)} %copy-done.96, s32[8]{0:T(128)} %copy-done.109, bf16[9,2048,64]{2,1,0:T(8,128)(2,1)} %get-tuple-element.357.q_ref, bf16[9,4096,64]{2,1,0:T(8,128)(2,1)} %get-tuple-element.346.k_ref, ...), custom_call_target="tpu_custom_call" | custom-call | flops 12079595520 | bytes 37748736 | tf_op jit(solution)/shard_map/attention_forward/pallas_call | solution.py:669
  423.7 25.6 %attention_forward.4 = (bf16[512,576]{1,0:T(8,128)(2,1)}, f32[2,9,256]{2,1,0:T(8,128)}, f32[2,9,256]{2,1,0:T(8,128)}) custom-call(s32[32]{0:T(128)} %copy-done.96, s32[8]{0:T(128)} %copy-done.109, bf16[9,2048,64]{2,1,0:T(8,128)(2,1)} %get-tuple-element.357.q_ref, bf16[9,4096,64]{2,1,0:T(8,128)(2,1)} %get-tuple-element.346.k_ref, ...), custom_call_target="tpu_custom_call" | custom-call | flops 12079595520 | bytes 37748736 | tf_op jit(solution)/shard_map/attention_forward/pallas_call | solution.py:669
  472.9 12.6 fusion.63
  632.4 12.7 fusion.69
  673.3 13.3 fusion.71
  698.9 14.2 %fusion.72 = f32[1472,2304]{1,0:T(8,128)} fusion(bf16[1024,1472]{0,1:T(8,128)(2,1)S(1)} %copy-done.39, bf16[1024,2304]{1,0:T(8,128)(2,1)} %copy-done.72), kind=kOutput, calls=%fused_computation.356 | convolution fusion | flops 6945767424 | bytes 21299200 | tf_op jit(solution)/shard_map/dot_general | solution.py:409
  737.3 12.7 fusion.75
  815.0 13.4 convolution_convert_fusion.3
  858.5 26.7 %attention_delta.1 = (bf16[9,2048,64]{2,1,0:T(8,128)(2,1)}, f32[8,9,256]{2,1,0:T(8,128)}, bf16[576,2304]{1,0:T(8,128)(2,1)}) custom-call(bf16[256,2304]{1,0:T(8,128)(2,1)} %get-tuple-element.455.refs_0_, bf16[256,2304]{1,0:T(8,128)(2,1)} %collective-permute-done.49.refs_1_, bf16[256,2304]{1,0:T(8,128)(2,1)} %collective-permute-done.50.refs_2_, ...), custom_call_target="tpu_custom_call" | custom-call | flops 5435817984 | bytes 9437184 | tf_op jit(solution)/shard_map/attention_delta/pallas_call | solution.py:720
  898.0 51.6 %attention_backward.3 = (f32[3,2048,64]{2,1,0:T(8,128)}, bf16[3,4096,64]{2,1,0:T(8,128)(2,1)}, bf16[3,4096,64]{2,1,0:T(8,128)(2,1)}) custom-call(s32[32]{0:T(128)} %copy-done.96, s32[8]{0:T(128)} %copy-done.109, bf16[9,2048,64]{2,1,0:T(8,128)(2,1)} %get-tuple-element.357.q_ref, bf16[9,2048,64]{2,1,0:T(8,128)(2,1)} %get-tuple-element.520.g_ref, ...), custom_call_target="tpu_custom_call" | custom-call | flops 32212254720 | bytes 25165824 | tf_op jit(solution)/shard_map/attention_backward/pallas_call | solution.py:817
  967.1 51.4 %attention_backward.4 = (f32[3,2048,64]{2,1,0:T(8,128)}, bf16[3,4096,64]{2,1,0:T(8,128)(2,1)}, bf16[3,4096,64]{2,1,0:T(8,128)(2,1)}) custom-call(s32[32]{0:T(128)} %copy-done.96, s32[8]{0:T(128)} %copy-done.109, bf16[9,2048,64]{2,1,0:T(8,128)(2,1)} %get-tuple-element.357.q_ref, bf16[9,2048,64]{2,1,0:T(8,128)(2,1)} %get-tuple-element.520.g_ref, ...), custom_call_target="tpu_custom_call" | custom-call | flops 32212254720 | bytes 25165824 | tf_op jit(solution)/shard_map/attention_backward/pallas_call | solution.py:817
  1074.5 51.6 %attention_backward.5 = (f32[3,2048,64]{2,1,0:T(8,128)}, bf16[3,4096,64]{2,1,0:T(8,128)(2,1)}, bf16[3,4096,64]{2,1,0:T(8,128)(2,1)}) custom-call(s32[32]{0:T(128)} %copy-done.96, s32[8]{0:T(128)} %copy-done.109, bf16[9,2048,64]{2,1,0:T(8,128)(2,1)} %get-tuple-element.357.q_ref, bf16[9,2048,64]{2,1,0:T(8,128)(2,1)} %get-tuple-element.520.g_ref, ...), custom_call_target="tpu_custom_call" | custom-call | flops 32212254720 | bytes 25165824 | tf_op jit(solution)/shard_map/attention_backward/pallas_call | solution.py:817
  1131.3 12.8 collective-permute-done.75
  1197.0 15.4 %unproject.2 = bf16[1024,2304]{1,0:T(8,128)(2,1)} custom-call(bf16[2048,576]{1,0:T(8,128)(2,1)} %unturn.3.a_ref, bf16[2048,576]{1,0:T(8,128)(2,1)} %unturn.4.b_ref, bf16[2048,576]{1,0:T(8,128)(2,1)} %unturn.5.c_ref, bf16[8,4,80,1728]{3,2,1,0:T(8,128)(2,1)} %bitcast.409), custom_call_target="tpu_custom_call" | custom-call | flops 8153726976 | bytes 9437184 | tf_op jit(solution)/shard_map/unproject/pallas_call | solution.py:940
  1254.8 15.4 %unproject.3 = bf16[1024,2304]{1,0:T(8,128)(2,1)} custom-call(bf16[2048,576]{1,0:T(8,128)(2,1)} %unturn.3.a_ref, bf16[2048,576]{1,0:T(8,128)(2,1)} %unturn.4.b_ref, bf16[2048,576]{1,0:T(8,128)(2,1)} %unturn.5.c_ref, bf16[8,4,80,1728]{3,2,1,0:T(8,128)(2,1)} %bitcast.410), custom_call_target="tpu_custom_call" | custom-call | flops 8153726976 | bytes 9437184 | tf_op jit(solution)/shard_map/unproject/pallas_call | solution.py:940
  (751 shorter events, 835.8 us)
Async XLA Ops:
  7.2 176.5 %all-gather.15.cloned.1.call-start = ((), (), s32[]{:S(2)}) async-start(), calls=%async_computation.19 | async-start | bytes 10321920 | tf_op jit(solution)/shard_map/all_gather | solution.py:1131
  99.3 272.6 %all-gather.7.cloned.1.call-start = ((), (), s32[]{:S(2)}) async-start(), calls=%async_computation.8 | async-start | bytes 2985984 | tf_op jit(solution)/shard_map/all_gather | solution.py:1133
  218.6 254.3 %all-gather.9.cloned.1.call-start = ((), (), s32[]{:S(2)}) async-start(), calls=%async_computation.9 | async-start | bytes 7630848 | tf_op jit(solution)/shard_map/all_gather | solution.py:1177
  311.0 219.8 %all-gather.11.cloned.1.call-start = ((), (), s32[]{:S(2)}) async-start(), calls=%async_computation.10 | async-start | bytes 7630848 | tf_op jit(solution)/shard_map/all_gather | solution.py:1177
  314.2 229.1 %all-gather.13.cloned.1.call-start = ((), (), s32[]{:S(2)}) async-start(), calls=%async_computation.11 | async-start | bytes 7630848 | tf_op jit(solution)/shard_map/all_gather | solution.py:1177
  384.7 64.6 %collective-permute-start.31 = (bf16[256,2304]{1,0:T(8,128)(2,1)}, bf16[256,2304]{1,0:T(8,128)(2,1)}, u32[]{:S(2)}, u32[]{:S(2)}) collective-permute-start(bf16[256,2304]{1,0:T(8,128)(2,1)} %slice.506), channel_id=1, source_target_pairs={{0,8},{8,0},{16,24},{24,16},{1,9},{9,1},{17,25},{25,17},{2,10},{10... | collective-permute-start | bytes 3538952 | tf_op jit(solution)/shard_map/ppermute | solution.py:1006
  386.3 63.0 %collective-permute-start.32 = (bf16[256,2304]{1,0:T(8,128)(2,1)}, bf16[256,2304]{1,0:T(8,128)(2,1)}, u32[]{:S(2)}, u32[]{:S(2)}) collective-permute-start(bf16[256,2304]{1,0:T(8,128)(2,1)} %slice.507), channel_id=1, source_target_pairs={{0,16},{8,24},{16,0},{24,8},{1,17},{9,25},{17,1},{25,9},{2,18},{10... | collective-permute-start | bytes 3538952 | tf_op jit(solution)/shard_map/ppermute | solution.py:1006
  423.7 461.6 %reduce-scatter.8.cloned.1.call-start = ((), (), s32[]{:S(2)}) async-start(), calls=%async_computation.12 | async-start | bytes 7630848 | tf_op jit(solution)/shard_map/reduce_scatter | solution.py:1251
  737.2 212.5 %reduce-scatter.10.cloned.1.call-start = ((), (), s32[]{:S(2)}) async-start(), calls=%async_computation.13 | async-start | bytes 7630848 | tf_op jit(solution)/shard_map/reduce_scatter | solution.py:1251
  783.0 239.2 %reduce-scatter.12.cloned.1.call-start = ((), (), s32[]{:S(2)}) async-start(), calls=%async_computation.14 | async-start | bytes 7630848 | tf_op jit(solution)/shard_map/reduce_scatter | solution.py:1251
  845.9 346.5 %reduce-scatter.14.cloned.1.call-start = ((), (), s32[]{:S(2)}) async-start(), calls=%async_computation.15 | async-start | bytes 3686400 | tf_op jit(solution)/shard_map/reduce_scatter | solution.py:1293
  888.8 60.9 %collective-permute-start.63 = (bf16[512,2304]{1,0:T(8,128)(2,1)}, bf16[512,2304]{1,0:T(8,128)(2,1)}, u32[]{:S(2)}, u32[]{:S(2)}) collective-permute-start(bf16[512,2304]{1,0:T(8,128)(2,1)} %pad_maximum_fusion.18), channel_id=1, source_target_pairs={{0,8},{8,0},{16,24},{24,16},{1,9},{9,1},{17,25},{25,17},{2,10},{10... | collective-permute-start | bytes 7077896 | tf_op jit(solution)/shard_map/ppermute | solution.py:1006
  893.3 56.4 %collective-permute-start.64 = (bf16[512,2304]{1,0:T(8,128)(2,1)}, bf16[512,2304]{1,0:T(8,128)(2,1)}, u32[]{:S(2)}, u32[]{:S(2)}) collective-permute-start(bf16[512,2304]{1,0:T(8,128)(2,1)} %pad_maximum_fusion.19), channel_id=1, source_target_pairs={{0,16},{8,24},{16,0},{24,8},{1,17},{9,25},{17,1},{25,9},{2,18},{10... | collective-permute-start | bytes 7077896 | tf_op jit(solution)/shard_map/ppermute | solution.py:1006
  963.6 58.7 %collective-permute-start.65 = (bf16[128,2304]{1,0:T(8,128)(2,1)}, bf16[128,2304]{1,0:T(8,128)(2,1)}, u32[]{:S(2)}, u32[]{:S(2)}) collective-permute-start(bf16[128,2304]{1,0:T(8,128)(2,1)} %get-tuple-element.751), channel_id=1, source_target_pairs={{0,2},{2,0},{4,6},{6,4},{1,3},{3,1},{5,7},{7,5},{8,10},{10,8},{12,... | collective-permute-start | bytes 1769480 | tf_op jit(solution)/shard_map/ppermute | solution.py:1060
  963.6 58.7 %collective-permute-start.66 = (bf16[128,2304]{1,0:T(8,128)(2,1)}, bf16[128,2304]{1,0:T(8,128)(2,1)}, u32[]{:S(2)}, u32[]{:S(2)}) collective-permute-start(bf16[128,2304]{1,0:T(8,128)(2,1)} %get-tuple-element.750), channel_id=1, source_target_pairs={{0,4},{2,6},{4,0},{6,2},{1,5},{3,7},{5,1},{7,3},{8,12},{10,14},{12... | collective-permute-start | bytes 1769480 | tf_op jit(solution)/shard_map/ppermute | solution.py:1060
  963.6 58.7 %collective-permute-start.67 = (bf16[128,2304]{1,0:T(8,128)(2,1)}, bf16[128,2304]{1,0:T(8,128)(2,1)}, u32[]{:S(2)}, u32[]{:S(2)}) collective-permute-start(bf16[128,2304]{1,0:T(8,128)(2,1)} %get-tuple-element.749), channel_id=1, source_target_pairs={{0,6},{2,4},{4,2},{6,0},{1,7},{3,5},{5,3},{7,1},{8,14},{10,12},{12... | collective-permute-start | bytes 1769480 | tf_op jit(solution)/shard_map/ppermute | solution.py:1060
  1062.1 208.2 %reduce-scatter.18.cloned.1.call-start = ((), (), s32[]{:S(2)}) async-start(), calls=%async_computation.17 | async-start | bytes 2985984 | tf_op jit(solution)/shard_map/reduce_scatter | solution.py:1251
  1065.3 212.5 %reduce-scatter.16.cloned.1.call-start = ((), (), s32[]{:S(2)}) async-start(), calls=%async_computation.16 | async-start | bytes 3686400 | tf_op jit(solution)/shard_map/reduce_scatter | solution.py:1293
  1068.3 57.7 %collective-permute-start.71 = (bf16[128,2304]{1,0:T(8,128)(2,1)}, bf16[128,2304]{1,0:T(8,128)(2,1)}, u32[]{:S(2)}, u32[]{:S(2)}) collective-permute-start(bf16[128,2304]{1,0:T(8,128)(2,1)} %get-tuple-element.746), channel_id=1, source_target_pairs={{0,24},{8,16},{16,8},{24,0},{1,25},{9,17},{17,9},{25,1},{2,26},{10... | collective-permute-start | bytes 1769480 | tf_op jit(solution)/shard_map/ppermute | solution.py:1060
  1069.8 58.1 %collective-permute-start.70 = (bf16[128,2304]{1,0:T(8,128)(2,1)}, bf16[128,2304]{1,0:T(8,128)(2,1)}, u32[]{:S(2)}, u32[]{:S(2)}) collective-permute-start(bf16[128,2304]{1,0:T(8,128)(2,1)} %get-tuple-element.747), channel_id=1, source_target_pairs={{0,16},{8,24},{16,0},{24,8},{1,17},{9,25},{17,1},{25,9},{2,18},{10... | collective-permute-start | bytes 1769480 | tf_op jit(solution)/shard_map/ppermute | solution.py:1060
  1071.5 56.6 %collective-permute-start.69 = (bf16[128,2304]{1,0:T(8,128)(2,1)}, bf16[128,2304]{1,0:T(8,128)(2,1)}, u32[]{:S(2)}, u32[]{:S(2)}) collective-permute-start(bf16[128,2304]{1,0:T(8,128)(2,1)} %get-tuple-element.748), channel_id=1, source_target_pairs={{0,8},{8,0},{16,24},{24,16},{1,9},{9,1},{17,25},{25,17},{2,10},{10... | collective-permute-start | bytes 1769480 | tf_op jit(solution)/shard_map/ppermute | solution.py:1060
  1071.8 76.7 %collective-permute-start.72 = (bf16[2048,384]{1,0:T(8,128)(2,1)}, bf16[2048,384]{1,0:T(8,128)(2,1)S(1)}, u32[]{:S(2)}, u32[]{:S(2)}) collective-permute-start(bf16[2048,384]{1,0:T(8,128)(2,1)} %get-tuple-element.528), channel_id=1, source_target_pairs={{0,1},{1,0},{2,3},{3,2},{4,5},{5,4},{6,7},{7,6},{8,9},{9,8},{10,11... | collective-permute-start | bytes 4718600 | tf_op jit(solution)/shard_map/ppermute | solution.py:1296
  1073.0 58.4 %collective-permute-start.76 = (bf16[3,184,576]{2,1,0:T(8,128)(2,1)}, bf16[3,184,576]{2,1,0:T(8,128)(2,1)S(1)}, u32[]{:S(2)}, u32[]{:S(2)}) collective-permute-start(bf16[3,184,576]{2,1,0:T(8,128)(2,1)} %get-tuple-element.723), channel_id=1, source_target_pairs={{0,24},{8,16},{16,8},{24,0},{1,25},{9,17},{17,9},{25,1},{2,26},{10... | collective-permute-start | bytes 1907720 | tf_op jit(solution)/shard_map/ppermute | solution.py:1060
  1183.8 195.7 %reduce-scatter.20.cloned.1.call-start = ((), (), s32[]{:S(2)}) async-start(), calls=%async_computation.18 | async-start | bytes 3686400 | tf_op jit(solution)/shard_map/reduce_scatter | solution.py:1293
  (210 other events, 3774.6 us)
Sparse Core Ops, SparseCore 0:
  98.6 84.9 all-gather.14
  218.7 44.4 all-gather.6
  311.1 65.7 all-gather.8
  378.4 67.4 all-gather.10
  447.4 67.4 all-gather.12
  737.3 69.9 reduce-scatter.7
  809.6 73.0 reduce-scatter.9
  885.0 73.6 reduce-scatter.11
  1062.2 36.6 reduce-scatter.13
  1101.2 36.3 reduce-scatter.17
  1183.9 35.0 reduce-scatter.15
  1254.9 48.5 reduce-scatter.19
